TPU v7x, 128 devices: a whole 4x4x4 slice. The times are simulated.
128 devices in a mesh: tbl: 16 (over z, y), row: 8 (over x, core).
Axes of the slice: x: 4, y: 4, z: 4, core: 2. Of those that a mesh axis runs over, the one named last changes fastest.
Arguments:
- slab: bfloat16 [8192, 256], P(('tbl', 'row')), may hold values from -1.1953125 to 1.1953125
- counts: int32 [16384, 8192], P(None, ('tbl', 'row')), may hold values 0 or 1
- cross_down: bfloat16 [4096, 512], replicated, may hold values from -0.09375 to 0.09375
- cross_up: bfloat16 [512, 4096], replicated, may hold values from -0.25 to 0.25
- cross_bias: float32 [4096], replicated, may hold values from -3 to 3
- out_weight: float32 [4096], replicated, may hold values from -0.09375 to 0.09375
- labels: int32 [16384], P(('tbl', 'row')), may hold values 0 or 1
Outputs:
- grad_slab: float32 [8192, 256], P(('tbl', 'row'))
- grad_down: bfloat16 [4096, 512], P(('tbl', 'row'))
- grad_up: bfloat16 [512, 4096], P(None, ('tbl', 'row'))
- grad_bias: float32 [4096], P(('tbl', 'row'))
- grad_out: float32 [4096], P(('tbl', 'row'))
All inputs are finite; a program needn't handle non-finite values. No bound on the sum of `counts` or of `labels` on one device may be relied on, other than what follows from the above.
Results may differ from a plain program's by a relative error of at most 0.022.
Values may be sent and summed in bfloat16 or wider, within the bound.
No kernel may reach another device: no remote copies, remote signals or barrier semaphores. Data moves between devices by JAX's collectives and lax.ppermute only.
A program may use at most 128 MiB of HBM per device.

v0:
```python
import jax
import jax.numpy as jnp
from jax import lax
from jax.experimental import pallas as pl
from jax.experimental.pallas import tpu as pltpu
from jax.sharding import Mesh
from jax.sharding import PartitionSpec as P


ALL = ("z", "y", "x", "c")
PLANE = ("y", "x", "c")
NZ, NY, NX, NC = 4, 4, 4, 2
NK = NX * NC
PEERS = NY * NK
OWN = 128
ROWS = 64
EMBED = 256
RANK = 512
COLS = 1024
SAMPLES = NZ * OWN
EXT = 16
PACK = 400
HALF = EMBED // 2
FAR = SAMPLES - OWN
F32 = jnp.float32
BF16 = jnp.bfloat16


def dot(a, b, da, db):
    return lax.dot_general(a, b, (((da,), (db,)), ((), ())), preferred_element_type=F32)


def flat(z, y, x, c):
    return (((z % NZ) * NY + y % NY) * NX + x % NX) * NC + c % NC


def shift(value, dz=0, dy=0, dx=0, dc=0):
    pairs = [
        (flat(z, y, x, c), flat(z + dz, y + dy, x + dx, c + dc))
        for z in range(NZ)
        for y in range(NY)
        for x in range(NX)
        for c in range(NC)
    ]
    return lax.ppermute(value, ALL, pairs)


def near(value):
    return pltpu.with_memory_space_constraint(value, pltpu.VMEM)


def far(value):
    return pltpu.with_memory_space_constraint(value, pltpu.HBM)


def call(body, outs, args, specs=None, scratch=(), mib=24, cost=None):
    return pl.pallas_call(
        body,
        in_specs=specs or [pl.BlockSpec(memory_space=pltpu.VMEM)] * len(args),
        out_specs=[pl.BlockSpec(memory_space=pltpu.VMEM)] * len(outs),
        out_shape=outs,
        scratch_shapes=list(scratch),
        compiler_params=pltpu.CompilerParams(vmem_limit_bytes=mib << 20),
        cost_estimate=cost,
    )(*args)


IN_SMEM = pl.BlockSpec(memory_space=pltpu.SMEM)
IN_VMEM = pl.BlockSpec(memory_space=pltpu.VMEM)
IN_HBM = pl.BlockSpec(memory_space=pltpu.HBM)


def strips(place_ref, counts_ref, held, sems, blocks):
    strip = NK * OWN

    def copy(y, n, i):
        start = pl.multiple_of(lax.rem(place_ref[0] + i, NZ) * (NY * strip) + y * strip, strip)
        return pltpu.make_async_copy(counts_ref.at[:, pl.ds(start, strip)], held.at[y, n], sems.at[y, n])

    return [(y, n, copy(y, n, i)) for y in range(NY) for n, i in enumerate(blocks)]


def strip_scratch(blocks):
    return [pltpu.VMEM((NY, blocks, ROWS, NK * OWN), jnp.int32), pltpu.SemaphoreType.DMA((NY, blocks))]


def unpack(strip_list, held, out):
    for y, n, copy in strip_list:
        copy.wait()
        for k in range(NK):
            out[y * NK + k, :, n * OWN : (n + 1) * OWN] = (
                held[y, n, :, k * OWN : (k + 1) * OWN].astype(F32).astype(BF16)
            )


def pack_counts(place, counts_t, slab):
    def body(place_ref, counts_ref, slab_ref, out, held, slab_s, sems, slab_sem):
        slab_copy = pltpu.make_async_copy(slab_ref, slab_s, slab_sem)
        slab_copy.start()
        copies = strips(place_ref, counts_ref, held, sems, range(1, NZ))
        for _, _, copy in copies:
            copy.start()
        slab_copy.wait()
        for k in range(PEERS):
            half = k % NC
            out[k, :, FAR:] = slab_s[:, half * HALF : (half + 1) * HALF]
        unpack(copies, held, out)

    held, sems = strip_scratch(NZ - 1)
    return call(
        body,
        [pltpu.VMEM((PEERS, ROWS, FAR + HALF), BF16)],
        (place, far(counts_t), far(slab)),
        [IN_SMEM, IN_HBM, IN_HBM],
        [held, pltpu.VMEM((ROWS, EMBED), BF16), sems, pltpu.SemaphoreType.DMA],
    )[0]


def prepare(place, down, up, w, bias):
    def body(place_ref, down_ref, up_ref, w_ref, bias_ref, rows_out, cols_out, own_out, up_out, down_s, up_s, w_s, bias_s, sems):
        start = pl.multiple_of(place_ref[0] * COLS, COLS)
        copies = [
            pltpu.make_async_copy(down_ref.at[pl.ds(start, COLS), :], down_s, sems.at[0]),
            pltpu.make_async_copy(up_ref.at[:, pl.ds(start, COLS)], up_s, sems.at[1]),
            pltpu.make_async_copy(w_ref.at[:, pl.ds(start, COLS)], w_s, sems.at[2]),
            pltpu.make_async_copy(bias_ref.at[:, pl.ds(start, COLS)], bias_s, sems.at[3]),
        ]
        for copy in copies:
            copy.start()
        for copy in copies:
            copy.wait()
        w = w_s[...]
        scaled_up = (up_s[...].astype(F32) * w).astype(BF16)
        rows_out[0:RANK, :] = down_s[...].T
        rows_out[RANK : 2 * RANK, :] = scaled_up
        v = w * (1.0 + bias_s[...])
        high = v.astype(BF16).astype(F32)
        at = lax.broadcasted_iota(jnp.int32, (EXT, COLS), 0)
        rows_out[2 * RANK :, :] = jnp.where(at < 2, high, jnp.where(at == 2, v - high, 0.0)).astype(BF16)
        cols_out[:, 0:RANK] = down_s[...]
        cols_out[:, RANK:] = scaled_up.T
        k = place_ref[2] * NC + place_ref[3]
        strip = pl.multiple_of((place_ref[1] * 2 + lax.div(k, 4)) * 128, 128)
        offset = lax.rem(k, 4) * 32
        lane = lax.broadcasted_iota(jnp.int32, (32, 128), 1)
        row = lax.broadcasted_iota(jnp.int32, (32, 128), 0)
        own = lane == row + offset
        w_own = jnp.sum(jnp.where(own, w_s[:, pl.ds(strip, 128)], 0.0), axis=1, keepdims=True)
        bias_own = jnp.sum(jnp.where(own, bias_s[:, pl.ds(strip, 128)], 0.0), axis=1, keepdims=True)
        place_own = (row + offset).astype(F32)
        own_out[...] = jnp.where(lane == 0, w_own, jnp.where(lane == 1, bias_own, place_own))
        up_out[...] = dot(jnp.where(own, 1.0, 0.0).astype(BF16), up_s[:, pl.ds(strip, 128)], 1, 1)

    return call(
        body,
        [
            pltpu.VMEM((2 * RANK + EXT, COLS), BF16),
            pltpu.VMEM((COLS, 2 * RANK), BF16),
            pltpu.VMEM((32, 128), F32),
            pltpu.VMEM((32, RANK), F32),
        ],
        (place, *(far(v) for v in (down, up, w, bias))),
        [IN_SMEM] + [IN_HBM] * 4,
        [
            pltpu.VMEM((COLS, RANK), BF16),
            pltpu.VMEM((RANK, COLS), BF16),
            pltpu.VMEM((1, COLS), F32),
            pltpu.VMEM((1, COLS), F32),
            pltpu.SemaphoreType.DMA((4,)),
        ],
        cost=pl.CostEstimate(flops=1 << 30, bytes_accessed=6 << 20, transcendentals=0),
    )


def head_of(rows_ref, pooled):
    head = dot(rows_ref[2 * RANK :, :], pooled, 1, 0)
    sums = head[0:1] + head[2:3]
    high = sums.astype(BF16).astype(F32)
    at = lax.broadcasted_iota(jnp.int32, (EXT, pooled.shape[1]), 0)
    return jnp.where(at == 0, high, jnp.where(at == 1, sums - high, 0.0)).astype(BF16)


def forward_far(place, arrived, other, rows, counts_t):
    def body(place_ref, in_ref, other_ref, rows_ref, counts_ref, pooled_ref, slab_out, sent, c1, c2, c3, held, sems):
        copies = strips(place_ref, counts_ref, held, sems, range(1))
        for _, _, copy in copies:
            copy.start()
        low_core = place_ref[3] == 0
        for y in range(NY):
            at = slice(y * 512, (y + 1) * 512)
            own, partner = in_ref[at, FAR:].T, other_ref[at, :].T
            slab = jnp.concatenate(
                [jnp.where(low_core, own, partner), jnp.where(low_core, partner, own)], axis=0
            )
            table = slice(y * EMBED, (y + 1) * EMBED)
            slab_out[table, :] = slab
            pooled_ref[table, :] = dot(slab, in_ref[at, :FAR], 1, 0).astype(BF16)
        pooled = pooled_ref[...]
        for part in range(4):
            at = slice(part * 256, (part + 1) * 256)
            product = dot(rows_ref[at, :], pooled, 1, 0).astype(BF16)
            for i, out in enumerate((c1, c2, c3)):
                out[at, :] = product[:, i * OWN : (i + 1) * OWN]
        ext = head_of(rows_ref, pooled)
        for i, out in enumerate((c1, c2, c3)):
            out[2 * RANK :, :] = ext[:, i * OWN : (i + 1) * OWN]
        unpack(copies, held, sent)

    return call(
        body,
        [
            pltpu.VMEM((COLS, FAR), BF16),
            pltpu.VMEM((COLS, 512), BF16),
            pltpu.VMEM((PEERS, ROWS, OWN), BF16),
        ]
        + [pltpu.VMEM((2 * RANK + EXT, OWN), BF16)] * (NZ - 1),
        (place, near(arrived), near(other), near(rows), far(counts_t)),
        [IN_SMEM] + [IN_VMEM] * 3 + [IN_HBM],
        strip_scratch(1),
        cost=pl.CostEstimate(flops=3 << 30, bytes_accessed=4 << 20, transcendentals=0),
    )


def forward_own(arrived, slab, rows):
    def body(in_ref, slab_ref, rows_ref, pooled_ref, out):
        for y in range(NY):
            table = slice(y * EMBED, (y + 1) * EMBED)
            pooled_ref[table, :] = dot(slab_ref[table, :], in_ref[y * 512 : (y + 1) * 512, :], 1, 0).astype(BF16)
        pooled = pooled_ref[...]
        out[0 : 2 * RANK, :] = dot(rows_ref[0 : 2 * RANK, :], pooled, 1, 0).astype(BF16)
        out[2 * RANK :, :] = head_of(rows_ref, pooled)

    return call(
        body,
        [pltpu.VMEM((COLS, OWN), BF16), pltpu.VMEM((2 * RANK + EXT, OWN), BF16)],
        (near(arrived), near(slab), near(rows)),
        cost=pl.CostEstimate(flops=1 << 30, bytes_accessed=1 << 20, transcendentals=0),
    )


def own_samples(parts, labels):
    def body(p0, p1, p2, p3, labels_ref, out):
        def total(rows):
            a, b, c, d = (p[rows, :].astype(F32) for p in (p0, p1, p2, p3))
            return (a + b) + (c + d)

        squeezed = total(slice(0, RANK)).astype(BF16).astype(F32)
        other = total(slice(RANK, 2 * RANK))
        ext = total(slice(2 * RANK, 2 * RANK + EXT))
        logits = ext[0:1] + ext[1:2] + jnp.sum(squeezed * other, axis=0, keepdims=True)
        g = jax.nn.sigmoid(logits) - labels_ref[...].astype(F32)
        out[0:RANK, :] = (g * other).astype(BF16)
        out[RANK : 2 * RANK, :] = (g * squeezed).astype(BF16)
        high = g.astype(BF16).astype(F32)
        at = lax.broadcasted_iota(jnp.int32, (EXT, OWN), 0)
        rows = jnp.where((at == 0) | (at == 2), high, jnp.where(at == 1, g - high, 0.0))
        out[2 * RANK :, :] = rows.astype(BF16)

    return call(body, [pltpu.VMEM((2 * RANK + EXT, OWN), BF16)], (*(near(p) for p in parts), labels))[0]


def weight_sums(pooled, g, both_of, sums_of):
    for j in range(4):
        both_of(j, dot(pooled, g[j * 256 : (j + 1) * 256], 1, 1))
    sums_of(dot(g[2 * RANK :], pooled, 1, 1))


def slab_sums(y, counts, g, rows_ref, cols_ref):
    table = slice(y * EMBED, (y + 1) * EMBED)
    grad_pooled = (
        dot(cols_ref[table, :], g[: 2 * RANK], 1, 0) + dot(rows_ref[2 * RANK :, table], g[2 * RANK :], 0, 0)
    ).astype(BF16)
    return dot(counts, grad_pooled, 1, 1)


def backward_first(block0, block3, pooled0, pooled_far, arrived0, arrived, rows, cols):
    def body(b0, b3, pooled0_ref, pooled_ref, in0_ref, in_ref, rows_ref, cols_ref, both_out, sums_out, slab_out):
        g = jnp.concatenate([b0[...], b3[...]], axis=1)
        pooled = jnp.concatenate([pooled0_ref[...], pooled_ref[:, 2 * OWN :]], axis=1)

        def both_of(j, value):
            both_out[:, j * 256 : (j + 1) * 256] = value

        def sums_of(value):
            sums_out[...] = value

        weight_sums(pooled, g, both_of, sums_of)
        for y in range(NY):
            at = slice(y * 512, (y + 1) * 512)
            counts = jnp.concatenate([in0_ref[at, :], in_ref[at, 2 * OWN : FAR]], axis=1)
            slab_out[at, :] = slab_sums(y, counts, g, rows_ref, cols_ref)

    return call(
        body,
        [
            pltpu.VMEM((COLS, 2 * RANK), F32),
            pltpu.VMEM((EXT, COLS), F32),
            pltpu.VMEM((PEERS * ROWS, EMBED), F32),
        ],
        tuple(near(v) for v in (block0, block3, pooled0, pooled_far, arrived0, arrived, rows, cols)),
        cost=pl.CostEstimate(flops=2 << 30, bytes_accessed=6 << 20, transcendentals=0),
    )


def put(low_core, mine, other, targets, at, value):
    pair = value.astype(BF16).reshape(-1, NC, *value.shape[1:])
    even, odd = pair[:, 0], pair[:, 1]
    mine[targets, at, :] = jnp.where(low_core, even, odd)
    other[targets, at, :] = jnp.where(low_core, odd, even)


EVERYONE = slice(0, NY * NX)


def backward_weights(place, block1, block2, pooled_far, both, sums):
    def body(place_ref, b1, b2, pooled_ref, both_ref, sums_ref, mine, other):
        low_core = place_ref[3] == 0
        g = jnp.concatenate([b1[...], b2[...]], axis=1)

        def both_of(j, value):
            for h in range(2):
                at = (2 * j + h) * 128
                held = both_ref[:, at : at + 128] + value[:, h * 128 : (h + 1) * 128]
                to = slice((2 * j + h) * 32, (2 * j + h + 1) * 32)
                put(low_core, mine, other, EVERYONE, to, held.reshape(PEERS, 32, 128))

        def sums_of(value):
            held = (value + sums_ref[...]).astype(BF16)
            for strip in range(8):
                row = held[:, strip * 128 : (strip + 1) * 128]
                for i in range(2):
                    mine[strip * 2 + i, 256:, :] = row
                    other[strip * 2 + i, 256:, :] = row

        weight_sums(pooled_ref[:, : 2 * OWN], g, both_of, sums_of)

    return call(
        body,
        [pltpu.VMEM((NY * NX, 272, 128), BF16)] * 2,
        (place, *(near(v) for v in (block1, block2, pooled_far, both, sums))),
        [IN_SMEM] + [IN_VMEM] * 5,
        cost=pl.CostEstimate(flops=1 << 30, bytes_accessed=4 << 20, transcendentals=0),
    )


def backward_slab(place, block1, block2, arrived, rows, cols, slab_first):
    def body(place_ref, b1, b2, in_ref, rows_ref, cols_ref, first_ref, mine, other):
        low_core = place_ref[3] == 0
        g = jnp.concatenate([b1[...], b2[...]], axis=1)
        for y in range(NY):
            at = slice(y * 512, (y + 1) * 512)
            slab = first_ref[at, :] + slab_sums(y, in_ref[at, : 2 * OWN], g, rows_ref, cols_ref)
            for j in range(2):
                put(
                    low_core,
                    mine,
                    other,
                    slice(y * NX, (y + 1) * NX),
                    slice(j * ROWS, (j + 1) * ROWS),
                    slab[:, j * 128 : (j + 1) * 128].reshape(NK, ROWS, 128),
                )

    return call(
        body,
        [pltpu.VMEM((NY * NX, 2 * ROWS, 128), BF16)] * 2,
        (place, *(near(v) for v in (block1, block2, arrived, rows, cols, slab_first))),
        [IN_SMEM] + [IN_VMEM] * 6,
        cost=pl.CostEstimate(flops=1 << 30, bytes_accessed=4 << 20, transcendentals=0),
    )


def pair_sums(slab, slab_partner, weights, weights_partner):
    def body(a, b, c, d, out):
        out[:, : 2 * ROWS, :] = (a[...].astype(F32) + b[...].astype(F32)).astype(BF16)
        out[:, 2 * ROWS :, :] = (c[...].astype(F32) + d[...].astype(F32)).astype(BF16)

    return call(
        body,
        [pltpu.VMEM((NY * NX, PACK, 128), BF16)],
        tuple(near(v) for v in (slab, slab_partner, weights, weights_partner)),
    )[0]


def finish(shares, own, up_own):
    def body(in_ref, own_ref, up_ref, slab_out, down_out, up_out, bias_out, out_out):
        def total(at):
            held = in_ref[0, at, :].astype(F32)
            for i in range(1, NY * NX):
                held = held + in_ref[i, at, :].astype(F32)
            return held

        slab_out[:, :128] = total(slice(0, ROWS))
        slab_out[:, 128:] = total(slice(ROWS, 2 * ROWS))
        both = [total(slice(128 + j * 32, 160 + j * 32)) for j in range(8)]
        for j in range(4):
            down_out[:, j * 128 : (j + 1) * 128] = both[j].astype(BF16)
        product = jnp.concatenate(both[4:], axis=1)
        w_own, bias_own = own_ref[:, 0:1], own_ref[:, 1:2]
        up_out[...] = (product * w_own).astype(BF16)
        lane = lax.broadcasted_iota(jnp.int32, (32, 128), 1)
        row = lax.broadcasted_iota(jnp.int32, (32, 128), 0)
        last = total(slice(384, 400))
        own = lane.astype(F32) == own_ref[:, 2:3]
        sums = jnp.sum(jnp.where(own, last[0:1] + last[1:2], 0.0), axis=1, keepdims=True)
        out = (1.0 + bias_own) * sums + jnp.sum(product * up_ref[...], axis=1, keepdims=True)
        bias_out[...] = jnp.sum(jnp.where(lane == row, w_own * sums, 0.0), axis=0, keepdims=True)[:, :32]
        out_out[...] = jnp.sum(jnp.where(lane == row, out, 0.0), axis=0, keepdims=True)[:, :32]

    return call(
        body,
        [
            jax.ShapeDtypeStruct((ROWS, EMBED), F32),
            jax.ShapeDtypeStruct((32, RANK), BF16),
            jax.ShapeDtypeStruct((32, RANK), BF16),
            jax.ShapeDtypeStruct((1, 32), F32),
            jax.ShapeDtypeStruct((1, 32), F32),
        ],
        (near(shares), near(own), near(up_own)),
    )


def local(slab, counts, cross_down, cross_up, cross_bias, out_weight, labels):
    place = jnp.stack([lax.axis_index(a) for a in ALL]).astype(jnp.int32)
    counts_t = counts.T
    rows, cols, own, up_own = prepare(
        place, cross_down, cross_up, out_weight.reshape(1, -1), cross_bias.reshape(1, -1)
    )
    sent = pack_counts(place, counts_t, slab)
    arrived = lax.all_to_all(sent, PLANE, 0, 0, tiled=True).reshape(PEERS * ROWS, FAR + HALF)
    other = shift(arrived[:, FAR:], dc=1)
    pooled, slab_t, sent0, *chunks = forward_far(place, arrived, other, rows, counts_t)
    parts = []
    for i in range(1, NZ):
        parts.append(shift(chunks[i - 1], dz=i))
    arrived0 = lax.all_to_all(sent0, PLANE, 0, 0, tiled=True).reshape(PEERS * ROWS, OWN)
    pooled0, chunk0 = forward_own(arrived0, slab_t, rows)
    block0 = own_samples([chunk0] + parts, labels.reshape(1, OWN))
    block1, block2, block3 = (shift(block0, dz=-i) for i in range(1, NZ))
    both, sums, slab_first = backward_first(block0, block3, pooled0, pooled, arrived0, arrived, rows, cols)
    weights, given = backward_weights(place, block1, block2, pooled, both, sums)
    weights_partner = shift(given, dc=1)
    slabs, given = backward_slab(place, block1, block2, arrived, rows, cols, slab_first)
    paired = pair_sums(slabs, shift(given, dc=1), weights, weights_partner)
    shares = lax.all_to_all(paired, ("y", "x"), 0, 0, tiled=True)
    grad_slab, grad_down, grad_up, grad_bias, grad_out = finish(shares, own, up_own)
    return grad_slab, grad_down, grad_up.T, grad_bias.reshape(32), grad_out.reshape(32)


def solution(mesh):
    torus = Mesh(mesh.devices.reshape(NZ, NY, NX, NC), ALL)
    return jax.shard_map(
        local,
        mesh=torus,
        in_specs=(P(ALL, None), P(None, ALL), P(), P(), P(), P(), P(ALL)),
        out_specs=(P(ALL, None), P(ALL, None), P(None, ALL), P(ALL), P(ALL)),
        check_vma=False,
    )
```

profile of v0, /device:TPU:0, one launch (start us, length us, event | category | flops | bytes accessed | tf_op | source)
XLA Modules:
  0.0 128.2 jit_solution(7362691828108256436)
XLA Ops:
  0.6 0.1 pad_add_fusion.place_ref
  0.7 2.7 %shard_map.110 = bf16[32,64,512]{2,1,0:T(8,128)(2,1)S(1)} custom-call(s32[4]{0:T(128)S(1)} %pad_add_fusion.place_ref, s32[64,16384]{1,0:T(8,128)} %bitcast.20, bf16[64,256]{1,0:T(8,128)(2,1)} %slab_ref.1), custom_call_target="tpu_custom_call" | custom-call | tf_op jit(solution)/shard_map/pallas_call | solution.py:57
  3.4 35.7 %all_to_all.15 = bf16[32,64,512]{2,1,0:T(8,128)(2,1)S(1)} all-to-all(bf16[32,64,512]{2,1,0:T(8,128)(2,1)S(1)} %shard_map.110), channel_id=1, replica_groups=mesh['z'=4,'y'=4,'x'=4,'c'=2] {'y','x','c'}, dimensions={0} | all-to-all | bytes 4194304 | tf_op jit(solution)/shard_map/all_to_all | solution.py:429
  39.1 0.1 slice.4
  39.1 0.2 collective-permute-start
  39.3 3.0 %shard_map.111 = (bf16[1040,1024]{1,0:T(8,128)(2,1)S(1)}, bf16[1024,1024]{1,0:T(8,128)(2,1)S(1)}, f32[32,128]{1,0:T(8,128)S(1)}, f32[32,512]{1,0:T(8,128)S(1)}) custom-call(s32[4]{0:T(128)S(1)} %pad_add_fusion.place_ref, bf16[4096,512]{1,0:T(8,128)(2,1)} %down_ref.1, bf16[512,4096]{1,0:T(8,128)(2,1)} %up_ref.1, f32[1,4096]{1,0:T(1,128)} %bitcast.22, ...), custom_call_target="tpu_custom_call" | custom-call | flops 1073741824 | bytes 6291456 | tf_op jit(solution)/shard_map/pallas_call | solution.py:57
  42.3 0.0 copy-start
  42.3 0.0 copy-start.3
  42.3 0.0 collective-permute-done.other_ref
  42.3 3.6 %shard_map.112 = (bf16[1024,384]{1,0:T(8,128)(2,1)S(1)}, bf16[1024,512]{1,0:T(8,128)(2,1)S(1)}, bf16[32,64,128]{2,1,0:T(8,128)(2,1)S(1)}, bf16[1040,128]{1,0:T(8...) custom-call(s32[4]{0:T(128)S(1)} %pad_add_fusion.place_ref, bf16[2048,512]{1,0:T(8,128)(2,1)S(1)} %bitcast.14, ...), custom_call_target="tpu_custom_call" | custom-call | flops 3221225472 | bytes 4194304 | tf_op jit(solution)/shard_map/pallas_call | solution.py:57
  46.0 0.0 copy-done
  46.0 0.0 copy-done.3
  46.0 0.0 copy-start.5
  46.0 0.8 copy-done.5
  46.8 0.0 copy-start.7
  46.8 0.7 copy-done.7
  47.5 0.0 copy-start.8
  47.5 0.7 copy-done.8
  48.2 0.0 copy-start.9
  48.2 0.7 copy-done.9
  48.9 0.0 copy-start.10
  48.9 1.0 copy-done.10
  49.9 3.9 %all-to-all-start.1 = ((bf16[32,64,128]{2,1,0:T(8,128)(2,1)}), bf16[32,64,128]{2,1,0:T(8,128)(2,1)S(1)}, u32[]{:S(2)}, u32[]{:S(2)}) async-start(bf16[32,64,128]{2,1,0:T(8,128)(2,1)} %copy-done.5), calls=%async_computation.1 | async-start | bytes 1048576 | tf_op jit(solution)/shard_map/all_to_all | solution.py:435
  53.9 0.0 copy-start.6
  53.9 2.0 %collective-permute-start.1 = (bf16[1040,128]{1,0:T(8,128)(2,1)}, bf16[1040,128]{1,0:T(8,128)(2,1)}, u32[]{:S(2)}, u32[]{:S(2)}) collective-permute-start(bf16[1040,128]{1,0:T(8,128)(2,1)} %copy-done.9), channel_id=1, source_target_pairs={{0,32},{1,33},{2,34},{3,35},{4,36},{5,37},{6,38},{7,39},{8,40},{9,... | collective-permute-start | bytes 798728 | tf_op jit(solution)/shard_map/ppermute | solution.py:45
  55.9 3.6 %collective-permute-start.2 = (bf16[1040,128]{1,0:T(8,128)(2,1)}, bf16[1040,128]{1,0:T(8,128)(2,1)}, u32[]{:S(2)}, u32[]{:S(2)}) collective-permute-start(bf16[1040,128]{1,0:T(8,128)(2,1)} %copy-done.8), channel_id=1, source_target_pairs={{0,64},{1,65},{2,66},{3,67},{4,68},{5,69},{6,70},{7,71},{8,72},{9,... | collective-permute-start | bytes 798728 | tf_op jit(solution)/shard_map/ppermute | solution.py:45
  59.5 1.0 collective-permute-start.3
  60.4 5.0 %all-to-all-done.1 = bf16[32,64,128]{2,1,0:T(8,128)(2,1)S(1)} async-done(((bf16[32,64,128]{2,1,0:T(8,128)(2,1)}), bf16[32,64,128]{2,1,0:T(8,128)(2,1)S(1)}, u32[]{:S(2)}, u32[]{:S(2)}) %all-to-all-start.1) | async-done | bytes 524320 | tf_op jit(solution)/shard_map/all_to_all | solution.py:435
  65.4 0.0 copy-start.1
  65.4 1.6 %copy-done.1 = bf16[1040,1024]{1,0:T(8,128)(2,1)S(1)} copy-done((bf16[1040,1024]{1,0:T(8,128)(2,1)S(1)}, bf16[1040,1024]{1,0:T(8,128)(2,1)}, u32[]{:S(2)}) %copy-start.1) | copy-done | bytes 2129944
  67.0 0.0 copy-start.11
  67.0 1.2 copy-done.11
  68.3 0.0 copy-start.2
  68.3 0.0 copy-start.4
  68.3 1.1 shard_map.113
  69.3 0.0 collective-permute-done.1.p1
  69.4 2.7 %collective-permute-done.2.p2 = bf16[1040,128]{1,0:T(8,128)(2,1)} collective-permute-done((bf16[1040,128]{1,0:T(8,128)(2,1)}, bf16[1040,128]{1,0:T(8,128)(2,1)}, u32[]{:S(2)}, u32[]{:S(2)}) %collective-permute-start.2) | collective-permute-done | bytes 266272 | tf_op jit(solution)/shard_map/ppermute | solution.py:45
  72.0 0.0 collective-permute-done.3.p3
  72.0 0.0 copy-done.6
  72.0 1.4 %shard_map.114.b0 = bf16[1040,128]{1,0:T(8,128)(2,1)S(1)} custom-call(bf16[1040,128]{1,0:T(8,128)(2,1)S(1)} %get-tuple-element.32.p0, bf16[1040,128]{1,0:T(8,128)(2,1)} %collective-permute-done.1.p1, bf16[1040,128]{1,0:T(8,128)(2,1)} %collective-permute-done.2.p2, bf16[1040,128]{1,0:T(8,128)(2,1)} %collective-permute-done.3.p3, s32[1,128]{1,0:T(1,128)S(1)} %bitcast.19), custom_call_target="tpu_custom_call" | custom-call | tf_op jit(solution)/shard_map/pallas_call | solution.py:57
  73.4 1.3 %collective-permute-start.6 = (bf16[1040,128]{1,0:T(8,128)(2,1)S(1)}, bf16[1040,128]{1,0:T(8,128)(2,1)S(1)}, u32[]{:S(2)}, u32[]{:S(2)}) collective-permute-start(bf16[1040,128]{1,0:T(8,128)(2,1)S(1)} %shard_map.114.b0), channel_id=1, source_target_pairs={{0,32},{1,33},{2,34},{3,35},{4,36},{5,37},{6,38},{7,39},{8,40},{9,... | collective-permute-start | bytes 798728 | tf_op jit(solution)/shard_map/ppermute | solution.py:45
  74.7 2.4 %collective-permute-start.5 = (bf16[1040,128]{1,0:T(8,128)(2,1)S(1)}, bf16[1040,128]{1,0:T(8,128)(2,1)S(1)}, u32[]{:S(2)}, u32[]{:S(2)}) collective-permute-start(bf16[1040,128]{1,0:T(8,128)(2,1)S(1)} %shard_map.114.b0), channel_id=1, source_target_pairs={{0,64},{1,65},{2,66},{3,67},{4,68},{5,69},{6,70},{7,71},{8,72},{9,... | collective-permute-start | bytes 798728 | tf_op jit(solution)/shard_map/ppermute | solution.py:45
  77.1 1.2 collective-permute-start.4
  78.3 4.1 %collective-permute-done.6.b3 = bf16[1040,128]{1,0:T(8,128)(2,1)S(1)} collective-permute-done((bf16[1040,128]{1,0:T(8,128)(2,1)S(1)}, bf16[1040,128]{1,0:T(8,128)(2,1)S(1)}, u32[]{:S(2)}, u32[]{:S(2)}) %collective-permute-start.6) | collective-permute-done | bytes 266272 | tf_op jit(solution)/shard_map/ppermute | solution.py:45
  82.4 0.0 copy-done.2
  82.4 0.0 copy-done.4
  82.4 3.2 %shard_map.115 = (f32[1024,1024]{1,0:T(8,128)S(1)}, f32[16,1024]{1,0:T(8,128)S(1)}, f32[2048,256]{1,0:T(8,128)S(1)}) custom-call(bf16[1040,128]{1,0:T(8,128)(2,1)S(1)} %shard_map.114.b0, bf16[1040,128]{1,0:T(8,128)(2,1)S(1)} %collective-permute-done.6.b3, bf16[1024,128]{1,0:T(8,128)(2,1)S(1)} %get-tuple-element.37.pooled0_ref, ...), custom_call_target="tpu_custom_call" | custom-call | flops 2147483648 | bytes 6291456 | tf_op jit(solution)/shard_map/pallas_call | solution.py:57
  85.6 3.5 %collective-permute-done.5.b2 = bf16[1040,128]{1,0:T(8,128)(2,1)S(1)} collective-permute-done((bf16[1040,128]{1,0:T(8,128)(2,1)S(1)}, bf16[1040,128]{1,0:T(8,128)(2,1)S(1)}, u32[]{:S(2)}, u32[]{:S(2)}) %collective-permute-start.5) | collective-permute-done | bytes 266272 | tf_op jit(solution)/shard_map/ppermute | solution.py:45
  89.1 0.0 collective-permute-done.4.b1
  89.1 1.4 %shard_map.117 = (bf16[16,272,128]{2,1,0:T(8,128)(2,1)S(1)}, bf16[16,272,128]{2,1,0:T(8,128)(2,1)S(1)}) custom-call(s32[4]{0:T(128)S(1)} %pad_add_fusion.place_ref, bf16[1040,128]{1,0:T(8,128)(2,1)S(1)} %collective-permute-done.4.b1, bf16[1040,128]{1,0:T(8,128)(2,1)S(1)} %collective-permute-done.5.b2, bf16[1024,384]{1,0:T(8,128)(2,1)S(1)} %get-tuple-element.38.pooled_ref, ...), custom_call_target="tpu_custom_call" | custom-call | flops 1073741824 | bytes 4194304 | tf_op jit(solution)/shard_map/pallas_call | solution.py:57
  90.5 0.2 collective-permute-start.8
  90.7 3.1 %shard_map.116 = (bf16[16,128,128]{2,1,0:T(8,128)(2,1)S(1)}, bf16[16,128,128]{2,1,0:T(8,128)(2,1)S(1)}) custom-call(s32[4]{0:T(128)S(1)} %pad_add_fusion.place_ref, bf16[1040,128]{1,0:T(8,128)(2,1)S(1)} %collective-permute-done.4.b1, bf16[1040,128]{1,0:T(8,128)(2,1)S(1)} %collective-permute-done.5.b2, bf16[2048,512]{1,0:T(8,128)(2,1)S(1)} %bitcast.16, ...), custom_call_target="tpu_custom_call" | custom-call | flops 1073741824 | bytes 4194304 | tf_op jit(solution)/shard_map/pallas_call | solution.py:57
  93.9 0.6 collective-permute-start.7
  94.4 1.5 %collective-permute-done.7.b = bf16[16,128,128]{2,1,0:T(8,128)(2,1)S(1)} collective-permute-done((bf16[16,128,128]{2,1,0:T(8,128)(2,1)S(1)}, bf16[16,128,128]{2,1,0:T(8,128)(2,1)S(1)}, u32[]{:S(2)}, u32[]{:S(2)}) %collective-permute-start.7) | collective-permute-done | bytes 524320 | tf_op jit(solution)/shard_map/ppermute | solution.py:45
  96.0 0.0 collective-permute-done.8.d
  96.0 0.4 shard_map.118
  96.3 30.9 %all_to_all.16.in_ref = bf16[16,400,128]{2,1,0:T(8,128)(2,1)S(1)} all-to-all(bf16[16,400,128]{2,1,0:T(8,128)(2,1)S(1)} %shard_map.118), channel_id=1, replica_groups=mesh['z'=4,'y'=4,'x'=4,'c'=2] {'y','x'}, dimensions={0} | all-to-all | bytes 3276800 | tf_op jit(solution)/shard_map/all_to_all | solution.py:444
  127.2 0.9 shard_map.119
Async XLA Ops:
  39.1 3.2 %collective-permute-start = (bf16[2048,128]{1,0:T(8,128)(2,1)S(1)}, bf16[2048,128]{1,0:T(8,128)(2,1)S(1)}, u32[]{:S(2)}, u32[]{:S(2)}) collective-permute-start(bf16[2048,128]{1,0:T(8,128)(2,1)S(1)} %slice.4), channel_id=1, source_target_pairs={{0,1},{1,0},{2,3},{3,2},{4,5},{5,4},{6,7},{7,6},{8,9},{9,8},{10,11... | collective-permute-start | bytes 1572872 | tf_op jit(solution)/shard_map/ppermute | solution.py:45
  42.3 3.7 %copy-start = (bf16[1040,1024]{1,0:T(8,128)(2,1)}, bf16[1040,1024]{1,0:T(8,128)(2,1)S(1)}, u32[]{:S(2)}) copy-start(bf16[1040,1024]{1,0:T(8,128)(2,1)S(1)} %get-tuple-element.29.rows_ref) | copy-start | bytes 6389764
  42.3 3.7 %copy-start.3 = (bf16[1024,1024]{1,0:T(8,128)(2,1)}, bf16[1024,1024]{1,0:T(8,128)(2,1)S(1)}, u32[]{:S(2)}) copy-start(bf16[1024,1024]{1,0:T(8,128)(2,1)S(1)} %get-tuple-element.36.cols_ref) | copy-start | bytes 6291460
  46.0 0.8 copy-start.5
  46.8 0.7 copy-start.7
  47.5 0.7 copy-start.8
  48.2 0.7 copy-start.9
  48.9 1.0 copy-start.10
  49.9 15.5 %all-to-all-start.1 = ((bf16[32,64,128]{2,1,0:T(8,128)(2,1)}), bf16[32,64,128]{2,1,0:T(8,128)(2,1)S(1)}, u32[]{:S(2)}, u32[]{:S(2)}) async-start(bf16[32,64,128]{2,1,0:T(8,128)(2,1)} %copy-done.5), calls=%async_computation.1 | async-start | bytes 1048576 | tf_op jit(solution)/shard_map/all_to_all | solution.py:435
  53.9 18.2 %copy-start.6 = (s32[128]{0:T(128)S(1)}, s32[128]{0:T(128)}, u32[]{:S(2)}) copy-start(s32[128]{0:T(128)} %param.13) | copy-start | bytes 1540
  53.9 15.5 %collective-permute-start.1 = (bf16[1040,128]{1,0:T(8,128)(2,1)}, bf16[1040,128]{1,0:T(8,128)(2,1)}, u32[]{:S(2)}, u32[]{:S(2)}) collective-permute-start(bf16[1040,128]{1,0:T(8,128)(2,1)} %copy-done.9), channel_id=1, source_target_pairs={{0,32},{1,33},{2,34},{3,35},{4,36},{5,37},{6,38},{7,39},{8,40},{9,... | collective-permute-start | bytes 798728 | tf_op jit(solution)/shard_map/ppermute | solution.py:45
  55.9 16.2 %collective-permute-start.2 = (bf16[1040,128]{1,0:T(8,128)(2,1)}, bf16[1040,128]{1,0:T(8,128)(2,1)}, u32[]{:S(2)}, u32[]{:S(2)}) collective-permute-start(bf16[1040,128]{1,0:T(8,128)(2,1)} %copy-done.8), channel_id=1, source_target_pairs={{0,64},{1,65},{2,66},{3,67},{4,68},{5,69},{6,70},{7,71},{8,72},{9,... | collective-permute-start | bytes 798728 | tf_op jit(solution)/shard_map/ppermute | solution.py:45
  59.5 12.6 %collective-permute-start.3 = (bf16[1040,128]{1,0:T(8,128)(2,1)}, bf16[1040,128]{1,0:T(8,128)(2,1)}, u32[]{:S(2)}, u32[]{:S(2)}) collective-permute-start(bf16[1040,128]{1,0:T(8,128)(2,1)} %copy-done.7), channel_id=1, source_target_pairs={{0,96},{1,97},{2,98},{3,99},{4,100},{5,101},{6,102},{7,103},{8,104... | collective-permute-start | bytes 798728 | tf_op jit(solution)/shard_map/ppermute | solution.py:45
  65.4 1.6 %copy-start.1 = (bf16[1040,1024]{1,0:T(8,128)(2,1)S(1)}, bf16[1040,1024]{1,0:T(8,128)(2,1)}, u32[]{:S(2)}) copy-start(bf16[1040,1024]{1,0:T(8,128)(2,1)} %copy-done) | copy-start | bytes 6389764
  67.0 1.2 copy-start.11
  68.3 14.2 %copy-start.2 = (bf16[1040,1024]{1,0:T(8,128)(2,1)S(1)}, bf16[1040,1024]{1,0:T(8,128)(2,1)}, u32[]{:S(2)}) copy-start(bf16[1040,1024]{1,0:T(8,128)(2,1)} %copy-done) | copy-start | bytes 6389764
  68.3 14.2 %copy-start.4 = (bf16[1024,1024]{1,0:T(8,128)(2,1)S(1)}, bf16[1024,1024]{1,0:T(8,128)(2,1)}, u32[]{:S(2)}) copy-start(bf16[1024,1024]{1,0:T(8,128)(2,1)} %copy-done.3) | copy-start | bytes 6291460
  73.4 9.0 %collective-permute-start.6 = (bf16[1040,128]{1,0:T(8,128)(2,1)S(1)}, bf16[1040,128]{1,0:T(8,128)(2,1)S(1)}, u32[]{:S(2)}, u32[]{:S(2)}) collective-permute-start(bf16[1040,128]{1,0:T(8,128)(2,1)S(1)} %shard_map.114.b0), channel_id=1, source_target_pairs={{0,32},{1,33},{2,34},{3,35},{4,36},{5,37},{6,38},{7,39},{8,40},{9,... | collective-permute-start | bytes 798728 | tf_op jit(solution)/shard_map/ppermute | solution.py:45
  74.7 14.4 %collective-permute-start.5 = (bf16[1040,128]{1,0:T(8,128)(2,1)S(1)}, bf16[1040,128]{1,0:T(8,128)(2,1)S(1)}, u32[]{:S(2)}, u32[]{:S(2)}) collective-permute-start(bf16[1040,128]{1,0:T(8,128)(2,1)S(1)} %shard_map.114.b0), channel_id=1, source_target_pairs={{0,64},{1,65},{2,66},{3,67},{4,68},{5,69},{6,70},{7,71},{8,72},{9,... | collective-permute-start | bytes 798728 | tf_op jit(solution)/shard_map/ppermute | solution.py:45
  77.1 12.0 %collective-permute-start.4 = (bf16[1040,128]{1,0:T(8,128)(2,1)S(1)}, bf16[1040,128]{1,0:T(8,128)(2,1)S(1)}, u32[]{:S(2)}, u32[]{:S(2)}) collective-permute-start(bf16[1040,128]{1,0:T(8,128)(2,1)S(1)} %shard_map.114.b0), channel_id=1, source_target_pairs={{0,96},{1,97},{2,98},{3,99},{4,100},{5,101},{6,102},{7,103},{8,104... | collective-permute-start | bytes 798728 | tf_op jit(solution)/shard_map/ppermute | solution.py:45
  90.5 5.5 %collective-permute-start.8 = (bf16[16,272,128]{2,1,0:T(8,128)(2,1)S(1)}, bf16[16,272,128]{2,1,0:T(8,128)(2,1)S(1)}, u32[]{:S(2)}, u32[]{:S(2)}) collective-permute-start(bf16[16,272,128]{2,1,0:T(8,128)(2,1)S(1)} %get-tuple-element.45), channel_id=1, source_target_pairs={{0,1},{1,0},{2,3},{3,2},{4,5},{5,4},{6,7},{7,6},{8,9},{9,8},{10,11... | collective-permute-start | bytes 3342344 | tf_op jit(solution)/shard_map/ppermute | solution.py:45
  93.9 2.1 %collective-permute-start.7 = (bf16[16,128,128]{2,1,0:T(8,128)(2,1)S(1)}, bf16[16,128,128]{2,1,0:T(8,128)(2,1)S(1)}, u32[]{:S(2)}, u32[]{:S(2)}) collective-permute-start(bf16[16,128,128]{2,1,0:T(8,128)(2,1)S(1)} %get-tuple-element.41), channel_id=1, source_target_pairs={{0,1},{1,0},{2,3},{3,2},{4,5},{5,4},{6,7},{7,6},{8,9},{9,8},{10,11... | collective-permute-start | bytes 1572872 | tf_op jit(solution)/shard_map/ppermute | solution.py:45
where the time goes:
time: 129 us; the launch traced here: 128 us
  blocking collectives  66.5 us (52%)
  Pallas kernels  20.7 us (16%)
  waiting for transfers between devices  16.8 us (13%)
  starting transfers between devices  16.4 us (13%)
  local copies, waits for them, and re-layouts  6.84 us (5%)
    all_to_all x1, blocking collectives, local(): lax.all_to_all(sent, PLANE, 0, 0, tiled=True)  35.7 us
    all_to_all x1, blocking collectives, local(): shares = lax.all_to_all(paired, ('y', 'x'), 0, 0, tiled=True)  30.9 us
    pallas_call x10, Pallas kernels, call(): pl.pallas_call(body, in_specs=specs or [pl.BlockSpec(memory_space=pltpu.V...  20.7 us
    ppermute x9, starting transfers between devices, shift(): return lax.ppermute(value, ALL, pairs)  12.5 us
    ppermute x9, waiting for transfers between devices, shift(): return lax.ppermute(value, ALL, pairs)  11.8 us
    unnamed x24, local copies, waits for them, and re-layouts  6.78 us
    all_to_all x1, waiting for transfers between devices, local(): lax.all_to_all(sent0, PLANE, 0, 0, tiled=True).reshape(PEERS * ROWS, OWN)  5 us
    all_to_all x1, starting transfers between devices, local(): lax.all_to_all(sent0, PLANE, 0, 0, tiled=True).reshape(PEERS * ROWS, OWN)  3.92 us
  transfers between devices with their start and end apart: 10, of which 5 were waited for; matrix products, arithmetic and copies ran while one was open for 0% of the time, Pallas kernels for 8%

commit v1 on v0

--- a/solution.py
+++ b/solution.py
@@ -22,6 +22,7 @@
 PACK = 400
 HALF = EMBED // 2
 FAR = SAMPLES - OWN
+ORDER = (0, 2, 1, 3)
 F32 = jnp.float32
 BF16 = jnp.bfloat16
 
@@ -70,54 +71,48 @@
 IN_HBM = pl.BlockSpec(memory_space=pltpu.HBM)
 
 
-def strips(place_ref, counts_ref, held, sems, blocks):
+def pack_counts(place, counts_t, slab):
     strip = NK * OWN
 
-    def copy(y, n, i):
-        start = pl.multiple_of(lax.rem(place_ref[0] + i, NZ) * (NY * strip) + y * strip, strip)
-        return pltpu.make_async_copy(counts_ref.at[:, pl.ds(start, strip)], held.at[y, n], sems.at[y, n])
-
-    return [(y, n, copy(y, n, i)) for y in range(NY) for n, i in enumerate(blocks)]
-
-
-def strip_scratch(blocks):
-    return [pltpu.VMEM((NY, blocks, ROWS, NK * OWN), jnp.int32), pltpu.SemaphoreType.DMA((NY, blocks))]
-
-
-def unpack(strip_list, held, out):
-    for y, n, copy in strip_list:
-        copy.wait()
-        for k in range(NK):
-            out[y * NK + k, :, n * OWN : (n + 1) * OWN] = (
-                held[y, n, :, k * OWN : (k + 1) * OWN].astype(F32).astype(BF16)
-            )
-
-
-def pack_counts(place, counts_t, slab):
     def body(place_ref, counts_ref, slab_ref, out, held, slab_s, sems, slab_sem):
+        def copy(y, n):
+            z = lax.rem(place_ref[0] + ORDER[n], NZ)
+            start = pl.multiple_of(z * (NY * strip) + y * strip, strip)
+            return pltpu.make_async_copy(counts_ref.at[:, pl.ds(start, strip)], held.at[y, n], sems.at[y, n])
+
         slab_copy = pltpu.make_async_copy(slab_ref, slab_s, slab_sem)
         slab_copy.start()
-        copies = strips(place_ref, counts_ref, held, sems, range(1, NZ))
-        for _, _, copy in copies:
-            copy.start()
+        for y in range(NY):
+            for n in range(NZ):
+                copy(y, n).start()
         slab_copy.wait()
         for k in range(PEERS):
             half = k % NC
-            out[k, :, FAR:] = slab_s[:, half * HALF : (half + 1) * HALF]
-        unpack(copies, held, out)
-
-    held, sems = strip_scratch(NZ - 1)
-    return call(
-        body,
-        [pltpu.VMEM((PEERS, ROWS, FAR + HALF), BF16)],
+            out[k, :, SAMPLES:] = slab_s[:, half * HALF : (half + 1) * HALF]
+        for y in range(NY):
+            for n in range(NZ):
+                copy(y, n).wait()
+                for k in range(NK):
+                    out[y * NK + k, :, n * OWN : (n + 1) * OWN] = (
+                        held[y, n, :, k * OWN : (k + 1) * OWN].astype(F32).astype(BF16)
+                    )
+
+    return call(
+        body,
+        [pltpu.VMEM((PEERS, ROWS, SAMPLES + HALF), BF16)],
         (place, far(counts_t), far(slab)),
         [IN_SMEM, IN_HBM, IN_HBM],
-        [held, pltpu.VMEM((ROWS, EMBED), BF16), sems, pltpu.SemaphoreType.DMA],
+        [
+            pltpu.VMEM((NY, NZ, ROWS, strip), jnp.int32),
+            pltpu.VMEM((ROWS, EMBED), BF16),
+            pltpu.SemaphoreType.DMA((NY, NZ)),
+            pltpu.SemaphoreType.DMA,
+        ],
     )[0]
 
 
 def prepare(place, down, up, w, bias):
-    def body(place_ref, down_ref, up_ref, w_ref, bias_ref, rows_out, cols_out, own_out, up_out, down_s, up_s, w_s, bias_s, sems):
+    def body(place_ref, down_ref, up_ref, w_ref, bias_ref, rows_out, own_out, up_out, down_s, up_s, w_s, bias_s, sems):
         start = pl.multiple_of(place_ref[0] * COLS, COLS)
         copies = [
             pltpu.make_async_copy(down_ref.at[pl.ds(start, COLS), :], down_s, sems.at[0]),
@@ -137,8 +132,6 @@
         high = v.astype(BF16).astype(F32)
         at = lax.broadcasted_iota(jnp.int32, (EXT, COLS), 0)
         rows_out[2 * RANK :, :] = jnp.where(at < 2, high, jnp.where(at == 2, v - high, 0.0)).astype(BF16)
-        cols_out[:, 0:RANK] = down_s[...]
-        cols_out[:, RANK:] = scaled_up.T
         k = place_ref[2] * NC + place_ref[3]
         strip = pl.multiple_of((place_ref[1] * 2 + lax.div(k, 4)) * 128, 128)
         offset = lax.rem(k, 4) * 32
@@ -155,7 +148,6 @@
         body,
         [
             pltpu.VMEM((2 * RANK + EXT, COLS), BF16),
-            pltpu.VMEM((COLS, 2 * RANK), BF16),
             pltpu.VMEM((32, 128), F32),
             pltpu.VMEM((32, RANK), F32),
         ],
@@ -180,43 +172,34 @@
     return jnp.where(at == 0, high, jnp.where(at == 1, sums - high, 0.0)).astype(BF16)
 
 
-def forward_far(place, arrived, other, rows, counts_t):
-    def body(place_ref, in_ref, other_ref, rows_ref, counts_ref, pooled_ref, slab_out, sent, c1, c2, c3, held, sems):
-        copies = strips(place_ref, counts_ref, held, sems, range(1))
-        for _, _, copy in copies:
-            copy.start()
+def forward_far(place, arrived, other, rows):
+    def body(place_ref, in_ref, other_ref, rows_ref, pooled_ref, slab_out, *outs):
         low_core = place_ref[3] == 0
         for y in range(NY):
             at = slice(y * 512, (y + 1) * 512)
-            own, partner = in_ref[at, FAR:].T, other_ref[at, :].T
+            own, partner = in_ref[at, SAMPLES:].T, other_ref[at, :].T
             slab = jnp.concatenate(
                 [jnp.where(low_core, own, partner), jnp.where(low_core, partner, own)], axis=0
             )
             table = slice(y * EMBED, (y + 1) * EMBED)
             slab_out[table, :] = slab
-            pooled_ref[table, :] = dot(slab, in_ref[at, :FAR], 1, 0).astype(BF16)
+            pooled_ref[table, :] = dot(slab, in_ref[at, OWN:SAMPLES], 1, 0).astype(BF16)
         pooled = pooled_ref[...]
         for part in range(4):
             at = slice(part * 256, (part + 1) * 256)
             product = dot(rows_ref[at, :], pooled, 1, 0).astype(BF16)
-            for i, out in enumerate((c1, c2, c3)):
+            for i, out in enumerate(outs):
                 out[at, :] = product[:, i * OWN : (i + 1) * OWN]
         ext = head_of(rows_ref, pooled)
-        for i, out in enumerate((c1, c2, c3)):
+        for i, out in enumerate(outs):
             out[2 * RANK :, :] = ext[:, i * OWN : (i + 1) * OWN]
-        unpack(copies, held, sent)
-
-    return call(
-        body,
-        [
-            pltpu.VMEM((COLS, FAR), BF16),
-            pltpu.VMEM((COLS, 512), BF16),
-            pltpu.VMEM((PEERS, ROWS, OWN), BF16),
-        ]
+
+    return call(
+        body,
+        [pltpu.VMEM((COLS, FAR), BF16), pltpu.VMEM((COLS, 512), BF16)]
         + [pltpu.VMEM((2 * RANK + EXT, OWN), BF16)] * (NZ - 1),
-        (place, near(arrived), near(other), near(rows), far(counts_t)),
-        [IN_SMEM] + [IN_VMEM] * 3 + [IN_HBM],
-        strip_scratch(1),
+        (place, near(arrived), near(other), near(rows)),
+        [IN_SMEM] + [IN_VMEM] * 3,
         cost=pl.CostEstimate(flops=3 << 30, bytes_accessed=4 << 20, transcendentals=0),
     )
 
@@ -225,7 +208,8 @@
     def body(in_ref, slab_ref, rows_ref, pooled_ref, out):
         for y in range(NY):
             table = slice(y * EMBED, (y + 1) * EMBED)
-            pooled_ref[table, :] = dot(slab_ref[table, :], in_ref[y * 512 : (y + 1) * 512, :], 1, 0).astype(BF16)
+            at = slice(y * 512, (y + 1) * 512)
+            pooled_ref[table, :] = dot(slab_ref[table, :], in_ref[at, :OWN], 1, 0).astype(BF16)
         pooled = pooled_ref[...]
         out[0 : 2 * RANK, :] = dot(rows_ref[0 : 2 * RANK, :], pooled, 1, 0).astype(BF16)
         out[2 * RANK :, :] = head_of(rows_ref, pooled)
@@ -259,36 +243,27 @@
     return call(body, [pltpu.VMEM((2 * RANK + EXT, OWN), BF16)], (*(near(p) for p in parts), labels))[0]
 
 
-def weight_sums(pooled, g, both_of, sums_of):
-    for j in range(4):
-        both_of(j, dot(pooled, g[j * 256 : (j + 1) * 256], 1, 1))
-    sums_of(dot(g[2 * RANK :], pooled, 1, 1))
-
-
-def slab_sums(y, counts, g, rows_ref, cols_ref):
+def by_sample(*blocks):
+    return jnp.concatenate([b[...].T for b in blocks], axis=0)
+
+
+def slab_sums(y, counts, g, rows_ref):
     table = slice(y * EMBED, (y + 1) * EMBED)
-    grad_pooled = (
-        dot(cols_ref[table, :], g[: 2 * RANK], 1, 0) + dot(rows_ref[2 * RANK :, table], g[2 * RANK :], 0, 0)
-    ).astype(BF16)
-    return dot(counts, grad_pooled, 1, 1)
-
-
-def backward_first(block0, block3, pooled0, pooled_far, arrived0, arrived, rows, cols):
-    def body(b0, b3, pooled0_ref, pooled_ref, in0_ref, in_ref, rows_ref, cols_ref, both_out, sums_out, slab_out):
-        g = jnp.concatenate([b0[...], b3[...]], axis=1)
-        pooled = jnp.concatenate([pooled0_ref[...], pooled_ref[:, 2 * OWN :]], axis=1)
-
-        def both_of(j, value):
-            both_out[:, j * 256 : (j + 1) * 256] = value
-
-        def sums_of(value):
-            sums_out[...] = value
-
-        weight_sums(pooled, g, both_of, sums_of)
+    return dot(counts, dot(g, rows_ref[:, table], 1, 0).astype(BF16), 1, 0)
+
+
+def backward_first(block0, block2, pooled_own, pooled_far, arrived, rows):
+    def body(b0, b2, own_ref, far_ref, in_ref, rows_ref, both_out, sums_out, slab_out):
+        g = by_sample(b0, b2)
+        pooled = jnp.concatenate([own_ref[...], far_ref[:, :OWN]], axis=1)
+        for j in range(4):
+            at = slice(j * 256, (j + 1) * 256)
+            both_out[:, at] = dot(pooled, g[:, at], 1, 0)
+        ext = jnp.concatenate([b0[2 * RANK :, :], b2[2 * RANK :, :]], axis=1)
+        sums_out[...] = dot(ext, pooled, 1, 1)
         for y in range(NY):
             at = slice(y * 512, (y + 1) * 512)
-            counts = jnp.concatenate([in0_ref[at, :], in_ref[at, 2 * OWN : FAR]], axis=1)
-            slab_out[at, :] = slab_sums(y, counts, g, rows_ref, cols_ref)
+            slab_out[at, :] = slab_sums(y, in_ref[at, : 2 * OWN], g, rows_ref)
 
     return call(
         body,
@@ -297,7 +272,7 @@
             pltpu.VMEM((EXT, COLS), F32),
             pltpu.VMEM((PEERS * ROWS, EMBED), F32),
         ],
-        tuple(near(v) for v in (block0, block3, pooled0, pooled_far, arrived0, arrived, rows, cols)),
+        tuple(near(v) for v in (block0, block2, pooled_own, pooled_far, arrived, rows)),
         cost=pl.CostEstimate(flops=2 << 30, bytes_accessed=6 << 20, transcendentals=0),
     )
 
@@ -312,44 +287,43 @@
 EVERYONE = slice(0, NY * NX)
 
 
-def backward_weights(place, block1, block2, pooled_far, both, sums):
-    def body(place_ref, b1, b2, pooled_ref, both_ref, sums_ref, mine, other):
+def backward_weights(place, block1, block3, pooled_far, both, sums):
+    def body(place_ref, b1, b3, pooled_ref, both_ref, sums_ref, mine, other, g_out):
         low_core = place_ref[3] == 0
-        g = jnp.concatenate([b1[...], b2[...]], axis=1)
-
-        def both_of(j, value):
+        g = by_sample(b1, b3)
+        g_out[...] = g
+        pooled = pooled_ref[:, OWN:]
+        for j in range(4):
+            value = dot(pooled, g[:, j * 256 : (j + 1) * 256], 1, 0)
             for h in range(2):
                 at = (2 * j + h) * 128
                 held = both_ref[:, at : at + 128] + value[:, h * 128 : (h + 1) * 128]
                 to = slice((2 * j + h) * 32, (2 * j + h + 1) * 32)
                 put(low_core, mine, other, EVERYONE, to, held.reshape(PEERS, 32, 128))
-
-        def sums_of(value):
-            held = (value + sums_ref[...]).astype(BF16)
-            for strip in range(8):
-                row = held[:, strip * 128 : (strip + 1) * 128]
-                for i in range(2):
-                    mine[strip * 2 + i, 256:, :] = row
-                    other[strip * 2 + i, 256:, :] = row
-
-        weight_sums(pooled_ref[:, : 2 * OWN], g, both_of, sums_of)
-
-    return call(
-        body,
-        [pltpu.VMEM((NY * NX, 272, 128), BF16)] * 2,
-        (place, *(near(v) for v in (block1, block2, pooled_far, both, sums))),
+        ext = jnp.concatenate([b1[2 * RANK :, :], b3[2 * RANK :, :]], axis=1)
+        held = (dot(ext, pooled, 1, 1) + sums_ref[...]).astype(BF16)
+        for strip in range(8):
+            row = held[:, strip * 128 : (strip + 1) * 128]
+            for i in range(2):
+                mine[strip * 2 + i, 256:, :] = row
+                other[strip * 2 + i, 256:, :] = row
+
+    return call(
+        body,
+        [pltpu.VMEM((NY * NX, 272, 128), BF16)] * 2 + [pltpu.VMEM((2 * OWN, 2 * RANK + EXT), BF16)],
+        (place, *(near(v) for v in (block1, block3, pooled_far, both, sums))),
         [IN_SMEM] + [IN_VMEM] * 5,
         cost=pl.CostEstimate(flops=1 << 30, bytes_accessed=4 << 20, transcendentals=0),
     )
 
 
-def backward_slab(place, block1, block2, arrived, rows, cols, slab_first):
-    def body(place_ref, b1, b2, in_ref, rows_ref, cols_ref, first_ref, mine, other):
+def backward_slab(place, g, arrived, rows, slab_first):
+    def body(place_ref, g_ref, in_ref, rows_ref, first_ref, mine, other):
         low_core = place_ref[3] == 0
-        g = jnp.concatenate([b1[...], b2[...]], axis=1)
+        g = g_ref[...]
         for y in range(NY):
             at = slice(y * 512, (y + 1) * 512)
-            slab = first_ref[at, :] + slab_sums(y, in_ref[at, : 2 * OWN], g, rows_ref, cols_ref)
+            slab = first_ref[at, :] + slab_sums(y, in_ref[at, 2 * OWN : SAMPLES], g, rows_ref)
             for j in range(2):
                 put(
                     low_core,
@@ -363,8 +337,8 @@
     return call(
         body,
         [pltpu.VMEM((NY * NX, 2 * ROWS, 128), BF16)] * 2,
-        (place, *(near(v) for v in (block1, block2, arrived, rows, cols, slab_first))),
-        [IN_SMEM] + [IN_VMEM] * 6,
+        (place, *(near(v) for v in (g, arrived, rows, slab_first))),
+        [IN_SMEM] + [IN_VMEM] * 4,
         cost=pl.CostEstimate(flops=1 << 30, bytes_accessed=4 << 20, transcendentals=0),
     )
 
@@ -421,25 +395,26 @@
 
 def local(slab, counts, cross_down, cross_up, cross_bias, out_weight, labels):
     place = jnp.stack([lax.axis_index(a) for a in ALL]).astype(jnp.int32)
-    counts_t = counts.T
-    rows, cols, own, up_own = prepare(
+    rows, own, up_own = prepare(
         place, cross_down, cross_up, out_weight.reshape(1, -1), cross_bias.reshape(1, -1)
     )
-    sent = pack_counts(place, counts_t, slab)
-    arrived = lax.all_to_all(sent, PLANE, 0, 0, tiled=True).reshape(PEERS * ROWS, FAR + HALF)
-    other = shift(arrived[:, FAR:], dc=1)
-    pooled, slab_t, sent0, *chunks = forward_far(place, arrived, other, rows, counts_t)
+    sent = pack_counts(place, counts.T, slab)
+    arrived = lax.all_to_all(sent, PLANE, 0, 0, tiled=True).reshape(PEERS * ROWS, SAMPLES + HALF)
+    other = shift(arrived[:, SAMPLES:], dc=1)
+    pooled, slab_t, *chunks = forward_far(place, arrived, other, rows)
     parts = []
-    for i in range(1, NZ):
-        parts.append(shift(chunks[i - 1], dz=i))
-    arrived0 = lax.all_to_all(sent0, PLANE, 0, 0, tiled=True).reshape(PEERS * ROWS, OWN)
-    pooled0, chunk0 = forward_own(arrived0, slab_t, rows)
-    block0 = own_samples([chunk0] + parts, labels.reshape(1, OWN))
-    block1, block2, block3 = (shift(block0, dz=-i) for i in range(1, NZ))
-    both, sums, slab_first = backward_first(block0, block3, pooled0, pooled, arrived0, arrived, rows, cols)
-    weights, given = backward_weights(place, block1, block2, pooled, both, sums)
+    for i, chunk in zip(ORDER[1:], chunks):
+        parts.append(shift(chunk, dz=i))
+    pooled_own, chunk = forward_own(arrived, slab_t, rows)
+    block0 = own_samples([chunk] + parts, labels.reshape(1, OWN))
+    blocks = []
+    for i in ORDER[1:]:
+        blocks.append(shift(block0, dz=-i))
+    block2, block1, block3 = blocks
+    both, sums, slab_first = backward_first(block0, block2, pooled_own, pooled, arrived, rows)
+    weights, given, g = backward_weights(place, block1, block3, pooled, both, sums)
     weights_partner = shift(given, dc=1)
-    slabs, given = backward_slab(place, block1, block2, arrived, rows, cols, slab_first)
+    slabs, given = backward_slab(place, g, arrived, rows, slab_first)
     paired = pair_sums(slabs, shift(given, dc=1), weights, weights_partner)
     shares = lax.all_to_all(paired, ("y", "x"), 0, 0, tiled=True)
     grad_slab, grad_down, grad_up, grad_bias, grad_out = finish(shares, own, up_own)

time: 129 us -> 120 us (0.930)
  local copies, waits for them, and re-layouts: 6.84 us -> 0.04 us
  starting transfers between devices: 16.4 us -> 13.5 us
  blocking collectives: 66.5 us -> 68.5 us
  Pallas kernels: 20.7 us -> 19 us
    unnamed x24 -> x2, local copies, waits for them, and re-layouts: 6.78 us -> 0.01 us
    ppermute x9, waiting for transfers between devices: 11.8 us -> 17.7 us  [shift(): return lax.ppermute(value, ALL, pairs)]
    all_to_all x1, blocking collectives: 35.7 us -> 41.3 us  [local(): lax.all_to_all(sent, PLANE, 0, 0, tiled=True)]
    all_to_all x1 -> x0, waiting for transfers between devices: 5 us -> none  [local(): lax.all_to_all(sent0, PLANE, 0, 0, tiled=True).reshape(PEERS * ROWS, OWN)]
    all_to_all x1 -> x0, starting transfers between devices: 3.92 us -> none  [local(): lax.all_to_all(sent0, PLANE, 0, 0, tiled=True).reshape(PEERS * ROWS, OWN)]
    all_to_all x1, blocking collectives: 30.9 us -> 27.3 us  [local(): shares = lax.all_to_all(paired, ('y', 'x'), 0, 0, tiled=True)]
    pallas_call x10, Pallas kernels: 20.7 us -> 19 us  [call(): pl.pallas_call(body, in_specs=specs or [pl.BlockSpec(memory_space=pltpu.V...]
  transfers between devices with their start and end apart: 10 -> 9, of which waited for: 5 -> 7; matrix products, arithmetic and copies ran while one was open for 0% -> 0% of each run, Pallas kernels for 8% -> 9%
where the time goes in v1:
time: 120 us
  blocking collectives  68.5 us (57%)
  Pallas kernels  19 us (16%)
  waiting for transfers between devices  17.7 us (15%)
  starting transfers between devices  13.5 us (11%)
    all_to_all x1, blocking collectives, local(): lax.all_to_all(sent, PLANE, 0, 0, tiled=True)  41.3 us
    all_to_all x1, blocking collectives, local(): shares = lax.all_to_all(paired, ('y', 'x'), 0, 0, tiled=True)  27.3 us
    pallas_call x10, Pallas kernels, call(): pl.pallas_call(body, in_specs=specs or [pl.BlockSpec(memory_space=pltpu.V...  19 us
    ppermute x9, waiting for transfers between devices, shift(): return lax.ppermute(value, ALL, pairs)  17.7 us
    ppermute x9, starting transfers between devices, shift(): return lax.ppermute(value, ALL, pairs)  13.5 us
  transfers between devices with their start and end apart: 9, of which 7 were waited for; matrix products, arithmetic and copies ran while one was open for 0% of the time, Pallas kernels for 9%

profile of v1, /device:TPU:0, one launch (start us, length us, event | category | flops | bytes accessed | tf_op | source)
XLA Modules:
  0.0 119.6 jit_solution(1789627529380122458)
XLA Ops:
  0.6 0.1 pad_add_fusion.place_ref
  0.7 3.1 %shard_map.110 = bf16[32,64,640]{2,1,0:T(8,128)(2,1)S(1)} custom-call(s32[4]{0:T(128)S(1)} %pad_add_fusion.place_ref, s32[64,16384]{1,0:T(8,128)} %bitcast.18, bf16[64,256]{1,0:T(8,128)(2,1)} %slab_ref.1), custom_call_target="tpu_custom_call" | custom-call | tf_op jit(solution)/shard_map/pallas_call | solution.py:58
  3.8 41.3 %all_to_all.10 = bf16[32,64,640]{2,1,0:T(8,128)(2,1)S(1)} all-to-all(bf16[32,64,640]{2,1,0:T(8,128)(2,1)S(1)} %shard_map.110), channel_id=1, replica_groups=mesh['z'=4,'y'=4,'x'=4,'c'=2] {'y','x','c'}, dimensions={0} | all-to-all | bytes 5242880 | tf_op jit(solution)/shard_map/all_to_all | solution.py:402
  45.1 0.2 collective-permute-start
  45.3 2.9 %shard_map.111 = (bf16[1040,1024]{1,0:T(8,128)(2,1)S(1)}, f32[32,128]{1,0:T(8,128)S(1)}, f32[32,512]{1,0:T(8,128)S(1)}) custom-call(s32[4]{0:T(128)S(1)} %pad_add_fusion.place_ref, bf16[4096,512]{1,0:T(8,128)(2,1)} %down_ref.1, bf16[512,4096]{1,0:T(8,128)(2,1)} %up_ref.1, f32[1,4096]{1,0:T(1,128)} %bitcast.19, f32[1,4096]{1,0:T(1,128)} %bitcast.20), custom_call_target="tpu_custom_call" | custom-call | flops 1073741824 | bytes 6291456 | tf_op jit(solution)/shard_map/pallas_call | solution.py:58
  48.2 0.0 collective-permute-done.other_ref
  48.3 2.6 %shard_map.112 = (bf16[1024,384]{1,0:T(8,128)(2,1)S(1)}, bf16[1024,512]{1,0:T(8,128)(2,1)S(1)}, bf16[1040,128]{1,0:T(8,128)(2,1)S(1)}, bf16[1040,128]{1,0:T(8,128)(2,1)S(1)}, bf16[1040,128]{1,0:T(8,128)(2,1)S(1)}) custom-call(s32[4]{0:T(128)S(1)} %pad_add_fusion.place_ref, bf16[2048,640]{1,0:T(8,128)(2,1)S(1)} %bitcast.13, ...), custom_call_target="tpu_custom_call" | custom-call | flops 3221225472 | bytes 4194304 | tf_op jit(solution)/shard_map/pallas_call | solution.py:58
  50.8 3.9 %collective-permute-start.1 = (bf16[1040,128]{1,0:T(8,128)(2,1)S(1)}, bf16[1040,128]{1,0:T(8,128)(2,1)S(1)}, u32[]{:S(2)}, u32[]{:S(2)}) collective-permute-start(bf16[1040,128]{1,0:T(8,128)(2,1)S(1)} %get-tuple-element.31), channel_id=1, source_target_pairs={{0,64},{1,65},{2,66},{3,67},{4,68},{5,69},{6,70},{7,71},{8,72},{9,... | collective-permute-start | bytes 798728 | tf_op jit(solution)/shard_map/ppermute | solution.py:46
  54.8 1.0 collective-permute-start.2
  55.8 2.2 %collective-permute-start.3 = (bf16[1040,128]{1,0:T(8,128)(2,1)S(1)}, bf16[1040,128]{1,0:T(8,128)(2,1)S(1)}, u32[]{:S(2)}, u32[]{:S(2)}) collective-permute-start(bf16[1040,128]{1,0:T(8,128)(2,1)S(1)} %get-tuple-element.33), channel_id=1, source_target_pairs={{0,96},{1,97},{2,98},{3,99},{4,100},{5,101},{6,102},{7,103},{8,104... | collective-permute-start | bytes 798728 | tf_op jit(solution)/shard_map/ppermute | solution.py:46
  58.0 0.0 copy-start
  58.0 1.1 shard_map.113
  59.1 3.0 %collective-permute-done.1.p1 = bf16[1040,128]{1,0:T(8,128)(2,1)S(1)} collective-permute-done((bf16[1040,128]{1,0:T(8,128)(2,1)S(1)}, bf16[1040,128]{1,0:T(8,128)(2,1)S(1)}, u32[]{:S(2)}, u32[]{:S(2)}) %collective-permute-start.1) | collective-permute-done | bytes 266272 | tf_op jit(solution)/shard_map/ppermute | solution.py:46
  62.1 5.4 %collective-permute-done.2.p2 = bf16[1040,128]{1,0:T(8,128)(2,1)S(1)} collective-permute-done((bf16[1040,128]{1,0:T(8,128)(2,1)S(1)}, bf16[1040,128]{1,0:T(8,128)(2,1)S(1)}, u32[]{:S(2)}, u32[]{:S(2)}) %collective-permute-start.2) | collective-permute-done | bytes 266272 | tf_op jit(solution)/shard_map/ppermute | solution.py:46
  67.4 0.8 collective-permute-done.3.p3
  68.2 0.0 copy-done
  68.2 0.3 shard_map.114.b0
  68.5 2.1 %collective-permute-start.6 = (bf16[1040,128]{1,0:T(8,128)(2,1)S(1)}, bf16[1040,128]{1,0:T(8,128)(2,1)S(1)}, u32[]{:S(2)}, u32[]{:S(2)}) collective-permute-start(bf16[1040,128]{1,0:T(8,128)(2,1)S(1)} %shard_map.114.b0), channel_id=1, source_target_pairs={{0,64},{1,65},{2,66},{3,67},{4,68},{5,69},{6,70},{7,71},{8,72},{9,... | collective-permute-start | bytes 798728 | tf_op jit(solution)/shard_map/ppermute | solution.py:46
  70.6 1.5 %collective-permute-start.5 = (bf16[1040,128]{1,0:T(8,128)(2,1)S(1)}, bf16[1040,128]{1,0:T(8,128)(2,1)S(1)}, u32[]{:S(2)}, u32[]{:S(2)}) collective-permute-start(bf16[1040,128]{1,0:T(8,128)(2,1)S(1)} %shard_map.114.b0), channel_id=1, source_target_pairs={{0,32},{1,33},{2,34},{3,35},{4,36},{5,37},{6,38},{7,39},{8,40},{9,... | collective-permute-start | bytes 798728 | tf_op jit(solution)/shard_map/ppermute | solution.py:46
  72.1 1.8 %collective-permute-start.4 = (bf16[1040,128]{1,0:T(8,128)(2,1)S(1)}, bf16[1040,128]{1,0:T(8,128)(2,1)S(1)}, u32[]{:S(2)}, u32[]{:S(2)}) collective-permute-start(bf16[1040,128]{1,0:T(8,128)(2,1)S(1)} %shard_map.114.b0), channel_id=1, source_target_pairs={{0,96},{1,97},{2,98},{3,99},{4,100},{5,101},{6,102},{7,103},{8,104... | collective-permute-start | bytes 798728 | tf_op jit(solution)/shard_map/ppermute | solution.py:46
  73.9 5.5 %collective-permute-done.6.b2 = bf16[1040,128]{1,0:T(8,128)(2,1)S(1)} collective-permute-done((bf16[1040,128]{1,0:T(8,128)(2,1)S(1)}, bf16[1040,128]{1,0:T(8,128)(2,1)S(1)}, u32[]{:S(2)}, u32[]{:S(2)}) %collective-permute-start.6) | collective-permute-done | bytes 266272 | tf_op jit(solution)/shard_map/ppermute | solution.py:46
  79.4 3.2 %shard_map.115 = (f32[1024,1024]{1,0:T(8,128)S(1)}, f32[16,1024]{1,0:T(8,128)S(1)}, f32[2048,256]{1,0:T(8,128)S(1)}) custom-call(bf16[1040,128]{1,0:T(8,128)(2,1)S(1)} %shard_map.114.b0, bf16[1040,128]{1,0:T(8,128)(2,1)S(1)} %collective-permute-done.6.b2, bf16[1024,128]{1,0:T(8,128)(2,1)S(1)} %get-tuple-element.35.own_ref, ...), custom_call_target="tpu_custom_call" | custom-call | flops 2147483648 | bytes 6291456 | tf_op jit(solution)/shard_map/pallas_call | solution.py:58
  82.6 1.0 collective-permute-done.5.b3
  83.6 0.5 collective-permute-done.4.b1
  84.1 1.5 %shard_map.116 = (bf16[16,272,128]{2,1,0:T(8,128)(2,1)S(1)}, bf16[16,272,128]{2,1,0:T(8,128)(2,1)S(1)}, bf16[256,1040]{1,0:T(8,128)(2,1)S(1)}) custom-call(s32[4]{0:T(128)S(1)} %pad_add_fusion.place_ref, bf16[1040,128]{1,0:T(8,128)(2,1)S(1)} %collective-permute-done.4.b1, bf16[1040,128]{1,0:T(8,128)(2,1)S(1)} %collective-permute-done.5.b3, ...), custom_call_target="tpu_custom_call" | custom-call | flops 1073741824 | bytes 4194304 | tf_op jit(solution)/shard_map/pallas_call | solution.py:58
  85.6 0.2 collective-permute-start.8
  85.8 3.1 %shard_map.117 = (bf16[16,128,128]{2,1,0:T(8,128)(2,1)S(1)}, bf16[16,128,128]{2,1,0:T(8,128)(2,1)S(1)}) custom-call(s32[4]{0:T(128)S(1)} %pad_add_fusion.place_ref, bf16[256,1040]{1,0:T(8,128)(2,1)S(1)} %get-tuple-element.38.g_ref, bf16[2048,640]{1,0:T(8,128)(2,1)S(1)} %bitcast.16, bf16[1040,1024]{1,0:T(8,128)(2,1)S(1)} %get-tuple-element.28.rows_ref, ...), custom_call_target="tpu_custom_call" | custom-call | flops 1073741824 | bytes 4194304 | tf_op jit(solution)/shard_map/pallas_call | solution.py:58
  88.9 0.6 collective-permute-start.7
  89.5 1.5 %collective-permute-done.7.b = bf16[16,128,128]{2,1,0:T(8,128)(2,1)S(1)} collective-permute-done((bf16[16,128,128]{2,1,0:T(8,128)(2,1)S(1)}, bf16[16,128,128]{2,1,0:T(8,128)(2,1)S(1)}, u32[]{:S(2)}, u32[]{:S(2)}) %collective-permute-start.7) | collective-permute-done | bytes 524320 | tf_op jit(solution)/shard_map/ppermute | solution.py:46
  91.0 0.0 collective-permute-done.8.d
  91.0 0.4 shard_map.118
  91.4 27.3 %all_to_all.11.in_ref = bf16[16,400,128]{2,1,0:T(8,128)(2,1)S(1)} all-to-all(bf16[16,400,128]{2,1,0:T(8,128)(2,1)S(1)} %shard_map.118), channel_id=1, replica_groups=mesh['z'=4,'y'=4,'x'=4,'c'=2] {'y','x'}, dimensions={0} | all-to-all | bytes 3276800 | tf_op jit(solution)/shard_map/all_to_all | solution.py:419
  118.7 0.9 shard_map.119
  (1 shorter events, 0.0 us)
Async XLA Ops:
  45.1 3.1 %collective-permute-start = (bf16[2048,128]{1,0:T(8,128)(2,1)S(1)}, bf16[2048,128]{1,0:T(8,128)(2,1)S(1)}, u32[]{:S(2)}, u32[]{:S(2)}) collective-permute-start(bf16[2048,128]{1,0:T(8,128)(2,1)S(1)} %slice.4), channel_id=1, source_target_pairs={{0,1},{1,0},{2,3},{3,2},{4,5},{5,4},{6,7},{7,6},{8,9},{9,8},{10,11... | collective-permute-start | bytes 1572872 | tf_op jit(solution)/shard_map/ppermute | solution.py:46
  50.8 11.2 %collective-permute-start.1 = (bf16[1040,128]{1,0:T(8,128)(2,1)S(1)}, bf16[1040,128]{1,0:T(8,128)(2,1)S(1)}, u32[]{:S(2)}, u32[]{:S(2)}) collective-permute-start(bf16[1040,128]{1,0:T(8,128)(2,1)S(1)} %get-tuple-element.31), channel_id=1, source_target_pairs={{0,64},{1,65},{2,66},{3,67},{4,68},{5,69},{6,70},{7,71},{8,72},{9,... | collective-permute-start | bytes 798728 | tf_op jit(solution)/shard_map/ppermute | solution.py:46
  54.8 12.7 %collective-permute-start.2 = (bf16[1040,128]{1,0:T(8,128)(2,1)S(1)}, bf16[1040,128]{1,0:T(8,128)(2,1)S(1)}, u32[]{:S(2)}, u32[]{:S(2)}) collective-permute-start(bf16[1040,128]{1,0:T(8,128)(2,1)S(1)} %get-tuple-element.32), channel_id=1, source_target_pairs={{0,32},{1,33},{2,34},{3,35},{4,36},{5,37},{6,38},{7,39},{8,40},{9,... | collective-permute-start | bytes 798728 | tf_op jit(solution)/shard_map/ppermute | solution.py:46
  55.8 12.4 %collective-permute-start.3 = (bf16[1040,128]{1,0:T(8,128)(2,1)S(1)}, bf16[1040,128]{1,0:T(8,128)(2,1)S(1)}, u32[]{:S(2)}, u32[]{:S(2)}) collective-permute-start(bf16[1040,128]{1,0:T(8,128)(2,1)S(1)} %get-tuple-element.33), channel_id=1, source_target_pairs={{0,96},{1,97},{2,98},{3,99},{4,100},{5,101},{6,102},{7,103},{8,104... | collective-permute-start | bytes 798728 | tf_op jit(solution)/shard_map/ppermute | solution.py:46
  58.0 10.2 %copy-start = (s32[128]{0:T(128)S(1)}, s32[128]{0:T(128)}, u32[]{:S(2)}) copy-start(s32[128]{0:T(128)} %param.13) | copy-start | bytes 1540
  68.5 10.9 %collective-permute-start.6 = (bf16[1040,128]{1,0:T(8,128)(2,1)S(1)}, bf16[1040,128]{1,0:T(8,128)(2,1)S(1)}, u32[]{:S(2)}, u32[]{:S(2)}) collective-permute-start(bf16[1040,128]{1,0:T(8,128)(2,1)S(1)} %shard_map.114.b0), channel_id=1, source_target_pairs={{0,64},{1,65},{2,66},{3,67},{4,68},{5,69},{6,70},{7,71},{8,72},{9,... | collective-permute-start | bytes 798728 | tf_op jit(solution)/shard_map/ppermute | solution.py:46
  70.6 13.0 %collective-permute-start.5 = (bf16[1040,128]{1,0:T(8,128)(2,1)S(1)}, bf16[1040,128]{1,0:T(8,128)(2,1)S(1)}, u32[]{:S(2)}, u32[]{:S(2)}) collective-permute-start(bf16[1040,128]{1,0:T(8,128)(2,1)S(1)} %shard_map.114.b0), channel_id=1, source_target_pairs={{0,32},{1,33},{2,34},{3,35},{4,36},{5,37},{6,38},{7,39},{8,40},{9,... | collective-permute-start | bytes 798728 | tf_op jit(solution)/shard_map/ppermute | solution.py:46
  72.1 12.0 %collective-permute-start.4 = (bf16[1040,128]{1,0:T(8,128)(2,1)S(1)}, bf16[1040,128]{1,0:T(8,128)(2,1)S(1)}, u32[]{:S(2)}, u32[]{:S(2)}) collective-permute-start(bf16[1040,128]{1,0:T(8,128)(2,1)S(1)} %shard_map.114.b0), channel_id=1, source_target_pairs={{0,96},{1,97},{2,98},{3,99},{4,100},{5,101},{6,102},{7,103},{8,104... | collective-permute-start | bytes 798728 | tf_op jit(solution)/shard_map/ppermute | solution.py:46
  85.6 5.5 %collective-permute-start.8 = (bf16[16,272,128]{2,1,0:T(8,128)(2,1)S(1)}, bf16[16,272,128]{2,1,0:T(8,128)(2,1)S(1)}, u32[]{:S(2)}, u32[]{:S(2)}) collective-permute-start(bf16[16,272,128]{2,1,0:T(8,128)(2,1)S(1)} %get-tuple-element.43), channel_id=1, source_target_pairs={{0,1},{1,0},{2,3},{3,2},{4,5},{5,4},{6,7},{7,6},{8,9},{9,8},{10,11... | collective-permute-start | bytes 3342344 | tf_op jit(solution)/shard_map/ppermute | solution.py:46
  88.9 2.1 %collective-permute-start.7 = (bf16[16,128,128]{2,1,0:T(8,128)(2,1)S(1)}, bf16[16,128,128]{2,1,0:T(8,128)(2,1)S(1)}, u32[]{:S(2)}, u32[]{:S(2)}) collective-permute-start(bf16[16,128,128]{2,1,0:T(8,128)(2,1)S(1)} %get-tuple-element.41), channel_id=1, source_target_pairs={{0,1},{1,0},{2,3},{3,2},{4,5},{5,4},{6,7},{7,6},{8,9},{9,8},{10,11... | collective-permute-start | bytes 1572872 | tf_op jit(solution)/shard_map/ppermute | solution.py:46

commit v2 on v1

--- a/solution.py
+++ b/solution.py
@@ -21,7 +21,6 @@
 EXT = 16
 PACK = 400
 HALF = EMBED // 2
-FAR = SAMPLES - OWN
 ORDER = (0, 2, 1, 3)
 F32 = jnp.float32
 BF16 = jnp.bfloat16
@@ -112,37 +111,29 @@
 
 
 def prepare(place, down, up, w, bias):
-    def body(place_ref, down_ref, up_ref, w_ref, bias_ref, rows_out, own_out, up_out, down_s, up_s, w_s, bias_s, sems):
+    def body(place_ref, down_ref, up_ref, w_ref, bias_ref, rows_out, own_out, up_out):
         start = pl.multiple_of(place_ref[0] * COLS, COLS)
-        copies = [
-            pltpu.make_async_copy(down_ref.at[pl.ds(start, COLS), :], down_s, sems.at[0]),
-            pltpu.make_async_copy(up_ref.at[:, pl.ds(start, COLS)], up_s, sems.at[1]),
-            pltpu.make_async_copy(w_ref.at[:, pl.ds(start, COLS)], w_s, sems.at[2]),
-            pltpu.make_async_copy(bias_ref.at[:, pl.ds(start, COLS)], bias_s, sems.at[3]),
-        ]
-        for copy in copies:
-            copy.start()
-        for copy in copies:
-            copy.wait()
-        w = w_s[...]
-        scaled_up = (up_s[...].astype(F32) * w).astype(BF16)
-        rows_out[0:RANK, :] = down_s[...].T
-        rows_out[RANK : 2 * RANK, :] = scaled_up
-        v = w * (1.0 + bias_s[...])
+        here = pl.ds(start, COLS)
+        w = w_ref[:, here]
+        for part in range(4):
+            at = slice(part * 128, (part + 1) * 128)
+            rows_out[at, :] = down_ref[here, at].T
+        rows_out[RANK : 2 * RANK, :] = (up_ref[:, here].astype(F32) * w).astype(BF16)
+        v = w * (1.0 + bias_ref[:, here])
         high = v.astype(BF16).astype(F32)
         at = lax.broadcasted_iota(jnp.int32, (EXT, COLS), 0)
         rows_out[2 * RANK :, :] = jnp.where(at < 2, high, jnp.where(at == 2, v - high, 0.0)).astype(BF16)
         k = place_ref[2] * NC + place_ref[3]
-        strip = pl.multiple_of((place_ref[1] * 2 + lax.div(k, 4)) * 128, 128)
+        strip = pl.ds(pl.multiple_of(start + (place_ref[1] * 2 + lax.div(k, 4)) * 128, 128), 128)
         offset = lax.rem(k, 4) * 32
         lane = lax.broadcasted_iota(jnp.int32, (32, 128), 1)
         row = lax.broadcasted_iota(jnp.int32, (32, 128), 0)
         own = lane == row + offset
-        w_own = jnp.sum(jnp.where(own, w_s[:, pl.ds(strip, 128)], 0.0), axis=1, keepdims=True)
-        bias_own = jnp.sum(jnp.where(own, bias_s[:, pl.ds(strip, 128)], 0.0), axis=1, keepdims=True)
+        w_own = jnp.sum(jnp.where(own, w_ref[:, strip], 0.0), axis=1, keepdims=True)
+        bias_own = jnp.sum(jnp.where(own, bias_ref[:, strip], 0.0), axis=1, keepdims=True)
         place_own = (row + offset).astype(F32)
         own_out[...] = jnp.where(lane == 0, w_own, jnp.where(lane == 1, bias_own, place_own))
-        up_out[...] = dot(jnp.where(own, 1.0, 0.0).astype(BF16), up_s[:, pl.ds(strip, 128)], 1, 1)
+        up_out[...] = dot(jnp.where(own, 1.0, 0.0).astype(BF16), up_ref[:, strip], 1, 1)
 
     return call(
         body,
@@ -151,17 +142,25 @@
             pltpu.VMEM((32, 128), F32),
             pltpu.VMEM((32, RANK), F32),
         ],
-        (place, *(far(v) for v in (down, up, w, bias))),
-        [IN_SMEM] + [IN_HBM] * 4,
-        [
-            pltpu.VMEM((COLS, RANK), BF16),
-            pltpu.VMEM((RANK, COLS), BF16),
-            pltpu.VMEM((1, COLS), F32),
-            pltpu.VMEM((1, COLS), F32),
-            pltpu.SemaphoreType.DMA((4,)),
-        ],
-        cost=pl.CostEstimate(flops=1 << 30, bytes_accessed=6 << 20, transcendentals=0),
-    )
+        (place, *(near(v) for v in (down, up, w, bias))),
+        [IN_SMEM] + [IN_VMEM] * 4,
+        cost=pl.CostEstimate(flops=1 << 29, bytes_accessed=6 << 20, transcendentals=0),
+    )
+
+
+def pool_half(arrived):
+    def body(in_ref, pooled_ref):
+        for y in range(NY):
+            at = slice(y * 512, (y + 1) * 512)
+            half = slice(y * HALF, (y + 1) * HALF)
+            pooled_ref[half, :] = dot(in_ref[at, SAMPLES:].T, in_ref[at, :SAMPLES], 1, 0).astype(BF16)
+
+    return call(
+        body,
+        [pltpu.VMEM((NY * HALF, SAMPLES), BF16)],
+        (near(arrived),),
+        cost=pl.CostEstimate(flops=1 << 29, bytes_accessed=2 << 20, transcendentals=0),
+    )[0]
 
 
 def head_of(rows_ref, pooled):
@@ -172,19 +171,18 @@
     return jnp.where(at == 0, high, jnp.where(at == 1, sums - high, 0.0)).astype(BF16)
 
 
-def forward_far(place, arrived, other, rows):
-    def body(place_ref, in_ref, other_ref, rows_ref, pooled_ref, slab_out, *outs):
-        low_core = place_ref[3] == 0
+def forward_far(place, arrived, other, half, rows):
+    def body(place_ref, in_ref, other_ref, half_ref, rows_ref, pooled_ref, *outs):
+        core = place_ref[3]
         for y in range(NY):
             at = slice(y * 512, (y + 1) * 512)
-            own, partner = in_ref[at, SAMPLES:].T, other_ref[at, :].T
-            slab = jnp.concatenate(
-                [jnp.where(low_core, own, partner), jnp.where(low_core, partner, own)], axis=0
-            )
-            table = slice(y * EMBED, (y + 1) * EMBED)
-            slab_out[table, :] = slab
-            pooled_ref[table, :] = dot(slab, in_ref[at, OWN:SAMPLES], 1, 0).astype(BF16)
-        pooled = pooled_ref[...]
+            mine = pl.multiple_of(y * EMBED + core * HALF, HALF)
+            partners = pl.multiple_of(y * EMBED + (1 - core) * HALF, HALF)
+            pooled_ref[pl.ds(mine, HALF), :] = half_ref[y * HALF : (y + 1) * HALF, :]
+            pooled_ref[pl.ds(partners, HALF), :] = dot(
+                other_ref[at, :].T, in_ref[at, :SAMPLES], 1, 0
+            ).astype(BF16)
+        pooled = pooled_ref[:, OWN:]
         for part in range(4):
             at = slice(part * 256, (part + 1) * 256)
             product = dot(rows_ref[at, :], pooled, 1, 0).astype(BF16)
@@ -196,30 +194,25 @@
 
     return call(
         body,
-        [pltpu.VMEM((COLS, FAR), BF16), pltpu.VMEM((COLS, 512), BF16)]
-        + [pltpu.VMEM((2 * RANK + EXT, OWN), BF16)] * (NZ - 1),
-        (place, near(arrived), near(other), near(rows)),
-        [IN_SMEM] + [IN_VMEM] * 3,
+        [pltpu.VMEM((COLS, SAMPLES), BF16)] + [pltpu.VMEM((2 * RANK + EXT, OWN), BF16)] * (NZ - 1),
+        (place, near(arrived), near(other), near(half), near(rows)),
+        [IN_SMEM] + [IN_VMEM] * 4,
         cost=pl.CostEstimate(flops=3 << 30, bytes_accessed=4 << 20, transcendentals=0),
     )
 
 
-def forward_own(arrived, slab, rows):
-    def body(in_ref, slab_ref, rows_ref, pooled_ref, out):
-        for y in range(NY):
-            table = slice(y * EMBED, (y + 1) * EMBED)
-            at = slice(y * 512, (y + 1) * 512)
-            pooled_ref[table, :] = dot(slab_ref[table, :], in_ref[at, :OWN], 1, 0).astype(BF16)
-        pooled = pooled_ref[...]
+def forward_own(pooled, rows):
+    def body(pooled_ref, rows_ref, out):
+        pooled = pooled_ref[:, :OWN]
         out[0 : 2 * RANK, :] = dot(rows_ref[0 : 2 * RANK, :], pooled, 1, 0).astype(BF16)
         out[2 * RANK :, :] = head_of(rows_ref, pooled)
 
     return call(
         body,
-        [pltpu.VMEM((COLS, OWN), BF16), pltpu.VMEM((2 * RANK + EXT, OWN), BF16)],
-        (near(arrived), near(slab), near(rows)),
+        [pltpu.VMEM((2 * RANK + EXT, OWN), BF16)],
+        (near(pooled), near(rows)),
         cost=pl.CostEstimate(flops=1 << 30, bytes_accessed=1 << 20, transcendentals=0),
-    )
+    )[0]
 
 
 def own_samples(parts, labels):
@@ -247,23 +240,24 @@
     return jnp.concatenate([b[...].T for b in blocks], axis=0)
 
 
-def slab_sums(y, counts, g, rows_ref):
-    table = slice(y * EMBED, (y + 1) * EMBED)
-    return dot(counts, dot(g, rows_ref[:, table], 1, 0).astype(BF16), 1, 0)
-
-
-def backward_first(block0, block2, pooled_own, pooled_far, arrived, rows):
-    def body(b0, b2, own_ref, far_ref, in_ref, rows_ref, both_out, sums_out, slab_out):
+def grad_pooled_of(g, rows_ref):
+    tables = [slice(y * EMBED, (y + 1) * EMBED) for y in range(NY)]
+    return [dot(g, rows_ref[:, table], 1, 0).astype(BF16) for table in tables]
+
+
+def backward_first(block0, block2, pooled, arrived, rows):
+    def body(b0, b2, pooled_ref, in_ref, rows_ref, both_out, sums_out, slab_out):
         g = by_sample(b0, b2)
-        pooled = jnp.concatenate([own_ref[...], far_ref[:, :OWN]], axis=1)
+        products = grad_pooled_of(g, rows_ref)
+        pooled = pooled_ref[:, : 2 * OWN]
         for j in range(4):
             at = slice(j * 256, (j + 1) * 256)
             both_out[:, at] = dot(pooled, g[:, at], 1, 0)
         ext = jnp.concatenate([b0[2 * RANK :, :], b2[2 * RANK :, :]], axis=1)
         sums_out[...] = dot(ext, pooled, 1, 1)
-        for y in range(NY):
+        for y, grad_pooled in enumerate(products):
             at = slice(y * 512, (y + 1) * 512)
-            slab_out[at, :] = slab_sums(y, in_ref[at, : 2 * OWN], g, rows_ref)
+            slab_out[at, :] = dot(in_ref[at, : 2 * OWN], grad_pooled, 1, 0)
 
     return call(
         body,
@@ -272,7 +266,7 @@
             pltpu.VMEM((EXT, COLS), F32),
             pltpu.VMEM((PEERS * ROWS, EMBED), F32),
         ],
-        tuple(near(v) for v in (block0, block2, pooled_own, pooled_far, arrived, rows)),
+        tuple(near(v) for v in (block0, block2, pooled, arrived, rows)),
         cost=pl.CostEstimate(flops=2 << 30, bytes_accessed=6 << 20, transcendentals=0),
     )
 
@@ -287,12 +281,12 @@
 EVERYONE = slice(0, NY * NX)
 
 
-def backward_weights(place, block1, block3, pooled_far, both, sums):
+def backward_weights(place, block1, block3, pooled, both, sums):
     def body(place_ref, b1, b3, pooled_ref, both_ref, sums_ref, mine, other, g_out):
         low_core = place_ref[3] == 0
         g = by_sample(b1, b3)
         g_out[...] = g
-        pooled = pooled_ref[:, OWN:]
+        pooled = pooled_ref[:, 2 * OWN :]
         for j in range(4):
             value = dot(pooled, g[:, j * 256 : (j + 1) * 256], 1, 0)
             for h in range(2):
@@ -311,7 +305,7 @@
     return call(
         body,
         [pltpu.VMEM((NY * NX, 272, 128), BF16)] * 2 + [pltpu.VMEM((2 * OWN, 2 * RANK + EXT), BF16)],
-        (place, *(near(v) for v in (block1, block3, pooled_far, both, sums))),
+        (place, *(near(v) for v in (block1, block3, pooled, both, sums))),
         [IN_SMEM] + [IN_VMEM] * 5,
         cost=pl.CostEstimate(flops=1 << 30, bytes_accessed=4 << 20, transcendentals=0),
     )
@@ -320,10 +314,9 @@
 def backward_slab(place, g, arrived, rows, slab_first):
     def body(place_ref, g_ref, in_ref, rows_ref, first_ref, mine, other):
         low_core = place_ref[3] == 0
-        g = g_ref[...]
-        for y in range(NY):
+        for y, grad_pooled in enumerate(grad_pooled_of(g_ref[...], rows_ref)):
             at = slice(y * 512, (y + 1) * 512)
-            slab = first_ref[at, :] + slab_sums(y, in_ref[at, 2 * OWN : SAMPLES], g, rows_ref)
+            slab = first_ref[at, :] + dot(in_ref[at, 2 * OWN : SAMPLES], grad_pooled, 1, 0)
             for j in range(2):
                 put(
                     low_core,
@@ -401,17 +394,18 @@
     sent = pack_counts(place, counts.T, slab)
     arrived = lax.all_to_all(sent, PLANE, 0, 0, tiled=True).reshape(PEERS * ROWS, SAMPLES + HALF)
     other = shift(arrived[:, SAMPLES:], dc=1)
-    pooled, slab_t, *chunks = forward_far(place, arrived, other, rows)
+    half = pool_half(arrived)
+    pooled, *chunks = forward_far(place, arrived, other, half, rows)
     parts = []
     for i, chunk in zip(ORDER[1:], chunks):
         parts.append(shift(chunk, dz=i))
-    pooled_own, chunk = forward_own(arrived, slab_t, rows)
+    chunk = forward_own(pooled, rows)
     block0 = own_samples([chunk] + parts, labels.reshape(1, OWN))
     blocks = []
     for i in ORDER[1:]:
         blocks.append(shift(block0, dz=-i))
     block2, block1, block3 = blocks
-    both, sums, slab_first = backward_first(block0, block2, pooled_own, pooled, arrived, rows)
+    both, sums, slab_first = backward_first(block0, block2, pooled, arrived, rows)
     weights, given, g = backward_weights(place, block1, block3, pooled, both, sums)
     weights_partner = shift(given, dc=1)
     slabs, given = backward_slab(place, g, arrived, rows, slab_first)

time: 120 us -> 117 us (0.975)
  Pallas kernels: 19 us -> 14.7 us
  waiting for transfers between devices: 17.7 us -> 19.4 us
    pallas_call x10 -> x11, Pallas kernels: 19 us -> 14.7 us  [call(): pl.pallas_call(body, in_specs=specs or [pl.BlockSpec(memory_space=pltpu.V...]
    ppermute x9, waiting for transfers between devices: 17.7 us -> 19.4 us  [shift(): return lax.ppermute(value, ALL, pairs)]
  transfers between devices with their start and end apart: 9 -> 9, of which waited for: 7 -> 7; matrix products, arithmetic and copies ran while one was open for 0% -> 0% of each run, Pallas kernels for 9% -> 5%
where the time goes in v2:
time: 117 us
  blocking collectives  68.9 us (59%)
  waiting for transfers between devices  19.4 us (17%)
  Pallas kernels  14.7 us (13%)
  starting transfers between devices  13.4 us (11%)
    all_to_all x1, blocking collectives, local(): lax.all_to_all(sent, PLANE, 0, 0, tiled=True)  41.6 us
    all_to_all x1, blocking collectives, local(): shares = lax.all_to_all(paired, ('y', 'x'), 0, 0, tiled=True)  27.3 us
    ppermute x9, waiting for transfers between devices, shift(): return lax.ppermute(value, ALL, pairs)  19.4 us
    pallas_call x11, Pallas kernels, call(): pl.pallas_call(body, in_specs=specs or [pl.BlockSpec(memory_space=pltpu.V...  14.7 us
    ppermute x9, starting transfers between devices, shift(): return lax.ppermute(value, ALL, pairs)  13.4 us
  transfers between devices with their start and end apart: 9, of which 7 were waited for; matrix products, arithmetic and copies ran while one was open for 0% of the time, Pallas kernels for 5%

profile of v2, /device:TPU:0, one launch (start us, length us, event | category | flops | bytes accessed | tf_op | source)
XLA Modules:
  0.0 117.3 jit_solution(205110502277038620)
XLA Ops:
  0.6 0.1 pad_add_fusion.place_ref
  0.7 0.0 copy-start.1
  0.7 3.3 %shard_map.110 = bf16[32,64,640]{2,1,0:T(8,128)(2,1)S(1)} custom-call(s32[4]{0:T(128)S(1)} %pad_add_fusion.place_ref, s32[64,16384]{1,0:T(8,128)} %bitcast.20, bf16[64,256]{1,0:T(8,128)(2,1)} %slab_ref.1), custom_call_target="tpu_custom_call" | custom-call | tf_op jit(solution)/shard_map/pallas_call | solution.py:57
  4.0 0.0 copy-start
  4.1 0.0 copy-start.2
  4.1 0.0 copy-start.3
  4.1 41.6 %all_to_all.10 = bf16[32,64,640]{2,1,0:T(8,128)(2,1)S(1)} all-to-all(bf16[32,64,640]{2,1,0:T(8,128)(2,1)S(1)} %shard_map.110), channel_id=1, replica_groups=mesh['z'=4,'y'=4,'x'=4,'c'=2] {'y','x','c'}, dimensions={0} | all-to-all | bytes 5242880 | tf_op jit(solution)/shard_map/all_to_all | solution.py:395
  45.7 0.2 collective-permute-start
  45.9 0.0 copy-done.1
  45.9 0.0 copy-done
  45.9 0.0 copy-done.2
  45.9 0.0 copy-done.3
  45.9 1.3 %shard_map.112 = (bf16[1040,1024]{1,0:T(8,128)(2,1)S(1)}, f32[32,128]{1,0:T(8,128)S(1)}, f32[32,512]{1,0:T(8,128)S(1)}) custom-call(s32[4]{0:T(128)S(1)} %pad_add_fusion.place_ref, bf16[4096,512]{1,0:T(8,128)(2,1)S(1)} %copy-done, bf16[512,4096]{1,0:T(8,128)(2,1)S(1)} %copy-done.1, f32[1,4096]{1,0:T(1,128)S(1)} %bitcast.17, f32[1,4096]{1,0:T(1,128)S(1)} %bitcast.18), custom_call_target="tpu_custom_call" | custom-call | flops 536870912 | bytes 6291456 | tf_op jit(solution)/shard_map/pallas_call | solution.py:57
  47.2 0.5 shard_map.111.half_ref
  47.7 0.0 collective-permute-done.other_ref
  47.7 2.4 %shard_map.113 = (bf16[1024,512]{1,0:T(8,128)(2,1)S(1)}, bf16[1040,128]{1,0:T(8,128)(2,1)S(1)}, bf16[1040,128]{1,0:T(8,128)(2,1)S(1)}, bf16[1040,128]{1,0:T(8,128)(2,1)S(1)}) custom-call(s32[4]{0:T(128)S(1)} %pad_add_fusion.place_ref, bf16[2048,640]{1,0:T(8,128)(2,1)S(1)} %bitcast.14, bf16[2048,128]{1,0:T(8,128)(2,1)S(1)} %collective-permute-done.other_ref, ...), custom_call_target="tpu_custom_call" | custom-call | flops 3221225472 | bytes 4194304 | tf_op jit(solution)/shard_map/pallas_call | solution.py:57
  50.0 0.0 copy-start.4
  50.1 4.0 %collective-permute-start.1 = (bf16[1040,128]{1,0:T(8,128)(2,1)S(1)}, bf16[1040,128]{1,0:T(8,128)(2,1)S(1)}, u32[]{:S(2)}, u32[]{:S(2)}) collective-permute-start(bf16[1040,128]{1,0:T(8,128)(2,1)S(1)} %get-tuple-element.27), channel_id=1, source_target_pairs={{0,64},{1,65},{2,66},{3,67},{4,68},{5,69},{6,70},{7,71},{8,72},{9,... | collective-permute-start | bytes 798728 | tf_op jit(solution)/shard_map/ppermute | solution.py:45
  54.0 1.0 collective-permute-start.2
  55.0 2.2 %collective-permute-start.3 = (bf16[1040,128]{1,0:T(8,128)(2,1)S(1)}, bf16[1040,128]{1,0:T(8,128)(2,1)S(1)}, u32[]{:S(2)}, u32[]{:S(2)}) collective-permute-start(bf16[1040,128]{1,0:T(8,128)(2,1)S(1)} %get-tuple-element.29), channel_id=1, source_target_pairs={{0,96},{1,97},{2,98},{3,99},{4,100},{5,101},{6,102},{7,103},{8,104... | collective-permute-start | bytes 798728 | tf_op jit(solution)/shard_map/ppermute | solution.py:45
  57.2 0.7 shard_map.114.p0
  58.0 3.3 %collective-permute-done.1.p1 = bf16[1040,128]{1,0:T(8,128)(2,1)S(1)} collective-permute-done((bf16[1040,128]{1,0:T(8,128)(2,1)S(1)}, bf16[1040,128]{1,0:T(8,128)(2,1)S(1)}, u32[]{:S(2)}, u32[]{:S(2)}) %collective-permute-start.1) | collective-permute-done | bytes 266272 | tf_op jit(solution)/shard_map/ppermute | solution.py:45
  61.3 5.4 %collective-permute-done.2.p2 = bf16[1040,128]{1,0:T(8,128)(2,1)S(1)} collective-permute-done((bf16[1040,128]{1,0:T(8,128)(2,1)S(1)}, bf16[1040,128]{1,0:T(8,128)(2,1)S(1)}, u32[]{:S(2)}, u32[]{:S(2)}) %collective-permute-start.2) | collective-permute-done | bytes 266272 | tf_op jit(solution)/shard_map/ppermute | solution.py:45
  66.7 0.8 collective-permute-done.3.p3
  67.4 0.0 copy-done.4
  67.4 0.3 shard_map.115.b0
  67.7 2.1 %collective-permute-start.6 = (bf16[1040,128]{1,0:T(8,128)(2,1)S(1)}, bf16[1040,128]{1,0:T(8,128)(2,1)S(1)}, u32[]{:S(2)}, u32[]{:S(2)}) collective-permute-start(bf16[1040,128]{1,0:T(8,128)(2,1)S(1)} %shard_map.115.b0), channel_id=1, source_target_pairs={{0,64},{1,65},{2,66},{3,67},{4,68},{5,69},{6,70},{7,71},{8,72},{9,... | collective-permute-start | bytes 798728 | tf_op jit(solution)/shard_map/ppermute | solution.py:45
  69.8 1.5 %collective-permute-start.5 = (bf16[1040,128]{1,0:T(8,128)(2,1)S(1)}, bf16[1040,128]{1,0:T(8,128)(2,1)S(1)}, u32[]{:S(2)}, u32[]{:S(2)}) collective-permute-start(bf16[1040,128]{1,0:T(8,128)(2,1)S(1)} %shard_map.115.b0), channel_id=1, source_target_pairs={{0,32},{1,33},{2,34},{3,35},{4,36},{5,37},{6,38},{7,39},{8,40},{9,... | collective-permute-start | bytes 798728 | tf_op jit(solution)/shard_map/ppermute | solution.py:45
  71.3 1.8 %collective-permute-start.4 = (bf16[1040,128]{1,0:T(8,128)(2,1)S(1)}, bf16[1040,128]{1,0:T(8,128)(2,1)S(1)}, u32[]{:S(2)}, u32[]{:S(2)}) collective-permute-start(bf16[1040,128]{1,0:T(8,128)(2,1)S(1)} %shard_map.115.b0), channel_id=1, source_target_pairs={{0,96},{1,97},{2,98},{3,99},{4,100},{5,101},{6,102},{7,103},{8,104... | collective-permute-start | bytes 798728 | tf_op jit(solution)/shard_map/ppermute | solution.py:45
  73.1 5.5 %collective-permute-done.6.b2 = bf16[1040,128]{1,0:T(8,128)(2,1)S(1)} collective-permute-done((bf16[1040,128]{1,0:T(8,128)(2,1)S(1)}, bf16[1040,128]{1,0:T(8,128)(2,1)S(1)}, u32[]{:S(2)}, u32[]{:S(2)}) %collective-permute-start.6) | collective-permute-done | bytes 266272 | tf_op jit(solution)/shard_map/ppermute | solution.py:45
  78.6 1.8 %shard_map.116 = (f32[1024,1024]{1,0:T(8,128)S(1)}, f32[16,1024]{1,0:T(8,128)S(1)}, f32[2048,256]{1,0:T(8,128)S(1)}) custom-call(bf16[1040,128]{1,0:T(8,128)(2,1)S(1)} %shard_map.115.b0, bf16[1040,128]{1,0:T(8,128)(2,1)S(1)} %collective-permute-done.6.b2, bf16[1024,512]{1,0:T(8,128)(2,1)S(1)} %get-tuple-element.26.pooled_ref, ...), custom_call_target="tpu_custom_call" | custom-call | flops 2147483648 | bytes 6291456 | tf_op jit(solution)/shard_map/pallas_call | solution.py:57
  80.4 2.4 %collective-permute-done.5.b3 = bf16[1040,128]{1,0:T(8,128)(2,1)S(1)} collective-permute-done((bf16[1040,128]{1,0:T(8,128)(2,1)S(1)}, bf16[1040,128]{1,0:T(8,128)(2,1)S(1)}, u32[]{:S(2)}, u32[]{:S(2)}) %collective-permute-start.5) | collective-permute-done | bytes 266272 | tf_op jit(solution)/shard_map/ppermute | solution.py:45
  82.8 0.5 collective-permute-done.4.b1
  83.3 1.4 %shard_map.117 = (bf16[16,272,128]{2,1,0:T(8,128)(2,1)S(1)}, bf16[16,272,128]{2,1,0:T(8,128)(2,1)S(1)}, bf16[256,1040]{1,0:T(8,128)(2,1)S(1)}) custom-call(s32[4]{0:T(128)S(1)} %pad_add_fusion.place_ref, bf16[1040,128]{1,0:T(8,128)(2,1)S(1)} %collective-permute-done.4.b1, bf16[1040,128]{1,0:T(8,128)(2,1)S(1)} %collective-permute-done.5.b3, ...), custom_call_target="tpu_custom_call" | custom-call | flops 1073741824 | bytes 4194304 | tf_op jit(solution)/shard_map/pallas_call | solution.py:57
  84.7 0.1 collective-permute-start.8
  84.8 1.7 %shard_map.118 = (bf16[16,128,128]{2,1,0:T(8,128)(2,1)S(1)}, bf16[16,128,128]{2,1,0:T(8,128)(2,1)S(1)}) custom-call(s32[4]{0:T(128)S(1)} %pad_add_fusion.place_ref, bf16[256,1040]{1,0:T(8,128)(2,1)S(1)} %get-tuple-element.32.g_ref, bf16[2048,640]{1,0:T(8,128)(2,1)S(1)} %bitcast.16, bf16[1040,1024]{1,0:T(8,128)(2,1)S(1)} %get-tuple-element.25.rows_ref, ...), custom_call_target="tpu_custom_call" | custom-call | flops 1073741824 | bytes 4194304 | tf_op jit(solution)/shard_map/pallas_call | solution.py:57
  86.5 0.6 collective-permute-start.7
  87.1 1.5 %collective-permute-done.7.b = bf16[16,128,128]{2,1,0:T(8,128)(2,1)S(1)} collective-permute-done((bf16[16,128,128]{2,1,0:T(8,128)(2,1)S(1)}, bf16[16,128,128]{2,1,0:T(8,128)(2,1)S(1)}, u32[]{:S(2)}, u32[]{:S(2)}) %collective-permute-start.7) | collective-permute-done | bytes 524320 | tf_op jit(solution)/shard_map/ppermute | solution.py:45
  88.6 0.0 collective-permute-done.8.d
  88.6 0.4 shard_map.119
  89.0 27.3 %all_to_all.11.in_ref = bf16[16,400,128]{2,1,0:T(8,128)(2,1)S(1)} all-to-all(bf16[16,400,128]{2,1,0:T(8,128)(2,1)S(1)} %shard_map.119), channel_id=1, replica_groups=mesh['z'=4,'y'=4,'x'=4,'c'=2] {'y','x'}, dimensions={0} | all-to-all | bytes 3276800 | tf_op jit(solution)/shard_map/all_to_all | solution.py:413
  116.3 0.9 shard_map.120
  (1 shorter events, 0.0 us)
Async XLA Ops:
  0.7 45.2 %copy-start.1 = (bf16[512,4096]{1,0:T(8,128)(2,1)S(1)}, bf16[512,4096]{1,0:T(8,128)(2,1)}, u32[]{:S(2)}) copy-start(bf16[512,4096]{1,0:T(8,128)(2,1)} %up_ref.1) | copy-start | bytes 12582916
  4.0 41.8 %copy-start = (bf16[4096,512]{1,0:T(8,128)(2,1)S(1)}, bf16[4096,512]{1,0:T(8,128)(2,1)}, u32[]{:S(2)}) copy-start(bf16[4096,512]{1,0:T(8,128)(2,1)} %down_ref.1) | copy-start | bytes 12582916
  4.1 41.8 %copy-start.2 = (f32[4096]{0:T(1024)S(1)}, f32[4096]{0:T(1024)}, u32[]{:S(2)}) copy-start(f32[4096]{0:T(1024)} %param.12) | copy-start | bytes 49156
  4.1 41.8 %copy-start.3 = (f32[4096]{0:T(1024)S(1)}, f32[4096]{0:T(1024)}, u32[]{:S(2)}) copy-start(f32[4096]{0:T(1024)} %param.11) | copy-start | bytes 49156
  45.7 2.0 %collective-permute-start = (bf16[2048,128]{1,0:T(8,128)(2,1)S(1)}, bf16[2048,128]{1,0:T(8,128)(2,1)S(1)}, u32[]{:S(2)}, u32[]{:S(2)}) collective-permute-start(bf16[2048,128]{1,0:T(8,128)(2,1)S(1)} %slice.4), channel_id=1, source_target_pairs={{0,1},{1,0},{2,3},{3,2},{4,5},{5,4},{6,7},{7,6},{8,9},{9,8},{10,11... | collective-permute-start | bytes 1572872 | tf_op jit(solution)/shard_map/ppermute | solution.py:45
  50.0 17.4 %copy-start.4 = (s32[128]{0:T(128)S(1)}, s32[128]{0:T(128)}, u32[]{:S(2)}) copy-start(s32[128]{0:T(128)} %param.13) | copy-start | bytes 1540
  50.1 11.2 %collective-permute-start.1 = (bf16[1040,128]{1,0:T(8,128)(2,1)S(1)}, bf16[1040,128]{1,0:T(8,128)(2,1)S(1)}, u32[]{:S(2)}, u32[]{:S(2)}) collective-permute-start(bf16[1040,128]{1,0:T(8,128)(2,1)S(1)} %get-tuple-element.27), channel_id=1, source_target_pairs={{0,64},{1,65},{2,66},{3,67},{4,68},{5,69},{6,70},{7,71},{8,72},{9,... | collective-permute-start | bytes 798728 | tf_op jit(solution)/shard_map/ppermute | solution.py:45
  54.0 12.6 %collective-permute-start.2 = (bf16[1040,128]{1,0:T(8,128)(2,1)S(1)}, bf16[1040,128]{1,0:T(8,128)(2,1)S(1)}, u32[]{:S(2)}, u32[]{:S(2)}) collective-permute-start(bf16[1040,128]{1,0:T(8,128)(2,1)S(1)} %get-tuple-element.28), channel_id=1, source_target_pairs={{0,32},{1,33},{2,34},{3,35},{4,36},{5,37},{6,38},{7,39},{8,40},{9,... | collective-permute-start | bytes 798728 | tf_op jit(solution)/shard_map/ppermute | solution.py:45
  55.0 12.4 %collective-permute-start.3 = (bf16[1040,128]{1,0:T(8,128)(2,1)S(1)}, bf16[1040,128]{1,0:T(8,128)(2,1)S(1)}, u32[]{:S(2)}, u32[]{:S(2)}) collective-permute-start(bf16[1040,128]{1,0:T(8,128)(2,1)S(1)} %get-tuple-element.29), channel_id=1, source_target_pairs={{0,96},{1,97},{2,98},{3,99},{4,100},{5,101},{6,102},{7,103},{8,104... | collective-permute-start | bytes 798728 | tf_op jit(solution)/shard_map/ppermute | solution.py:45
  67.7 10.9 %collective-permute-start.6 = (bf16[1040,128]{1,0:T(8,128)(2,1)S(1)}, bf16[1040,128]{1,0:T(8,128)(2,1)S(1)}, u32[]{:S(2)}, u32[]{:S(2)}) collective-permute-start(bf16[1040,128]{1,0:T(8,128)(2,1)S(1)} %shard_map.115.b0), channel_id=1, source_target_pairs={{0,64},{1,65},{2,66},{3,67},{4,68},{5,69},{6,70},{7,71},{8,72},{9,... | collective-permute-start | bytes 798728 | tf_op jit(solution)/shard_map/ppermute | solution.py:45
  69.8 13.0 %collective-permute-start.5 = (bf16[1040,128]{1,0:T(8,128)(2,1)S(1)}, bf16[1040,128]{1,0:T(8,128)(2,1)S(1)}, u32[]{:S(2)}, u32[]{:S(2)}) collective-permute-start(bf16[1040,128]{1,0:T(8,128)(2,1)S(1)} %shard_map.115.b0), channel_id=1, source_target_pairs={{0,32},{1,33},{2,34},{3,35},{4,36},{5,37},{6,38},{7,39},{8,40},{9,... | collective-permute-start | bytes 798728 | tf_op jit(solution)/shard_map/ppermute | solution.py:45
  71.3 12.0 %collective-permute-start.4 = (bf16[1040,128]{1,0:T(8,128)(2,1)S(1)}, bf16[1040,128]{1,0:T(8,128)(2,1)S(1)}, u32[]{:S(2)}, u32[]{:S(2)}) collective-permute-start(bf16[1040,128]{1,0:T(8,128)(2,1)S(1)} %shard_map.115.b0), channel_id=1, source_target_pairs={{0,96},{1,97},{2,98},{3,99},{4,100},{5,101},{6,102},{7,103},{8,104... | collective-permute-start | bytes 798728 | tf_op jit(solution)/shard_map/ppermute | solution.py:45
  84.7 3.9 %collective-permute-start.8 = (bf16[16,272,128]{2,1,0:T(8,128)(2,1)S(1)}, bf16[16,272,128]{2,1,0:T(8,128)(2,1)S(1)}, u32[]{:S(2)}, u32[]{:S(2)}) collective-permute-start(bf16[16,272,128]{2,1,0:T(8,128)(2,1)S(1)} %get-tuple-element.37), channel_id=1, source_target_pairs={{0,1},{1,0},{2,3},{3,2},{4,5},{5,4},{6,7},{7,6},{8,9},{9,8},{10,11... | collective-permute-start | bytes 3342344 | tf_op jit(solution)/shard_map/ppermute | solution.py:45
  86.5 2.1 %collective-permute-start.7 = (bf16[16,128,128]{2,1,0:T(8,128)(2,1)S(1)}, bf16[16,128,128]{2,1,0:T(8,128)(2,1)S(1)}, u32[]{:S(2)}, u32[]{:S(2)}) collective-permute-start(bf16[16,128,128]{2,1,0:T(8,128)(2,1)S(1)} %get-tuple-element.35), channel_id=1, source_target_pairs={{0,1},{1,0},{2,3},{3,2},{4,5},{5,4},{6,7},{7,6},{8,9},{9,8},{10,11... | collective-permute-start | bytes 1572872 | tf_op jit(solution)/shard_map/ppermute | solution.py:45

commit v3 on v2

--- a/solution.py
+++ b/solution.py
@@ -71,30 +71,29 @@
 
 
 def pack_counts(place, counts_t, slab):
-    strip = NK * OWN
+    group = 16
 
     def body(place_ref, counts_ref, slab_ref, out, held, slab_s, sems, slab_sem):
-        def copy(y, n):
-            z = lax.rem(place_ref[0] + ORDER[n], NZ)
-            start = pl.multiple_of(z * (NY * strip) + y * strip, strip)
-            return pltpu.make_async_copy(counts_ref.at[:, pl.ds(start, strip)], held.at[y, n], sems.at[y, n])
-
+        def copy(n):
+            rows = pl.ds(n * group, group)
+            return pltpu.make_async_copy(counts_ref.at[rows, :], held.at[rows, :], sems.at[n])
+
+        for n in range(ROWS // group):
+            copy(n).start()
         slab_copy = pltpu.make_async_copy(slab_ref, slab_s, slab_sem)
         slab_copy.start()
-        for y in range(NY):
-            for n in range(NZ):
-                copy(y, n).start()
         slab_copy.wait()
         for k in range(PEERS):
             half = k % NC
             out[k, :, SAMPLES:] = slab_s[:, half * HALF : (half + 1) * HALF]
-        for y in range(NY):
-            for n in range(NZ):
-                copy(y, n).wait()
-                for k in range(NK):
-                    out[y * NK + k, :, n * OWN : (n + 1) * OWN] = (
-                        held[y, n, :, k * OWN : (k + 1) * OWN].astype(F32).astype(BF16)
-                    )
+        starts = [lax.rem(place_ref[0] + z, NZ) * (PEERS * OWN) for z in ORDER]
+        for n in range(ROWS // group):
+            copy(n).wait()
+            rows = slice(n * group, (n + 1) * group)
+            for i, start in enumerate(starts):
+                for k in range(PEERS):
+                    at = pl.ds(pl.multiple_of(start + k * OWN, OWN), OWN)
+                    out[k, rows, i * OWN : (i + 1) * OWN] = held[rows, at].astype(F32).astype(BF16)
 
     return call(
         body,
@@ -102,18 +101,17 @@
         (place, far(counts_t), far(slab)),
         [IN_SMEM, IN_HBM, IN_HBM],
         [
-            pltpu.VMEM((NY, NZ, ROWS, strip), jnp.int32),
+            pltpu.VMEM((ROWS, NZ * PEERS * OWN), jnp.int32),
             pltpu.VMEM((ROWS, EMBED), BF16),
-            pltpu.SemaphoreType.DMA((NY, NZ)),
+            pltpu.SemaphoreType.DMA((ROWS // group,)),
             pltpu.SemaphoreType.DMA,
         ],
     )[0]
 
 
 def prepare(place, down, up, w, bias):
-    def body(place_ref, down_ref, up_ref, w_ref, bias_ref, rows_out, own_out, up_out):
-        start = pl.multiple_of(place_ref[0] * COLS, COLS)
-        here = pl.ds(start, COLS)
+    def body(place_ref, down_ref, up_ref, w_ref, bias_ref, rows_out):
+        here = pl.ds(pl.multiple_of(place_ref[0] * COLS, COLS), COLS)
         w = w_ref[:, here]
         for part in range(4):
             at = slice(part * 128, (part + 1) * 128)
@@ -123,8 +121,21 @@
         high = v.astype(BF16).astype(F32)
         at = lax.broadcasted_iota(jnp.int32, (EXT, COLS), 0)
         rows_out[2 * RANK :, :] = jnp.where(at < 2, high, jnp.where(at == 2, v - high, 0.0)).astype(BF16)
+
+    return call(
+        body,
+        [pltpu.VMEM((2 * RANK + EXT, COLS), BF16)],
+        (place, *(near(v) for v in (down, up, w, bias))),
+        [IN_SMEM] + [IN_VMEM] * 4,
+        cost=pl.CostEstimate(flops=1 << 29, bytes_accessed=6 << 20, transcendentals=0),
+    )[0]
+
+
+def prepare_own(place, up, w, bias):
+    def body(place_ref, up_ref, w_ref, bias_ref, own_out, up_out):
         k = place_ref[2] * NC + place_ref[3]
-        strip = pl.ds(pl.multiple_of(start + (place_ref[1] * 2 + lax.div(k, 4)) * 128, 128), 128)
+        start = place_ref[0] * COLS + (place_ref[1] * 2 + lax.div(k, 4)) * 128
+        strip = pl.ds(pl.multiple_of(start, 128), 128)
         offset = lax.rem(k, 4) * 32
         lane = lax.broadcasted_iota(jnp.int32, (32, 128), 1)
         row = lax.broadcasted_iota(jnp.int32, (32, 128), 0)
@@ -137,14 +148,10 @@
 
     return call(
         body,
-        [
-            pltpu.VMEM((2 * RANK + EXT, COLS), BF16),
-            pltpu.VMEM((32, 128), F32),
-            pltpu.VMEM((32, RANK), F32),
-        ],
-        (place, *(near(v) for v in (down, up, w, bias))),
-        [IN_SMEM] + [IN_VMEM] * 4,
-        cost=pl.CostEstimate(flops=1 << 29, bytes_accessed=6 << 20, transcendentals=0),
+        [pltpu.VMEM((32, 128), F32), pltpu.VMEM((32, RANK), F32)],
+        (place, *(near(v) for v in (up, w, bias))),
+        [IN_SMEM] + [IN_VMEM] * 3,
+        cost=pl.CostEstimate(flops=1 << 27, bytes_accessed=1 << 20, transcendentals=0),
     )
 
 
@@ -171,8 +178,19 @@
     return jnp.where(at == 0, high, jnp.where(at == 1, sums - high, 0.0)).astype(BF16)
 
 
+def products(rows_ref, pooled, outs):
+    for part in range(4):
+        at = slice(part * 256, (part + 1) * 256)
+        product = dot(rows_ref[at, :], pooled, 1, 0).astype(BF16)
+        for i, out in enumerate(outs):
+            out[at, :] = product[:, i * OWN : (i + 1) * OWN]
+    ext = head_of(rows_ref, pooled)
+    for i, out in enumerate(outs):
+        out[2 * RANK :, :] = ext[:, i * OWN : (i + 1) * OWN]
+
+
 def forward_far(place, arrived, other, half, rows):
-    def body(place_ref, in_ref, other_ref, half_ref, rows_ref, pooled_ref, *outs):
+    def body(place_ref, in_ref, other_ref, half_ref, rows_ref, pooled_ref, out):
         core = place_ref[3]
         for y in range(NY):
             at = slice(y * 512, (y + 1) * 512)
@@ -182,30 +200,32 @@
             pooled_ref[pl.ds(partners, HALF), :] = dot(
                 other_ref[at, :].T, in_ref[at, :SAMPLES], 1, 0
             ).astype(BF16)
-        pooled = pooled_ref[:, OWN:]
-        for part in range(4):
-            at = slice(part * 256, (part + 1) * 256)
-            product = dot(rows_ref[at, :], pooled, 1, 0).astype(BF16)
-            for i, out in enumerate(outs):
-                out[at, :] = product[:, i * OWN : (i + 1) * OWN]
-        ext = head_of(rows_ref, pooled)
-        for i, out in enumerate(outs):
-            out[2 * RANK :, :] = ext[:, i * OWN : (i + 1) * OWN]
-
-    return call(
-        body,
-        [pltpu.VMEM((COLS, SAMPLES), BF16)] + [pltpu.VMEM((2 * RANK + EXT, OWN), BF16)] * (NZ - 1),
+        products(rows_ref, pooled_ref[:, OWN : 2 * OWN], (out,))
+
+    return call(
+        body,
+        [pltpu.VMEM((COLS, SAMPLES), BF16), pltpu.VMEM((2 * RANK + EXT, OWN), BF16)],
         (place, near(arrived), near(other), near(half), near(rows)),
         [IN_SMEM] + [IN_VMEM] * 4,
         cost=pl.CostEstimate(flops=3 << 30, bytes_accessed=4 << 20, transcendentals=0),
     )
 
 
+def forward_near(pooled, rows):
+    def body(pooled_ref, rows_ref, *outs):
+        products(rows_ref, pooled_ref[:, 2 * OWN :], outs)
+
+    return call(
+        body,
+        [pltpu.VMEM((2 * RANK + EXT, OWN), BF16)] * 2,
+        (near(pooled), near(rows)),
+        cost=pl.CostEstimate(flops=1 << 30, bytes_accessed=2 << 20, transcendentals=0),
+    )
+
+
 def forward_own(pooled, rows):
     def body(pooled_ref, rows_ref, out):
-        pooled = pooled_ref[:, :OWN]
-        out[0 : 2 * RANK, :] = dot(rows_ref[0 : 2 * RANK, :], pooled, 1, 0).astype(BF16)
-        out[2 * RANK :, :] = head_of(rows_ref, pooled)
+        products(rows_ref, pooled_ref[:, :OWN], (out,))
 
     return call(
         body,
@@ -233,7 +253,9 @@
         rows = jnp.where((at == 0) | (at == 2), high, jnp.where(at == 1, g - high, 0.0))
         out[2 * RANK :, :] = rows.astype(BF16)
 
-    return call(body, [pltpu.VMEM((2 * RANK + EXT, OWN), BF16)], (*(near(p) for p in parts), labels))[0]
+    return call(
+        body, [pltpu.VMEM((2 * RANK + EXT, OWN), BF16)], (*(near(p) for p in parts), labels)
+    )[0]
 
 
 def by_sample(*blocks):
@@ -388,17 +410,19 @@
 
 def local(slab, counts, cross_down, cross_up, cross_bias, out_weight, labels):
     place = jnp.stack([lax.axis_index(a) for a in ALL]).astype(jnp.int32)
-    rows, own, up_own = prepare(
-        place, cross_down, cross_up, out_weight.reshape(1, -1), cross_bias.reshape(1, -1)
-    )
+    w_row, bias_row = out_weight.reshape(1, -1), cross_bias.reshape(1, -1)
+    rows = prepare(place, cross_down, cross_up, w_row, bias_row)
+    own, up_own = prepare_own(place, cross_up, w_row, bias_row)
     sent = pack_counts(place, counts.T, slab)
     arrived = lax.all_to_all(sent, PLANE, 0, 0, tiled=True).reshape(PEERS * ROWS, SAMPLES + HALF)
     other = shift(arrived[:, SAMPLES:], dc=1)
     half = pool_half(arrived)
-    pooled, *chunks = forward_far(place, arrived, other, half, rows)
-    parts = []
-    for i, chunk in zip(ORDER[1:], chunks):
-        parts.append(shift(chunk, dz=i))
+    pooled, chunk2 = forward_far(place, arrived, other, half, rows)
+    part2 = shift(chunk2, dz=2)
+    chunk1, chunk3 = forward_near(pooled, rows)
+    part1 = shift(chunk1, dz=1)
+    part3 = shift(chunk3, dz=3)
+    parts = [part2, part1, part3]
     chunk = forward_own(pooled, rows)
     block0 = own_samples([chunk] + parts, labels.reshape(1, OWN))
     blocks = []

time: 117 us -> 124 us (1.060)
  waiting for transfers between devices: 19.4 us -> 47.3 us
  blocking collectives: 68.9 us -> 41.6 us
  Pallas kernels: 14.7 us -> 16.9 us
  local copies, waits for them, and re-layouts: 0.06 us -> 2.25 us
    all_to_all x1 -> x0, blocking collectives: 27.3 us -> none  [local(): shares = lax.all_to_all(paired, ('y', 'x'), 0, 0, tiled=True)]
    all_to_all x0 -> x1, waiting for transfers between devices: none -> 25.2 us  [local(): shares = lax.all_to_all(paired, ('y', 'x'), 0, 0, tiled=True)]
    all_to_all x0 -> x1, starting transfers between devices: none -> 3.71 us  [local(): shares = lax.all_to_all(paired, ('y', 'x'), 0, 0, tiled=True)]
    ppermute x9, starting transfers between devices: 13.4 us -> 10.7 us  [shift(): return lax.ppermute(value, ALL, pairs)]
    ppermute x9, waiting for transfers between devices: 19.4 us -> 22.1 us  [shift(): return lax.ppermute(value, ALL, pairs)]
    unnamed x10 -> x12, local copies, waits for them, and re-layouts: 0.03 us -> 2.21 us
    pallas_call x11 -> x13, Pallas kernels: 14.7 us -> 16.9 us  [call(): pl.pallas_call(body, in_specs=specs or [pl.BlockSpec(memory_space=pltpu.V...]
  transfers between devices with their start and end apart: 9 -> 10, of which waited for: 7 -> 9; matrix products, arithmetic and copies ran while one was open for 0% -> 0% of each run, Pallas kernels for 5% -> 5%
where the time goes in v3:
time: 124 us; the launch traced here: 123 us
  waiting for transfers between devices  47.3 us (38%)
  blocking collectives  41.6 us (34%)
  Pallas kernels  16.9 us (14%)
  starting transfers between devices  14.4 us (12%)
  local copies, waits for them, and re-layouts  2.25 us (2%)
    all_to_all x1, blocking collectives, local(): lax.all_to_all(sent, PLANE, 0, 0, tiled=True)  41.6 us
    all_to_all x1, waiting for transfers between devices, local(): shares = lax.all_to_all(paired, ('y', 'x'), 0, 0, tiled=True)  25.2 us
    ppermute x9, waiting for transfers between devices, shift(): return lax.ppermute(value, ALL, pairs)  22.1 us
    pallas_call x13, Pallas kernels, call(): pl.pallas_call(body, in_specs=specs or [pl.BlockSpec(memory_space=pltpu.V...  16.9 us
    ppermute x9, starting transfers between devices, shift(): return lax.ppermute(value, ALL, pairs)  10.7 us
    all_to_all x1, starting transfers between devices, local(): shares = lax.all_to_all(paired, ('y', 'x'), 0, 0, tiled=True)  3.71 us
  transfers between devices with their start and end apart: 10, of which 9 were waited for; matrix products, arithmetic and copies ran while one was open for 0% of the time, Pallas kernels for 5%

profile of v3, /device:TPU:0, one launch (start us, length us, event | category | flops | bytes accessed | tf_op | source)
XLA Modules:
  0.0 123.2 jit_solution(6659623181705241553)
XLA Ops:
  0.6 0.1 pad_add_fusion.place_ref
  0.7 0.0 copy-start.2
  0.7 3.5 %shard_map.110 = bf16[32,64,640]{2,1,0:T(8,128)(2,1)S(1)} custom-call(s32[4]{0:T(128)S(1)} %pad_add_fusion.place_ref, s32[64,16384]{1,0:T(8,128)} %bitcast.22, bf16[64,256]{1,0:T(8,128)(2,1)} %slab_ref.1), custom_call_target="tpu_custom_call" | custom-call | tf_op jit(solution)/shard_map/pallas_call | solution.py:57
  4.2 0.0 copy-start
  4.3 0.0 copy-start.3
  4.3 0.0 copy-start.4
  4.3 41.6 %all_to_all.10 = bf16[32,64,640]{2,1,0:T(8,128)(2,1)S(1)} all-to-all(bf16[32,64,640]{2,1,0:T(8,128)(2,1)S(1)} %shard_map.110), channel_id=1, replica_groups=mesh['z'=4,'y'=4,'x'=4,'c'=2] {'y','x','c'}, dimensions={0} | all-to-all | bytes 5242880 | tf_op jit(solution)/shard_map/all_to_all | solution.py:417
  45.9 0.2 collective-permute-start
  46.1 0.0 copy-done.2
  46.1 0.0 copy-done
  46.1 0.0 copy-done.3
  46.1 0.0 copy-done.4
  46.1 1.2 shard_map.112.rows_ref
  47.3 0.5 shard_map.111.half_ref
  47.7 0.1 collective-permute-done.other_ref
  47.9 1.8 %shard_map.113 = (bf16[1024,512]{1,0:T(8,128)(2,1)S(1)}, bf16[1040,128]{1,0:T(8,128)(2,1)S(1)}) custom-call(s32[4]{0:T(128)S(1)} %pad_add_fusion.place_ref, bf16[2048,640]{1,0:T(8,128)(2,1)S(1)} %bitcast.14, bf16[2048,128]{1,0:T(8,128)(2,1)S(1)} %collective-permute-done.other_ref, bf16[512,512]{1,0:T(8,128)(2,1)S(1)} %shard_map.111.half_ref, ...), custom_call_target="tpu_custom_call" | custom-call | flops 3221225472 | bytes 4194304 | tf_op jit(solution)/shard_map/pallas_call | solution.py:57
  49.6 0.8 shard_map.115
  50.4 0.0 copy-start.5
  50.4 2.0 %collective-permute-start.2 = (bf16[1040,128]{1,0:T(8,128)(2,1)S(1)}, bf16[1040,128]{1,0:T(8,128)(2,1)S(1)}, u32[]{:S(2)}, u32[]{:S(2)}) collective-permute-start(bf16[1040,128]{1,0:T(8,128)(2,1)S(1)} %get-tuple-element.26), channel_id=1, source_target_pairs={{0,32},{1,33},{2,34},{3,35},{4,36},{5,37},{6,38},{7,39},{8,40},{9,... | collective-permute-start | bytes 798728 | tf_op jit(solution)/shard_map/ppermute | solution.py:45
  52.4 2.2 %collective-permute-start.3 = (bf16[1040,128]{1,0:T(8,128)(2,1)S(1)}, bf16[1040,128]{1,0:T(8,128)(2,1)S(1)}, u32[]{:S(2)}, u32[]{:S(2)}) collective-permute-start(bf16[1040,128]{1,0:T(8,128)(2,1)S(1)} %get-tuple-element.27), channel_id=1, source_target_pairs={{0,96},{1,97},{2,98},{3,99},{4,100},{5,101},{6,102},{7,103},{8,104... | collective-permute-start | bytes 798728 | tf_op jit(solution)/shard_map/ppermute | solution.py:45
  54.6 1.8 %collective-permute-start.1 = (bf16[1040,128]{1,0:T(8,128)(2,1)S(1)}, bf16[1040,128]{1,0:T(8,128)(2,1)S(1)}, u32[]{:S(2)}, u32[]{:S(2)}) collective-permute-start(bf16[1040,128]{1,0:T(8,128)(2,1)S(1)} %get-tuple-element.25), channel_id=1, source_target_pairs={{0,64},{1,65},{2,66},{3,67},{4,68},{5,69},{6,70},{7,71},{8,72},{9,... | collective-permute-start | bytes 798728 | tf_op jit(solution)/shard_map/ppermute | solution.py:45
  56.4 0.7 shard_map.114.p0
  57.1 4.2 %collective-permute-done.2.p2 = bf16[1040,128]{1,0:T(8,128)(2,1)S(1)} collective-permute-done((bf16[1040,128]{1,0:T(8,128)(2,1)S(1)}, bf16[1040,128]{1,0:T(8,128)(2,1)S(1)}, u32[]{:S(2)}, u32[]{:S(2)}) %collective-permute-start.2) | collective-permute-done | bytes 266272 | tf_op jit(solution)/shard_map/ppermute | solution.py:45
  61.4 5.1 %collective-permute-done.3.p3 = bf16[1040,128]{1,0:T(8,128)(2,1)S(1)} collective-permute-done((bf16[1040,128]{1,0:T(8,128)(2,1)S(1)}, bf16[1040,128]{1,0:T(8,128)(2,1)S(1)}, u32[]{:S(2)}, u32[]{:S(2)}) %collective-permute-start.3) | collective-permute-done | bytes 266272 | tf_op jit(solution)/shard_map/ppermute | solution.py:45
  66.4 1.8 %collective-permute-done.1.p1 = bf16[1040,128]{1,0:T(8,128)(2,1)S(1)} collective-permute-done((bf16[1040,128]{1,0:T(8,128)(2,1)S(1)}, bf16[1040,128]{1,0:T(8,128)(2,1)S(1)}, u32[]{:S(2)}, u32[]{:S(2)}) %collective-permute-start.1) | collective-permute-done | bytes 266272 | tf_op jit(solution)/shard_map/ppermute | solution.py:45
  68.2 0.0 copy-done.5
  68.2 0.3 shard_map.116.b0
  68.5 0.5 collective-permute-start.6
  69.0 3.4 %collective-permute-start.4 = (bf16[1040,128]{1,0:T(8,128)(2,1)S(1)}, bf16[1040,128]{1,0:T(8,128)(2,1)S(1)}, u32[]{:S(2)}, u32[]{:S(2)}) collective-permute-start(bf16[1040,128]{1,0:T(8,128)(2,1)S(1)} %shard_map.116.b0), channel_id=1, source_target_pairs={{0,96},{1,97},{2,98},{3,99},{4,100},{5,101},{6,102},{7,103},{8,104... | collective-permute-start | bytes 798728 | tf_op jit(solution)/shard_map/ppermute | solution.py:45
  72.4 0.0 collective-permute-start.5
  72.4 7.0 %collective-permute-done.6.b2 = bf16[1040,128]{1,0:T(8,128)(2,1)S(1)} collective-permute-done((bf16[1040,128]{1,0:T(8,128)(2,1)S(1)}, bf16[1040,128]{1,0:T(8,128)(2,1)S(1)}, u32[]{:S(2)}, u32[]{:S(2)}) %collective-permute-start.6) | collective-permute-done | bytes 266272 | tf_op jit(solution)/shard_map/ppermute | solution.py:45
  79.4 1.8 %shard_map.117 = (f32[1024,1024]{1,0:T(8,128)S(1)}, f32[16,1024]{1,0:T(8,128)S(1)}, f32[2048,256]{1,0:T(8,128)S(1)}) custom-call(bf16[1040,128]{1,0:T(8,128)(2,1)S(1)} %shard_map.116.b0, bf16[1040,128]{1,0:T(8,128)(2,1)S(1)} %collective-permute-done.6.b2, bf16[1024,512]{1,0:T(8,128)(2,1)S(1)} %get-tuple-element.24.pooled_ref, ...), custom_call_target="tpu_custom_call" | custom-call | flops 2147483648 | bytes 6291456 | tf_op jit(solution)/shard_map/pallas_call | solution.py:57
  81.2 1.5 %collective-permute-done.4.b1 = bf16[1040,128]{1,0:T(8,128)(2,1)S(1)} collective-permute-done((bf16[1040,128]{1,0:T(8,128)(2,1)S(1)}, bf16[1040,128]{1,0:T(8,128)(2,1)S(1)}, u32[]{:S(2)}, u32[]{:S(2)}) %collective-permute-start.4) | collective-permute-done | bytes 266272 | tf_op jit(solution)/shard_map/ppermute | solution.py:45
  82.7 0.8 collective-permute-done.5.b3
  83.5 1.4 %shard_map.118 = (bf16[16,272,128]{2,1,0:T(8,128)(2,1)S(1)}, bf16[16,272,128]{2,1,0:T(8,128)(2,1)S(1)}, bf16[256,1040]{1,0:T(8,128)(2,1)S(1)}) custom-call(s32[4]{0:T(128)S(1)} %pad_add_fusion.place_ref, bf16[1040,128]{1,0:T(8,128)(2,1)S(1)} %collective-permute-done.4.b1, bf16[1040,128]{1,0:T(8,128)(2,1)S(1)} %collective-permute-done.5.b3, ...), custom_call_target="tpu_custom_call" | custom-call | flops 1073741824 | bytes 4194304 | tf_op jit(solution)/shard_map/pallas_call | solution.py:57
  84.9 0.1 collective-permute-start.8
  85.0 1.7 %shard_map.119 = (bf16[16,128,128]{2,1,0:T(8,128)(2,1)S(1)}, bf16[16,128,128]{2,1,0:T(8,128)(2,1)S(1)}) custom-call(s32[4]{0:T(128)S(1)} %pad_add_fusion.place_ref, bf16[256,1040]{1,0:T(8,128)(2,1)S(1)} %get-tuple-element.30.g_ref, bf16[2048,640]{1,0:T(8,128)(2,1)S(1)} %bitcast.16, bf16[1040,1024]{1,0:T(8,128)(2,1)S(1)} %shard_map.112.rows_ref, ...), custom_call_target="tpu_custom_call" | custom-call | flops 1073741824 | bytes 4194304 | tf_op jit(solution)/shard_map/pallas_call | solution.py:57
  86.7 0.6 collective-permute-start.7
  87.3 1.5 %collective-permute-done.7.b = bf16[16,128,128]{2,1,0:T(8,128)(2,1)S(1)} collective-permute-done((bf16[16,128,128]{2,1,0:T(8,128)(2,1)S(1)}, bf16[16,128,128]{2,1,0:T(8,128)(2,1)S(1)}, u32[]{:S(2)}, u32[]{:S(2)}) %collective-permute-start.7) | collective-permute-done | bytes 524320 | tf_op jit(solution)/shard_map/ppermute | solution.py:45
  88.8 0.0 collective-permute-done.8.d
  88.8 1.6 %shard_map.120 = bf16[16,400,128]{2,1,0:T(8,128)(2,1)} custom-call(bf16[16,128,128]{2,1,0:T(8,128)(2,1)S(1)} %get-tuple-element.32.a, bf16[16,128,128]{2,1,0:T(8,128)(2,1)S(1)} %collective-permute-done.7.b, bf16[16,272,128]{2,1,0:T(8,128)(2,1)S(1)} %get-tuple-element.34.c, bf16[16,272,128]{2,1,0:T(8,128)(2,1)S(1)} %collective-permute-done.8.d), custom_call_target="tpu_custom_call" | custom-call | tf_op jit(solution)/shard_map/pallas_call | solution.py:57
  90.4 3.7 %all-to-all-start.1 = ((bf16[16,400,128]{2,1,0:T(8,128)(2,1)}), bf16[16,400,128]{2,1,0:T(8,128)(2,1)S(1)}, u32[]{:S(2)}, u32[]{:S(2)}) async-start(bf16[16,400,128]{2,1,0:T(8,128)(2,1)} %shard_map.120), calls=%async_computation.1 | async-start | bytes 3276800 | tf_op jit(solution)/shard_map/all_to_all | solution.py:437
  94.1 0.0 copy-start.1
  94.1 2.2 %copy-done.1 = bf16[512,4096]{1,0:T(8,128)(2,1)S(1)} copy-done((bf16[512,4096]{1,0:T(8,128)(2,1)S(1)}, bf16[512,4096]{1,0:T(8,128)(2,1)}, u32[]{:S(2)}) %copy-start.1) | copy-done | bytes 4194328
  96.3 0.7 shard_map.121
  97.0 25.2 %all-to-all-done.1.in_ref = bf16[16,400,128]{2,1,0:T(8,128)(2,1)S(1)} async-done(((bf16[16,400,128]{2,1,0:T(8,128)(2,1)}), bf16[16,400,128]{2,1,0:T(8,128)(2,1)S(1)}, u32[]{:S(2)}, u32[]{:S(2)}) %all-to-all-start.1) | async-done | bytes 1638432 | tf_op jit(solution)/shard_map/all_to_all | solution.py:437
  122.2 0.9 shard_map.122
  (1 shorter events, 0.0 us)
Async XLA Ops:
  0.7 45.4 %copy-start.2 = (bf16[4096,512]{1,0:T(8,128)(2,1)S(1)}, bf16[4096,512]{1,0:T(8,128)(2,1)}, u32[]{:S(2)}) copy-start(bf16[4096,512]{1,0:T(8,128)(2,1)} %down_ref.1) | copy-start | bytes 12582916
  4.2 41.8 %copy-start = (bf16[512,4096]{1,0:T(8,128)(2,1)S(1)}, bf16[512,4096]{1,0:T(8,128)(2,1)}, u32[]{:S(2)}) copy-start(bf16[512,4096]{1,0:T(8,128)(2,1)} %up_ref.3) | copy-start | bytes 12582916
  4.3 41.8 %copy-start.3 = (f32[4096]{0:T(1024)S(1)}, f32[4096]{0:T(1024)}, u32[]{:S(2)}) copy-start(f32[4096]{0:T(1024)} %param.12) | copy-start | bytes 49156
  4.3 41.8 %copy-start.4 = (f32[4096]{0:T(1024)S(1)}, f32[4096]{0:T(1024)}, u32[]{:S(2)}) copy-start(f32[4096]{0:T(1024)} %param.11) | copy-start | bytes 49156
  45.9 2.0 %collective-permute-start = (bf16[2048,128]{1,0:T(8,128)(2,1)S(1)}, bf16[2048,128]{1,0:T(8,128)(2,1)S(1)}, u32[]{:S(2)}, u32[]{:S(2)}) collective-permute-start(bf16[2048,128]{1,0:T(8,128)(2,1)S(1)} %slice.4), channel_id=1, source_target_pairs={{0,1},{1,0},{2,3},{3,2},{4,5},{5,4},{6,7},{7,6},{8,9},{9,8},{10,11... | collective-permute-start | bytes 1572872 | tf_op jit(solution)/shard_map/ppermute | solution.py:45
  50.4 17.8 %copy-start.5 = (s32[128]{0:T(128)S(1)}, s32[128]{0:T(128)}, u32[]{:S(2)}) copy-start(s32[128]{0:T(128)} %param.13) | copy-start | bytes 1540
  50.4 10.9 %collective-permute-start.2 = (bf16[1040,128]{1,0:T(8,128)(2,1)S(1)}, bf16[1040,128]{1,0:T(8,128)(2,1)S(1)}, u32[]{:S(2)}, u32[]{:S(2)}) collective-permute-start(bf16[1040,128]{1,0:T(8,128)(2,1)S(1)} %get-tuple-element.26), channel_id=1, source_target_pairs={{0,32},{1,33},{2,34},{3,35},{4,36},{5,37},{6,38},{7,39},{8,40},{9,... | collective-permute-start | bytes 798728 | tf_op jit(solution)/shard_map/ppermute | solution.py:45
  52.4 14.0 %collective-permute-start.3 = (bf16[1040,128]{1,0:T(8,128)(2,1)S(1)}, bf16[1040,128]{1,0:T(8,128)(2,1)S(1)}, u32[]{:S(2)}, u32[]{:S(2)}) collective-permute-start(bf16[1040,128]{1,0:T(8,128)(2,1)S(1)} %get-tuple-element.27), channel_id=1, source_target_pairs={{0,96},{1,97},{2,98},{3,99},{4,100},{5,101},{6,102},{7,103},{8,104... | collective-permute-start | bytes 798728 | tf_op jit(solution)/shard_map/ppermute | solution.py:45
  54.6 13.6 %collective-permute-start.1 = (bf16[1040,128]{1,0:T(8,128)(2,1)S(1)}, bf16[1040,128]{1,0:T(8,128)(2,1)S(1)}, u32[]{:S(2)}, u32[]{:S(2)}) collective-permute-start(bf16[1040,128]{1,0:T(8,128)(2,1)S(1)} %get-tuple-element.25), channel_id=1, source_target_pairs={{0,64},{1,65},{2,66},{3,67},{4,68},{5,69},{6,70},{7,71},{8,72},{9,... | collective-permute-start | bytes 798728 | tf_op jit(solution)/shard_map/ppermute | solution.py:45
  68.5 10.8 %collective-permute-start.6 = (bf16[1040,128]{1,0:T(8,128)(2,1)S(1)}, bf16[1040,128]{1,0:T(8,128)(2,1)S(1)}, u32[]{:S(2)}, u32[]{:S(2)}) collective-permute-start(bf16[1040,128]{1,0:T(8,128)(2,1)S(1)} %shard_map.116.b0), channel_id=1, source_target_pairs={{0,64},{1,65},{2,66},{3,67},{4,68},{5,69},{6,70},{7,71},{8,72},{9,... | collective-permute-start | bytes 798728 | tf_op jit(solution)/shard_map/ppermute | solution.py:45
  69.0 13.7 %collective-permute-start.4 = (bf16[1040,128]{1,0:T(8,128)(2,1)S(1)}, bf16[1040,128]{1,0:T(8,128)(2,1)S(1)}, u32[]{:S(2)}, u32[]{:S(2)}) collective-permute-start(bf16[1040,128]{1,0:T(8,128)(2,1)S(1)} %shard_map.116.b0), channel_id=1, source_target_pairs={{0,96},{1,97},{2,98},{3,99},{4,100},{5,101},{6,102},{7,103},{8,104... | collective-permute-start | bytes 798728 | tf_op jit(solution)/shard_map/ppermute | solution.py:45
  72.4 11.1 %collective-permute-start.5 = (bf16[1040,128]{1,0:T(8,128)(2,1)S(1)}, bf16[1040,128]{1,0:T(8,128)(2,1)S(1)}, u32[]{:S(2)}, u32[]{:S(2)}) collective-permute-start(bf16[1040,128]{1,0:T(8,128)(2,1)S(1)} %shard_map.116.b0), channel_id=1, source_target_pairs={{0,32},{1,33},{2,34},{3,35},{4,36},{5,37},{6,38},{7,39},{8,40},{9,... | collective-permute-start | bytes 798728 | tf_op jit(solution)/shard_map/ppermute | solution.py:45
  84.9 3.9 %collective-permute-start.8 = (bf16[16,272,128]{2,1,0:T(8,128)(2,1)S(1)}, bf16[16,272,128]{2,1,0:T(8,128)(2,1)S(1)}, u32[]{:S(2)}, u32[]{:S(2)}) collective-permute-start(bf16[16,272,128]{2,1,0:T(8,128)(2,1)S(1)} %get-tuple-element.35), channel_id=1, source_target_pairs={{0,1},{1,0},{2,3},{3,2},{4,5},{5,4},{6,7},{7,6},{8,9},{9,8},{10,11... | collective-permute-start | bytes 3342344 | tf_op jit(solution)/shard_map/ppermute | solution.py:45
  86.7 2.1 %collective-permute-start.7 = (bf16[16,128,128]{2,1,0:T(8,128)(2,1)S(1)}, bf16[16,128,128]{2,1,0:T(8,128)(2,1)S(1)}, u32[]{:S(2)}, u32[]{:S(2)}) collective-permute-start(bf16[16,128,128]{2,1,0:T(8,128)(2,1)S(1)} %get-tuple-element.33), channel_id=1, source_target_pairs={{0,1},{1,0},{2,3},{3,2},{4,5},{5,4},{6,7},{7,6},{8,9},{9,8},{10,11... | collective-permute-start | bytes 1572872 | tf_op jit(solution)/shard_map/ppermute | solution.py:45
  90.4 31.8 %all-to-all-start.1 = ((bf16[16,400,128]{2,1,0:T(8,128)(2,1)}), bf16[16,400,128]{2,1,0:T(8,128)(2,1)S(1)}, u32[]{:S(2)}, u32[]{:S(2)}) async-start(bf16[16,400,128]{2,1,0:T(8,128)(2,1)} %shard_map.120), calls=%async_computation.1 | async-start | bytes 3276800 | tf_op jit(solution)/shard_map/all_to_all | solution.py:437
  94.1 2.2 %copy-start.1 = (bf16[512,4096]{1,0:T(8,128)(2,1)S(1)}, bf16[512,4096]{1,0:T(8,128)(2,1)}, u32[]{:S(2)}) copy-start(bf16[512,4096]{1,0:T(8,128)(2,1)} %up_ref.3) | copy-start | bytes 12582916

commit v4 on v3

--- a/solution.py
+++ b/solution.py
@@ -253,9 +253,7 @@
         rows = jnp.where((at == 0) | (at == 2), high, jnp.where(at == 1, g - high, 0.0))
         out[2 * RANK :, :] = rows.astype(BF16)
 
-    return call(
-        body, [pltpu.VMEM((2 * RANK + EXT, OWN), BF16)], (*(near(p) for p in parts), labels)
-    )[0]
+    return call(body, [pltpu.VMEM((2 * RANK + EXT, OWN), BF16)], (*(near(p) for p in parts), labels))[0]
 
 
 def by_sample(*blocks):
@@ -358,25 +356,36 @@
     )
 
 
-def pair_sums(slab, slab_partner, weights, weights_partner):
-    def body(a, b, c, d, out):
-        out[:, : 2 * ROWS, :] = (a[...].astype(F32) + b[...].astype(F32)).astype(BF16)
-        out[:, 2 * ROWS :, :] = (c[...].astype(F32) + d[...].astype(F32)).astype(BF16)
-
-    return call(
-        body,
-        [pltpu.VMEM((NY * NX, PACK, 128), BF16)],
-        tuple(near(v) for v in (slab, slab_partner, weights, weights_partner)),
-    )[0]
+AWAY = (
+    (2, 2), (2, 1), (1, 2), (2, 3), (3, 2), (1, 1), (3, 3), (1, 3), (3, 1), (2, 0), (0, 2), (1, 0), (0, 1), (3, 0), (0, 3)
+)
+
+
+def pair_sums(place, slab, slab_partner, weights, weights_partner):
+    def body(place_ref, a, b, c, d, *outs):
+        for (dy, dx), out in zip(AWAY + ((0, 0),), outs):
+            at = lax.rem(place_ref[1] + dy, NY) * NX + lax.rem(place_ref[2] + dx, NX)
+            out[: 2 * ROWS, :] = (a[at].astype(F32) + b[at].astype(F32)).astype(BF16)
+            out[2 * ROWS :, :] = (c[at].astype(F32) + d[at].astype(F32)).astype(BF16)
+
+    return call(
+        body,
+        [pltpu.VMEM((PACK, 128), BF16)] * (NY * NX),
+        (place, *(near(v) for v in (slab, slab_partner, weights, weights_partner))),
+        [IN_SMEM] + [IN_VMEM] * 4,
+    )
 
 
 def finish(shares, own, up_own):
-    def body(in_ref, own_ref, up_ref, slab_out, down_out, up_out, bias_out, out_out):
+    def body(*refs):
+        ins = refs[: NY * NX]
+        own_ref, up_ref, slab_out, down_out, up_out, bias_out, out_out = refs[NY * NX :]
+
         def total(at):
-            held = in_ref[0, at, :].astype(F32)
-            for i in range(1, NY * NX):
-                held = held + in_ref[i, at, :].astype(F32)
-            return held
+            held = [ref[at, :].astype(F32) for ref in ins]
+            while len(held) > 1:
+                held = [a + b for a, b in zip(held[::2], held[1::2])]
+            return held[0]
 
         slab_out[:, :128] = total(slice(0, ROWS))
         slab_out[:, 128:] = total(slice(ROWS, 2 * ROWS))
@@ -404,7 +413,7 @@
             jax.ShapeDtypeStruct((1, 32), F32),
             jax.ShapeDtypeStruct((1, 32), F32),
         ],
-        (near(shares), near(own), near(up_own)),
+        (*(near(v) for v in shares), near(own), near(up_own)),
     )
 
 
@@ -433,8 +442,10 @@
     weights, given, g = backward_weights(place, block1, block3, pooled, both, sums)
     weights_partner = shift(given, dc=1)
     slabs, given = backward_slab(place, g, arrived, rows, slab_first)
-    paired = pair_sums(slabs, shift(given, dc=1), weights, weights_partner)
-    shares = lax.all_to_all(paired, ("y", "x"), 0, 0, tiled=True)
+    *leaving, kept = pair_sums(place, slabs, shift(given, dc=1), weights, weights_partner)
+    shares = [kept]
+    for (dy, dx), value in zip(AWAY, leaving):
+        shares.append(shift(value, dy=dy, dx=dx))
     grad_slab, grad_down, grad_up, grad_bias, grad_out = finish(shares, own, up_own)
     return grad_slab, grad_down, grad_up.T, grad_bias.reshape(32), grad_out.reshape(32)
 

time: 124 us -> 129 us (1.040)
  starting transfers between devices: 14.4 us -> 36.3 us
  waiting for transfers between devices: 47.3 us -> 33.5 us
  local copies, waits for them, and re-layouts: 2.25 us -> 0.06 us
    ppermute x9 -> x24, starting transfers between devices: 10.7 us -> 36.3 us  [shift(): return lax.ppermute(value, ALL, pairs)]
    all_to_all x1 -> x0, waiting for transfers between devices: 25.2 us -> none  [local(): shares = lax.all_to_all(paired, ('y', 'x'), 0, 0, tiled=True)]
    ppermute x9 -> x24, waiting for transfers between devices: 22.1 us -> 33.5 us  [shift(): return lax.ppermute(value, ALL, pairs)]
    all_to_all x1 -> x0, starting transfers between devices: 3.71 us -> none  [local(): shares = lax.all_to_all(paired, ('y', 'x'), 0, 0, tiled=True)]
    unnamed x12 -> x10, local copies, waits for them, and re-layouts: 2.21 us -> 0.03 us
  transfers between devices with their start and end apart: 10 -> 24, of which waited for: 9 -> 14; matrix products, arithmetic and copies ran while one was open for 0% -> 0% of each run, Pallas kernels for 5% -> 5%
where the time goes in v4:
time: 129 us
  blocking collectives  41.6 us (32%)
  starting transfers between devices  36.3 us (28%)
  waiting for transfers between devices  33.5 us (26%)
  Pallas kernels  16.2 us (13%)
    all_to_all x1, blocking collectives, local(): lax.all_to_all(sent, PLANE, 0, 0, tiled=True)  41.6 us
    ppermute x24, starting transfers between devices, shift(): return lax.ppermute(value, ALL, pairs)  36.3 us
    ppermute x24, waiting for transfers between devices, shift(): return lax.ppermute(value, ALL, pairs)  33.5 us
    pallas_call x13, Pallas kernels, call(): pl.pallas_call(body, in_specs=specs or [pl.BlockSpec(memory_space=pltpu.V...  16.2 us
  transfers between devices with their start and end apart: 24, of which 14 were waited for; matrix products, arithmetic and copies ran while one was open for 0% of the time, Pallas kernels for 5%

profile of v4, /device:TPU:0, one launch (start us, length us, event | category | flops | bytes accessed | tf_op | source)
XLA Modules:
  0.0 128.5 jit_solution(698281871708719738)
XLA Ops:
  0.6 0.1 pad_add_fusion.place_ref
  0.7 3.5 %shard_map.110 = bf16[32,64,640]{2,1,0:T(8,128)(2,1)S(1)} custom-call(s32[4]{0:T(128)S(1)} %pad_add_fusion.place_ref, s32[64,16384]{1,0:T(8,128)} %bitcast.22, bf16[64,256]{1,0:T(8,128)(2,1)} %slab_ref.1), custom_call_target="tpu_custom_call" | custom-call | tf_op jit(solution)/shard_map/pallas_call | solution.py:57
  4.2 0.0 copy-start
  4.3 0.0 copy-start.2
  4.3 0.0 copy-start.3
  4.3 41.6 %all_to_all.5 = bf16[32,64,640]{2,1,0:T(8,128)(2,1)S(1)} all-to-all(bf16[32,64,640]{2,1,0:T(8,128)(2,1)S(1)} %shard_map.110), channel_id=1, replica_groups=mesh['z'=4,'y'=4,'x'=4,'c'=2] {'y','x','c'}, dimensions={0} | all-to-all | bytes 5242880 | tf_op jit(solution)/shard_map/all_to_all | solution.py:426
  45.9 0.2 collective-permute-start
  46.1 1.2 shard_map.112.rows_ref
  47.3 0.5 shard_map.111.half_ref
  47.7 0.1 collective-permute-done.other_ref
  47.9 1.8 %shard_map.113 = (bf16[1024,512]{1,0:T(8,128)(2,1)S(1)}, bf16[1040,128]{1,0:T(8,128)(2,1)S(1)}) custom-call(s32[4]{0:T(128)S(1)} %pad_add_fusion.place_ref, bf16[2048,640]{1,0:T(8,128)(2,1)S(1)} %bitcast.14, bf16[2048,128]{1,0:T(8,128)(2,1)S(1)} %collective-permute-done.other_ref, bf16[512,512]{1,0:T(8,128)(2,1)S(1)} %shard_map.111.half_ref, ...), custom_call_target="tpu_custom_call" | custom-call | flops 3221225472 | bytes 4194304 | tf_op jit(solution)/shard_map/pallas_call | solution.py:57
  49.6 0.8 shard_map.115
  50.4 0.0 copy-start.4
  50.4 2.0 %collective-permute-start.2 = (bf16[1040,128]{1,0:T(8,128)(2,1)S(1)}, bf16[1040,128]{1,0:T(8,128)(2,1)S(1)}, u32[]{:S(2)}, u32[]{:S(2)}) collective-permute-start(bf16[1040,128]{1,0:T(8,128)(2,1)S(1)} %get-tuple-element.42), channel_id=1, source_target_pairs={{0,32},{1,33},{2,34},{3,35},{4,36},{5,37},{6,38},{7,39},{8,40},{9,... | collective-permute-start | bytes 798728 | tf_op jit(solution)/shard_map/ppermute | solution.py:45
  52.4 2.2 %collective-permute-start.3 = (bf16[1040,128]{1,0:T(8,128)(2,1)S(1)}, bf16[1040,128]{1,0:T(8,128)(2,1)S(1)}, u32[]{:S(2)}, u32[]{:S(2)}) collective-permute-start(bf16[1040,128]{1,0:T(8,128)(2,1)S(1)} %get-tuple-element.43), channel_id=1, source_target_pairs={{0,96},{1,97},{2,98},{3,99},{4,100},{5,101},{6,102},{7,103},{8,104... | collective-permute-start | bytes 798728 | tf_op jit(solution)/shard_map/ppermute | solution.py:45
  54.6 1.8 %collective-permute-start.1 = (bf16[1040,128]{1,0:T(8,128)(2,1)S(1)}, bf16[1040,128]{1,0:T(8,128)(2,1)S(1)}, u32[]{:S(2)}, u32[]{:S(2)}) collective-permute-start(bf16[1040,128]{1,0:T(8,128)(2,1)S(1)} %get-tuple-element.41), channel_id=1, source_target_pairs={{0,64},{1,65},{2,66},{3,67},{4,68},{5,69},{6,70},{7,71},{8,72},{9,... | collective-permute-start | bytes 798728 | tf_op jit(solution)/shard_map/ppermute | solution.py:45
  56.4 0.7 shard_map.114.p0
  57.1 4.3 %collective-permute-done.2.p2 = bf16[1040,128]{1,0:T(8,128)(2,1)S(1)} collective-permute-done((bf16[1040,128]{1,0:T(8,128)(2,1)S(1)}, bf16[1040,128]{1,0:T(8,128)(2,1)S(1)}, u32[]{:S(2)}, u32[]{:S(2)}) %collective-permute-start.2) | collective-permute-done | bytes 266272 | tf_op jit(solution)/shard_map/ppermute | solution.py:45
  61.4 5.1 %collective-permute-done.3.p3 = bf16[1040,128]{1,0:T(8,128)(2,1)S(1)} collective-permute-done((bf16[1040,128]{1,0:T(8,128)(2,1)S(1)}, bf16[1040,128]{1,0:T(8,128)(2,1)S(1)}, u32[]{:S(2)}, u32[]{:S(2)}) %collective-permute-start.3) | collective-permute-done | bytes 266272 | tf_op jit(solution)/shard_map/ppermute | solution.py:45
  66.5 1.8 %collective-permute-done.1.p1 = bf16[1040,128]{1,0:T(8,128)(2,1)S(1)} collective-permute-done((bf16[1040,128]{1,0:T(8,128)(2,1)S(1)}, bf16[1040,128]{1,0:T(8,128)(2,1)S(1)}, u32[]{:S(2)}, u32[]{:S(2)}) %collective-permute-start.1) | collective-permute-done | bytes 266272 | tf_op jit(solution)/shard_map/ppermute | solution.py:45
  68.3 0.3 shard_map.116.b0
  68.5 0.5 collective-permute-start.6
  69.0 3.4 %collective-permute-start.4 = (bf16[1040,128]{1,0:T(8,128)(2,1)S(1)}, bf16[1040,128]{1,0:T(8,128)(2,1)S(1)}, u32[]{:S(2)}, u32[]{:S(2)}) collective-permute-start(bf16[1040,128]{1,0:T(8,128)(2,1)S(1)} %shard_map.116.b0), channel_id=1, source_target_pairs={{0,96},{1,97},{2,98},{3,99},{4,100},{5,101},{6,102},{7,103},{8,104... | collective-permute-start | bytes 798728 | tf_op jit(solution)/shard_map/ppermute | solution.py:45
  72.4 0.0 collective-permute-start.5
  72.4 7.0 %collective-permute-done.6.b2 = bf16[1040,128]{1,0:T(8,128)(2,1)S(1)} collective-permute-done((bf16[1040,128]{1,0:T(8,128)(2,1)S(1)}, bf16[1040,128]{1,0:T(8,128)(2,1)S(1)}, u32[]{:S(2)}, u32[]{:S(2)}) %collective-permute-start.6) | collective-permute-done | bytes 266272 | tf_op jit(solution)/shard_map/ppermute | solution.py:45
  79.4 1.8 %shard_map.117 = (f32[1024,1024]{1,0:T(8,128)S(1)}, f32[16,1024]{1,0:T(8,128)S(1)}, f32[2048,256]{1,0:T(8,128)S(1)}) custom-call(bf16[1040,128]{1,0:T(8,128)(2,1)S(1)} %shard_map.116.b0, bf16[1040,128]{1,0:T(8,128)(2,1)S(1)} %collective-permute-done.6.b2, bf16[1024,512]{1,0:T(8,128)(2,1)S(1)} %get-tuple-element.40.pooled_ref, ...), custom_call_target="tpu_custom_call" | custom-call | flops 2147483648 | bytes 6291456 | tf_op jit(solution)/shard_map/pallas_call | solution.py:57
  81.2 1.6 %collective-permute-done.4.b1 = bf16[1040,128]{1,0:T(8,128)(2,1)S(1)} collective-permute-done((bf16[1040,128]{1,0:T(8,128)(2,1)S(1)}, bf16[1040,128]{1,0:T(8,128)(2,1)S(1)}, u32[]{:S(2)}, u32[]{:S(2)}) %collective-permute-start.4) | collective-permute-done | bytes 266272 | tf_op jit(solution)/shard_map/ppermute | solution.py:45
  82.8 0.8 collective-permute-done.5.b3
  83.6 1.4 %shard_map.118 = (bf16[16,272,128]{2,1,0:T(8,128)(2,1)S(1)}, bf16[16,272,128]{2,1,0:T(8,128)(2,1)S(1)}, bf16[256,1040]{1,0:T(8,128)(2,1)S(1)}) custom-call(s32[4]{0:T(128)S(1)} %pad_add_fusion.place_ref, bf16[1040,128]{1,0:T(8,128)(2,1)S(1)} %collective-permute-done.4.b1, bf16[1040,128]{1,0:T(8,128)(2,1)S(1)} %collective-permute-done.5.b3, ...), custom_call_target="tpu_custom_call" | custom-call | flops 1073741824 | bytes 4194304 | tf_op jit(solution)/shard_map/pallas_call | solution.py:57
  85.0 0.1 collective-permute-start.8
  85.0 1.7 %shard_map.119 = (bf16[16,128,128]{2,1,0:T(8,128)(2,1)S(1)}, bf16[16,128,128]{2,1,0:T(8,128)(2,1)S(1)}) custom-call(s32[4]{0:T(128)S(1)} %pad_add_fusion.place_ref, bf16[256,1040]{1,0:T(8,128)(2,1)S(1)} %get-tuple-element.46.g_ref, bf16[2048,640]{1,0:T(8,128)(2,1)S(1)} %bitcast.16, bf16[1040,1024]{1,0:T(8,128)(2,1)S(1)} %shard_map.112.rows_ref, ...), custom_call_target="tpu_custom_call" | custom-call | flops 1073741824 | bytes 4194304 | tf_op jit(solution)/shard_map/pallas_call | solution.py:57
  86.7 0.6 collective-permute-start.7
  87.3 1.5 %collective-permute-done.7.b = bf16[16,128,128]{2,1,0:T(8,128)(2,1)S(1)} collective-permute-done((bf16[16,128,128]{2,1,0:T(8,128)(2,1)S(1)}, bf16[16,128,128]{2,1,0:T(8,128)(2,1)S(1)}, u32[]{:S(2)}, u32[]{:S(2)}) %collective-permute-start.7) | collective-permute-done | bytes 524320 | tf_op jit(solution)/shard_map/ppermute | solution.py:45
  88.8 0.0 collective-permute-done.8.d
  88.8 0.9 shard_map.120
  89.8 1.6 %collective-permute-start.10 = (bf16[400,128]{1,0:T(8,128)(2,1)S(1)}, bf16[400,128]{1,0:T(8,128)(2,1)S(1)}, u32[]{:S(2)}, u32[]{:S(2)}) collective-permute-start(bf16[400,128]{1,0:T(8,128)(2,1)S(1)} %get-tuple-element.54), channel_id=1, source_target_pairs={{0,18},{1,19},{2,20},{3,21},{4,22},{5,23},{6,16},{7,17},{8,26},{9,... | collective-permute-start | bytes 307208 | tf_op jit(solution)/shard_map/ppermute | solution.py:45
  91.3 2.3 %collective-permute-start.11 = (bf16[400,128]{1,0:T(8,128)(2,1)S(1)}, bf16[400,128]{1,0:T(8,128)(2,1)S(1)}, u32[]{:S(2)}, u32[]{:S(2)}) collective-permute-start(bf16[400,128]{1,0:T(8,128)(2,1)S(1)} %get-tuple-element.55), channel_id=1, source_target_pairs={{0,12},{1,13},{2,14},{3,15},{4,8},{5,9},{6,10},{7,11},{8,20},{9,21... | collective-permute-start | bytes 307208 | tf_op jit(solution)/shard_map/ppermute | solution.py:45
  93.6 3.0 %collective-permute-start.12 = (bf16[400,128]{1,0:T(8,128)(2,1)S(1)}, bf16[400,128]{1,0:T(8,128)(2,1)S(1)}, u32[]{:S(2)}, u32[]{:S(2)}) collective-permute-start(bf16[400,128]{1,0:T(8,128)(2,1)S(1)} %get-tuple-element.56), channel_id=1, source_target_pairs={{0,22},{1,23},{2,16},{3,17},{4,18},{5,19},{6,20},{7,21},{8,30},{9,... | collective-permute-start | bytes 307208 | tf_op jit(solution)/shard_map/ppermute | solution.py:45
  96.7 3.2 %collective-permute-start.13 = (bf16[400,128]{1,0:T(8,128)(2,1)S(1)}, bf16[400,128]{1,0:T(8,128)(2,1)S(1)}, u32[]{:S(2)}, u32[]{:S(2)}) collective-permute-start(bf16[400,128]{1,0:T(8,128)(2,1)S(1)} %get-tuple-element.57), channel_id=1, source_target_pairs={{0,28},{1,29},{2,30},{3,31},{4,24},{5,25},{6,26},{7,27},{8,4},{9,5... | collective-permute-start | bytes 307208 | tf_op jit(solution)/shard_map/ppermute | solution.py:45
  99.9 0.0 collective-permute-start.14
  99.9 2.1 %collective-permute-done.10.refs_2_ = bf16[400,128]{1,0:T(8,128)(2,1)S(1)} collective-permute-done((bf16[400,128]{1,0:T(8,128)(2,1)S(1)}, bf16[400,128]{1,0:T(8,128)(2,1)S(1)}, u32[]{:S(2)}, u32[]{:S(2)}) %collective-permute-start.10) | collective-permute-done | bytes 102432 | tf_op jit(solution)/shard_map/ppermute | solution.py:45
  102.0 3.3 %collective-permute-start.15 = (bf16[400,128]{1,0:T(8,128)(2,1)S(1)}, bf16[400,128]{1,0:T(8,128)(2,1)S(1)}, u32[]{:S(2)}, u32[]{:S(2)}) collective-permute-start(bf16[400,128]{1,0:T(8,128)(2,1)S(1)} %get-tuple-element.59), channel_id=1, source_target_pairs={{0,30},{1,31},{2,24},{3,25},{4,26},{5,27},{6,28},{7,29},{8,6},{9,7... | collective-permute-start | bytes 307208 | tf_op jit(solution)/shard_map/ppermute | solution.py:45
  105.3 0.0 collective-permute-done.11.refs_3_
  105.3 0.0 collective-permute-start.16
  105.3 0.0 collective-permute-done.12.refs_4_
  105.3 4.1 %collective-permute-start.17 = (bf16[400,128]{1,0:T(8,128)(2,1)S(1)}, bf16[400,128]{1,0:T(8,128)(2,1)S(1)}, u32[]{:S(2)}, u32[]{:S(2)}) collective-permute-start(bf16[400,128]{1,0:T(8,128)(2,1)S(1)} %get-tuple-element.61), channel_id=1, source_target_pairs={{0,26},{1,27},{2,28},{3,29},{4,30},{5,31},{6,24},{7,25},{8,2},{9,3... | collective-permute-start | bytes 307208 | tf_op jit(solution)/shard_map/ppermute | solution.py:45
  109.4 0.0 collective-permute-done.13.refs_5_
  109.4 0.0 collective-permute-start.18
  109.4 0.0 collective-permute-done.14.refs_6_
  109.4 0.2 collective-permute-start.19
  109.6 0.0 collective-permute-done.15.refs_7_
  109.7 1.1 collective-permute-start.20
  110.8 2.1 %collective-permute-done.16.refs_8_ = bf16[400,128]{1,0:T(8,128)(2,1)S(1)} collective-permute-done((bf16[400,128]{1,0:T(8,128)(2,1)S(1)}, bf16[400,128]{1,0:T(8,128)(2,1)S(1)}, u32[]{:S(2)}, u32[]{:S(2)}) %collective-permute-start.16) | collective-permute-done | bytes 102432 | tf_op jit(solution)/shard_map/ppermute | solution.py:45
  112.8 0.0 collective-permute-start.21
  112.9 0.4 collective-permute-done.17.refs_9_
  113.2 5.7 %collective-permute-start.22 = (bf16[400,128]{1,0:T(8,128)(2,1)S(1)}, bf16[400,128]{1,0:T(8,128)(2,1)S(1)}, u32[]{:S(2)}, u32[]{:S(2)}) collective-permute-start(bf16[400,128]{1,0:T(8,128)(2,1)S(1)} %get-tuple-element.66), channel_id=1, source_target_pairs={{0,24},{1,25},{2,26},{3,27},{4,28},{5,29},{6,30},{7,31},{8,0},{9,1... | collective-permute-start | bytes 307208 | tf_op jit(solution)/shard_map/ppermute | solution.py:45
  118.9 0.0 collective-permute-done.18.refs_10_
  118.9 0.0 collective-permute-start.23
  118.9 1.1 collective-permute-start.9
  120.0 0.7 shard_map.121
  120.7 0.7 collective-permute-done.22.refs_14_
  121.4 2.1 %collective-permute-done.23.refs_15_ = bf16[400,128]{1,0:T(8,128)(2,1)S(1)} collective-permute-done((bf16[400,128]{1,0:T(8,128)(2,1)S(1)}, bf16[400,128]{1,0:T(8,128)(2,1)S(1)}, u32[]{:S(2)}, u32[]{:S(2)}) %collective-permute-start.23) | collective-permute-done | bytes 102432 | tf_op jit(solution)/shard_map/ppermute | solution.py:45
  123.5 4.0 %collective-permute-done.9.refs_1_ = bf16[400,128]{1,0:T(8,128)(2,1)S(1)} collective-permute-done((bf16[400,128]{1,0:T(8,128)(2,1)S(1)}, bf16[400,128]{1,0:T(8,128)(2,1)S(1)}, u32[]{:S(2)}, u32[]{:S(2)}) %collective-permute-start.9) | collective-permute-done | bytes 102432 | tf_op jit(solution)/shard_map/ppermute | solution.py:45
  127.5 1.0 shard_map.122
  (10 shorter events, 0.1 us)
Async XLA Ops:
  0.7 45.4 %copy-start.1 = (bf16[4096,512]{1,0:T(8,128)(2,1)S(1)}, bf16[4096,512]{1,0:T(8,128)(2,1)}, u32[]{:S(2)}) copy-start(bf16[4096,512]{1,0:T(8,128)(2,1)} %down_ref.1) | copy-start | bytes 12582916
  4.2 41.8 %copy-start = (bf16[512,4096]{1,0:T(8,128)(2,1)S(1)}, bf16[512,4096]{1,0:T(8,128)(2,1)}, u32[]{:S(2)}) copy-start(bf16[512,4096]{1,0:T(8,128)(2,1)} %up_ref.3) | copy-start | bytes 12582916
  4.3 41.8 %copy-start.2 = (f32[4096]{0:T(1024)S(1)}, f32[4096]{0:T(1024)}, u32[]{:S(2)}) copy-start(f32[4096]{0:T(1024)} %param.12) | copy-start | bytes 49156
  4.3 41.8 %copy-start.3 = (f32[4096]{0:T(1024)S(1)}, f32[4096]{0:T(1024)}, u32[]{:S(2)}) copy-start(f32[4096]{0:T(1024)} %param.11) | copy-start | bytes 49156
  45.9 2.0 %collective-permute-start = (bf16[2048,128]{1,0:T(8,128)(2,1)S(1)}, bf16[2048,128]{1,0:T(8,128)(2,1)S(1)}, u32[]{:S(2)}, u32[]{:S(2)}) collective-permute-start(bf16[2048,128]{1,0:T(8,128)(2,1)S(1)} %slice.4), channel_id=1, source_target_pairs={{0,1},{1,0},{2,3},{3,2},{4,5},{5,4},{6,7},{7,6},{8,9},{9,8},{10,11... | collective-permute-start | bytes 1572872 | tf_op jit(solution)/shard_map/ppermute | solution.py:45
  50.4 17.8 %copy-start.4 = (s32[128]{0:T(128)S(1)}, s32[128]{0:T(128)}, u32[]{:S(2)}) copy-start(s32[128]{0:T(128)} %param.13) | copy-start | bytes 1540
  50.4 11.0 %collective-permute-start.2 = (bf16[1040,128]{1,0:T(8,128)(2,1)S(1)}, bf16[1040,128]{1,0:T(8,128)(2,1)S(1)}, u32[]{:S(2)}, u32[]{:S(2)}) collective-permute-start(bf16[1040,128]{1,0:T(8,128)(2,1)S(1)} %get-tuple-element.42), channel_id=1, source_target_pairs={{0,32},{1,33},{2,34},{3,35},{4,36},{5,37},{6,38},{7,39},{8,40},{9,... | collective-permute-start | bytes 798728 | tf_op jit(solution)/shard_map/ppermute | solution.py:45
  52.4 14.1 %collective-permute-start.3 = (bf16[1040,128]{1,0:T(8,128)(2,1)S(1)}, bf16[1040,128]{1,0:T(8,128)(2,1)S(1)}, u32[]{:S(2)}, u32[]{:S(2)}) collective-permute-start(bf16[1040,128]{1,0:T(8,128)(2,1)S(1)} %get-tuple-element.43), channel_id=1, source_target_pairs={{0,96},{1,97},{2,98},{3,99},{4,100},{5,101},{6,102},{7,103},{8,104... | collective-permute-start | bytes 798728 | tf_op jit(solution)/shard_map/ppermute | solution.py:45
  54.6 13.6 %collective-permute-start.1 = (bf16[1040,128]{1,0:T(8,128)(2,1)S(1)}, bf16[1040,128]{1,0:T(8,128)(2,1)S(1)}, u32[]{:S(2)}, u32[]{:S(2)}) collective-permute-start(bf16[1040,128]{1,0:T(8,128)(2,1)S(1)} %get-tuple-element.41), channel_id=1, source_target_pairs={{0,64},{1,65},{2,66},{3,67},{4,68},{5,69},{6,70},{7,71},{8,72},{9,... | collective-permute-start | bytes 798728 | tf_op jit(solution)/shard_map/ppermute | solution.py:45
  68.5 10.8 %collective-permute-start.6 = (bf16[1040,128]{1,0:T(8,128)(2,1)S(1)}, bf16[1040,128]{1,0:T(8,128)(2,1)S(1)}, u32[]{:S(2)}, u32[]{:S(2)}) collective-permute-start(bf16[1040,128]{1,0:T(8,128)(2,1)S(1)} %shard_map.116.b0), channel_id=1, source_target_pairs={{0,64},{1,65},{2,66},{3,67},{4,68},{5,69},{6,70},{7,71},{8,72},{9,... | collective-permute-start | bytes 798728 | tf_op jit(solution)/shard_map/ppermute | solution.py:45
  69.0 13.8 %collective-permute-start.4 = (bf16[1040,128]{1,0:T(8,128)(2,1)S(1)}, bf16[1040,128]{1,0:T(8,128)(2,1)S(1)}, u32[]{:S(2)}, u32[]{:S(2)}) collective-permute-start(bf16[1040,128]{1,0:T(8,128)(2,1)S(1)} %shard_map.116.b0), channel_id=1, source_target_pairs={{0,96},{1,97},{2,98},{3,99},{4,100},{5,101},{6,102},{7,103},{8,104... | collective-permute-start | bytes 798728 | tf_op jit(solution)/shard_map/ppermute | solution.py:45
  72.4 11.1 %collective-permute-start.5 = (bf16[1040,128]{1,0:T(8,128)(2,1)S(1)}, bf16[1040,128]{1,0:T(8,128)(2,1)S(1)}, u32[]{:S(2)}, u32[]{:S(2)}) collective-permute-start(bf16[1040,128]{1,0:T(8,128)(2,1)S(1)} %shard_map.116.b0), channel_id=1, source_target_pairs={{0,32},{1,33},{2,34},{3,35},{4,36},{5,37},{6,38},{7,39},{8,40},{9,... | collective-permute-start | bytes 798728 | tf_op jit(solution)/shard_map/ppermute | solution.py:45
  85.0 3.9 %collective-permute-start.8 = (bf16[16,272,128]{2,1,0:T(8,128)(2,1)S(1)}, bf16[16,272,128]{2,1,0:T(8,128)(2,1)S(1)}, u32[]{:S(2)}, u32[]{:S(2)}) collective-permute-start(bf16[16,272,128]{2,1,0:T(8,128)(2,1)S(1)} %get-tuple-element.51), channel_id=1, source_target_pairs={{0,1},{1,0},{2,3},{3,2},{4,5},{5,4},{6,7},{7,6},{8,9},{9,8},{10,11... | collective-permute-start | bytes 3342344 | tf_op jit(solution)/shard_map/ppermute | solution.py:45
  86.7 2.1 %collective-permute-start.7 = (bf16[16,128,128]{2,1,0:T(8,128)(2,1)S(1)}, bf16[16,128,128]{2,1,0:T(8,128)(2,1)S(1)}, u32[]{:S(2)}, u32[]{:S(2)}) collective-permute-start(bf16[16,128,128]{2,1,0:T(8,128)(2,1)S(1)} %get-tuple-element.49), channel_id=1, source_target_pairs={{0,1},{1,0},{2,3},{3,2},{4,5},{5,4},{6,7},{7,6},{8,9},{9,8},{10,11... | collective-permute-start | bytes 1572872 | tf_op jit(solution)/shard_map/ppermute | solution.py:45
  89.8 12.2 %collective-permute-start.10 = (bf16[400,128]{1,0:T(8,128)(2,1)S(1)}, bf16[400,128]{1,0:T(8,128)(2,1)S(1)}, u32[]{:S(2)}, u32[]{:S(2)}) collective-permute-start(bf16[400,128]{1,0:T(8,128)(2,1)S(1)} %get-tuple-element.54), channel_id=1, source_target_pairs={{0,18},{1,19},{2,20},{3,21},{4,22},{5,23},{6,16},{7,17},{8,26},{9,... | collective-permute-start | bytes 307208 | tf_op jit(solution)/shard_map/ppermute | solution.py:45
  91.3 13.9 %collective-permute-start.11 = (bf16[400,128]{1,0:T(8,128)(2,1)S(1)}, bf16[400,128]{1,0:T(8,128)(2,1)S(1)}, u32[]{:S(2)}, u32[]{:S(2)}) collective-permute-start(bf16[400,128]{1,0:T(8,128)(2,1)S(1)} %get-tuple-element.55), channel_id=1, source_target_pairs={{0,12},{1,13},{2,14},{3,15},{4,8},{5,9},{6,10},{7,11},{8,20},{9,21... | collective-permute-start | bytes 307208 | tf_op jit(solution)/shard_map/ppermute | solution.py:45
  93.6 11.6 %collective-permute-start.12 = (bf16[400,128]{1,0:T(8,128)(2,1)S(1)}, bf16[400,128]{1,0:T(8,128)(2,1)S(1)}, u32[]{:S(2)}, u32[]{:S(2)}) collective-permute-start(bf16[400,128]{1,0:T(8,128)(2,1)S(1)} %get-tuple-element.56), channel_id=1, source_target_pairs={{0,22},{1,23},{2,16},{3,17},{4,18},{5,19},{6,20},{7,21},{8,30},{9,... | collective-permute-start | bytes 307208 | tf_op jit(solution)/shard_map/ppermute | solution.py:45
  96.7 12.7 %collective-permute-start.13 = (bf16[400,128]{1,0:T(8,128)(2,1)S(1)}, bf16[400,128]{1,0:T(8,128)(2,1)S(1)}, u32[]{:S(2)}, u32[]{:S(2)}) collective-permute-start(bf16[400,128]{1,0:T(8,128)(2,1)S(1)} %get-tuple-element.57), channel_id=1, source_target_pairs={{0,28},{1,29},{2,30},{3,31},{4,24},{5,25},{6,26},{7,27},{8,4},{9,5... | collective-permute-start | bytes 307208 | tf_op jit(solution)/shard_map/ppermute | solution.py:45
  99.9 9.5 %collective-permute-start.14 = (bf16[400,128]{1,0:T(8,128)(2,1)S(1)}, bf16[400,128]{1,0:T(8,128)(2,1)S(1)}, u32[]{:S(2)}, u32[]{:S(2)}) collective-permute-start(bf16[400,128]{1,0:T(8,128)(2,1)S(1)} %get-tuple-element.58), channel_id=1, source_target_pairs={{0,10},{1,11},{2,12},{3,13},{4,14},{5,15},{6,8},{7,9},{8,18},{9,19... | collective-permute-start | bytes 307208 | tf_op jit(solution)/shard_map/ppermute | solution.py:45
  102.0 7.6 %collective-permute-start.15 = (bf16[400,128]{1,0:T(8,128)(2,1)S(1)}, bf16[400,128]{1,0:T(8,128)(2,1)S(1)}, u32[]{:S(2)}, u32[]{:S(2)}) collective-permute-start(bf16[400,128]{1,0:T(8,128)(2,1)S(1)} %get-tuple-element.59), channel_id=1, source_target_pairs={{0,30},{1,31},{2,24},{3,25},{4,26},{5,27},{6,28},{7,29},{8,6},{9,7... | collective-permute-start | bytes 307208 | tf_op jit(solution)/shard_map/ppermute | solution.py:45
  105.3 7.6 %collective-permute-start.16 = (bf16[400,128]{1,0:T(8,128)(2,1)S(1)}, bf16[400,128]{1,0:T(8,128)(2,1)S(1)}, u32[]{:S(2)}, u32[]{:S(2)}) collective-permute-start(bf16[400,128]{1,0:T(8,128)(2,1)S(1)} %get-tuple-element.60), channel_id=1, source_target_pairs={{0,14},{1,15},{2,8},{3,9},{4,10},{5,11},{6,12},{7,13},{8,22},{9,23... | collective-permute-start | bytes 307208 | tf_op jit(solution)/shard_map/ppermute | solution.py:45
  105.3 7.9 %collective-permute-start.17 = (bf16[400,128]{1,0:T(8,128)(2,1)S(1)}, bf16[400,128]{1,0:T(8,128)(2,1)S(1)}, u32[]{:S(2)}, u32[]{:S(2)}) collective-permute-start(bf16[400,128]{1,0:T(8,128)(2,1)S(1)} %get-tuple-element.61), channel_id=1, source_target_pairs={{0,26},{1,27},{2,28},{3,29},{4,30},{5,31},{6,24},{7,25},{8,2},{9,3... | collective-permute-start | bytes 307208 | tf_op jit(solution)/shard_map/ppermute | solution.py:45
  109.4 9.5 %collective-permute-start.18 = (bf16[400,128]{1,0:T(8,128)(2,1)S(1)}, bf16[400,128]{1,0:T(8,128)(2,1)S(1)}, u32[]{:S(2)}, u32[]{:S(2)}) collective-permute-start(bf16[400,128]{1,0:T(8,128)(2,1)S(1)} %get-tuple-element.62), channel_id=1, source_target_pairs={{0,16},{1,17},{2,18},{3,19},{4,20},{5,21},{6,22},{7,23},{8,24},{9,... | collective-permute-start | bytes 307208 | tf_op jit(solution)/shard_map/ppermute | solution.py:45
  109.4 9.5 %collective-permute-start.19 = (bf16[400,128]{1,0:T(8,128)(2,1)S(1)}, bf16[400,128]{1,0:T(8,128)(2,1)S(1)}, u32[]{:S(2)}, u32[]{:S(2)}) collective-permute-start(bf16[400,128]{1,0:T(8,128)(2,1)S(1)} %get-tuple-element.63), channel_id=1, source_target_pairs={{0,4},{1,5},{2,6},{3,7},{4,0},{5,1},{6,2},{7,3},{8,12},{9,13},{10,... | collective-permute-start | bytes 307208 | tf_op jit(solution)/shard_map/ppermute | solution.py:45
  109.7 11.0 %collective-permute-start.20 = (bf16[400,128]{1,0:T(8,128)(2,1)S(1)}, bf16[400,128]{1,0:T(8,128)(2,1)S(1)}, u32[]{:S(2)}, u32[]{:S(2)}) collective-permute-start(bf16[400,128]{1,0:T(8,128)(2,1)S(1)} %get-tuple-element.64), channel_id=1, source_target_pairs={{0,8},{1,9},{2,10},{3,11},{4,12},{5,13},{6,14},{7,15},{8,16},{9,17... | collective-permute-start | bytes 307208 | tf_op jit(solution)/shard_map/ppermute | solution.py:45
  112.8 7.9 %collective-permute-start.21 = (bf16[400,128]{1,0:T(8,128)(2,1)S(1)}, bf16[400,128]{1,0:T(8,128)(2,1)S(1)}, u32[]{:S(2)}, u32[]{:S(2)}) collective-permute-start(bf16[400,128]{1,0:T(8,128)(2,1)S(1)} %get-tuple-element.65), channel_id=1, source_target_pairs={{0,2},{1,3},{2,4},{3,5},{4,6},{5,7},{6,0},{7,1},{8,10},{9,11},{10,... | collective-permute-start | bytes 307208 | tf_op jit(solution)/shard_map/ppermute | solution.py:45
  113.2 8.2 %collective-permute-start.22 = (bf16[400,128]{1,0:T(8,128)(2,1)S(1)}, bf16[400,128]{1,0:T(8,128)(2,1)S(1)}, u32[]{:S(2)}, u32[]{:S(2)}) collective-permute-start(bf16[400,128]{1,0:T(8,128)(2,1)S(1)} %get-tuple-element.66), channel_id=1, source_target_pairs={{0,24},{1,25},{2,26},{3,27},{4,28},{5,29},{6,30},{7,31},{8,0},{9,1... | collective-permute-start | bytes 307208 | tf_op jit(solution)/shard_map/ppermute | solution.py:45
  118.9 4.7 %collective-permute-start.23 = (bf16[400,128]{1,0:T(8,128)(2,1)S(1)}, bf16[400,128]{1,0:T(8,128)(2,1)S(1)}, u32[]{:S(2)}, u32[]{:S(2)}) collective-permute-start(bf16[400,128]{1,0:T(8,128)(2,1)S(1)} %get-tuple-element.67), channel_id=1, source_target_pairs={{0,6},{1,7},{2,0},{3,1},{4,2},{5,3},{6,4},{7,5},{8,14},{9,15},{10,... | collective-permute-start | bytes 307208 | tf_op jit(solution)/shard_map/ppermute | solution.py:45
  118.9 8.6 %collective-permute-start.9 = (bf16[400,128]{1,0:T(8,128)(2,1)S(1)}, bf16[400,128]{1,0:T(8,128)(2,1)S(1)}, u32[]{:S(2)}, u32[]{:S(2)}) collective-permute-start(bf16[400,128]{1,0:T(8,128)(2,1)S(1)} %get-tuple-element.53), channel_id=1, source_target_pairs={{0,20},{1,21},{2,22},{3,23},{4,16},{5,17},{6,18},{7,19},{8,28},{9,... | collective-permute-start | bytes 307208 | tf_op jit(solution)/shard_map/ppermute | solution.py:45

commit v5 on v3

--- a/solution.py
+++ b/solution.py
@@ -21,7 +21,8 @@
 EXT = 16
 PACK = 400
 HALF = EMBED // 2
-ORDER = (0, 2, 1, 3)
+EARLY = SAMPLES - OWN
+ORDER = (0, 1, 3, 2)
 F32 = jnp.float32
 BF16 = jnp.bfloat16
 
@@ -71,29 +72,30 @@
 
 
 def pack_counts(place, counts_t, slab):
-    group = 16
+    strip = NK * OWN
 
     def body(place_ref, counts_ref, slab_ref, out, held, slab_s, sems, slab_sem):
-        def copy(n):
-            rows = pl.ds(n * group, group)
-            return pltpu.make_async_copy(counts_ref.at[rows, :], held.at[rows, :], sems.at[n])
-
-        for n in range(ROWS // group):
-            copy(n).start()
+        def copy(y, n):
+            z = lax.rem(place_ref[0] + ORDER[n], NZ)
+            start = pl.multiple_of(z * (NY * strip) + y * strip, strip)
+            return pltpu.make_async_copy(counts_ref.at[:, pl.ds(start, strip)], held.at[y, n], sems.at[y, n])
+
         slab_copy = pltpu.make_async_copy(slab_ref, slab_s, slab_sem)
         slab_copy.start()
+        for y in range(NY):
+            for n in range(NZ):
+                copy(y, n).start()
         slab_copy.wait()
         for k in range(PEERS):
             half = k % NC
             out[k, :, SAMPLES:] = slab_s[:, half * HALF : (half + 1) * HALF]
-        starts = [lax.rem(place_ref[0] + z, NZ) * (PEERS * OWN) for z in ORDER]
-        for n in range(ROWS // group):
-            copy(n).wait()
-            rows = slice(n * group, (n + 1) * group)
-            for i, start in enumerate(starts):
-                for k in range(PEERS):
-                    at = pl.ds(pl.multiple_of(start + k * OWN, OWN), OWN)
-                    out[k, rows, i * OWN : (i + 1) * OWN] = held[rows, at].astype(F32).astype(BF16)
+        for y in range(NY):
+            for n in range(NZ):
+                copy(y, n).wait()
+                for k in range(NK):
+                    out[y * NK + k, :, n * OWN : (n + 1) * OWN] = (
+                        held[y, n, :, k * OWN : (k + 1) * OWN].astype(F32).astype(BF16)
+                    )
 
     return call(
         body,
@@ -101,9 +103,9 @@
         (place, far(counts_t), far(slab)),
         [IN_SMEM, IN_HBM, IN_HBM],
         [
-            pltpu.VMEM((ROWS, NZ * PEERS * OWN), jnp.int32),
+            pltpu.VMEM((NY, NZ, ROWS, strip), jnp.int32),
             pltpu.VMEM((ROWS, EMBED), BF16),
-            pltpu.SemaphoreType.DMA((ROWS // group,)),
+            pltpu.SemaphoreType.DMA((NY, NZ)),
             pltpu.SemaphoreType.DMA,
         ],
     )[0]
@@ -189,8 +191,8 @@
         out[2 * RANK :, :] = ext[:, i * OWN : (i + 1) * OWN]
 
 
-def forward_far(place, arrived, other, half, rows):
-    def body(place_ref, in_ref, other_ref, half_ref, rows_ref, pooled_ref, out):
+def forward_near(place, arrived, other, half, rows):
+    def body(place_ref, in_ref, other_ref, half_ref, rows_ref, pooled_ref, *outs):
         core = place_ref[3]
         for y in range(NY):
             at = slice(y * 512, (y + 1) * 512)
@@ -200,27 +202,27 @@
             pooled_ref[pl.ds(partners, HALF), :] = dot(
                 other_ref[at, :].T, in_ref[at, :SAMPLES], 1, 0
             ).astype(BF16)
-        products(rows_ref, pooled_ref[:, OWN : 2 * OWN], (out,))
-
-    return call(
-        body,
-        [pltpu.VMEM((COLS, SAMPLES), BF16), pltpu.VMEM((2 * RANK + EXT, OWN), BF16)],
+        products(rows_ref, pooled_ref[:, OWN:EARLY], outs)
+
+    return call(
+        body,
+        [pltpu.VMEM((COLS, SAMPLES), BF16)] + [pltpu.VMEM((2 * RANK + EXT, OWN), BF16)] * 2,
         (place, near(arrived), near(other), near(half), near(rows)),
         [IN_SMEM] + [IN_VMEM] * 4,
         cost=pl.CostEstimate(flops=3 << 30, bytes_accessed=4 << 20, transcendentals=0),
     )
 
 
-def forward_near(pooled, rows):
+def forward_far(pooled, rows):
     def body(pooled_ref, rows_ref, *outs):
-        products(rows_ref, pooled_ref[:, 2 * OWN :], outs)
-
-    return call(
-        body,
-        [pltpu.VMEM((2 * RANK + EXT, OWN), BF16)] * 2,
+        products(rows_ref, pooled_ref[:, EARLY:], outs)
+
+    return call(
+        body,
+        [pltpu.VMEM((2 * RANK + EXT, OWN), BF16)],
         (near(pooled), near(rows)),
         cost=pl.CostEstimate(flops=1 << 30, bytes_accessed=2 << 20, transcendentals=0),
-    )
+    )[0]
 
 
 def forward_own(pooled, rows):
@@ -253,9 +255,7 @@
         rows = jnp.where((at == 0) | (at == 2), high, jnp.where(at == 1, g - high, 0.0))
         out[2 * RANK :, :] = rows.astype(BF16)
 
-    return call(
-        body, [pltpu.VMEM((2 * RANK + EXT, OWN), BF16)], (*(near(p) for p in parts), labels)
-    )[0]
+    return call(body, [pltpu.VMEM((2 * RANK + EXT, OWN), BF16)], (*(near(p) for p in parts), labels))[0]
 
 
 def by_sample(*blocks):
@@ -267,19 +267,19 @@
     return [dot(g, rows_ref[:, table], 1, 0).astype(BF16) for table in tables]
 
 
-def backward_first(block0, block2, pooled, arrived, rows):
-    def body(b0, b2, pooled_ref, in_ref, rows_ref, both_out, sums_out, slab_out):
-        g = by_sample(b0, b2)
+def backward_first(block0, block1, block3, pooled, arrived, rows):
+    def body(b0, b1, b3, pooled_ref, in_ref, rows_ref, both_out, sums_out, slab_out):
+        g = by_sample(b0, b1, b3)
         products = grad_pooled_of(g, rows_ref)
-        pooled = pooled_ref[:, : 2 * OWN]
+        pooled = pooled_ref[:, :EARLY]
         for j in range(4):
             at = slice(j * 256, (j + 1) * 256)
             both_out[:, at] = dot(pooled, g[:, at], 1, 0)
-        ext = jnp.concatenate([b0[2 * RANK :, :], b2[2 * RANK :, :]], axis=1)
+        ext = jnp.concatenate([b[2 * RANK :, :] for b in (b0, b1, b3)], axis=1)
         sums_out[...] = dot(ext, pooled, 1, 1)
         for y, grad_pooled in enumerate(products):
             at = slice(y * 512, (y + 1) * 512)
-            slab_out[at, :] = dot(in_ref[at, : 2 * OWN], grad_pooled, 1, 0)
+            slab_out[at, :] = dot(in_ref[at, :EARLY], grad_pooled, 1, 0)
 
     return call(
         body,
@@ -288,7 +288,7 @@
             pltpu.VMEM((EXT, COLS), F32),
             pltpu.VMEM((PEERS * ROWS, EMBED), F32),
         ],
-        tuple(near(v) for v in (block0, block2, pooled, arrived, rows)),
+        tuple(near(v) for v in (block0, block1, block3, pooled, arrived, rows)),
         cost=pl.CostEstimate(flops=2 << 30, bytes_accessed=6 << 20, transcendentals=0),
     )
 
@@ -303,12 +303,12 @@
 EVERYONE = slice(0, NY * NX)
 
 
-def backward_weights(place, block1, block3, pooled, both, sums):
-    def body(place_ref, b1, b3, pooled_ref, both_ref, sums_ref, mine, other, g_out):
+def backward_weights(place, block2, pooled, both, sums):
+    def body(place_ref, b2, pooled_ref, both_ref, sums_ref, mine, other, g_out):
         low_core = place_ref[3] == 0
-        g = by_sample(b1, b3)
+        g = by_sample(b2)
         g_out[...] = g
-        pooled = pooled_ref[:, 2 * OWN :]
+        pooled = pooled_ref[:, EARLY:]
         for j in range(4):
             value = dot(pooled, g[:, j * 256 : (j + 1) * 256], 1, 0)
             for h in range(2):
@@ -316,8 +316,7 @@
                 held = both_ref[:, at : at + 128] + value[:, h * 128 : (h + 1) * 128]
                 to = slice((2 * j + h) * 32, (2 * j + h + 1) * 32)
                 put(low_core, mine, other, EVERYONE, to, held.reshape(PEERS, 32, 128))
-        ext = jnp.concatenate([b1[2 * RANK :, :], b3[2 * RANK :, :]], axis=1)
-        held = (dot(ext, pooled, 1, 1) + sums_ref[...]).astype(BF16)
+        held = (dot(b2[2 * RANK :, :], pooled, 1, 1) + sums_ref[...]).astype(BF16)
         for strip in range(8):
             row = held[:, strip * 128 : (strip + 1) * 128]
             for i in range(2):
@@ -326,9 +325,9 @@
 
     return call(
         body,
-        [pltpu.VMEM((NY * NX, 272, 128), BF16)] * 2 + [pltpu.VMEM((2 * OWN, 2 * RANK + EXT), BF16)],
-        (place, *(near(v) for v in (block1, block3, pooled, both, sums))),
-        [IN_SMEM] + [IN_VMEM] * 5,
+        [pltpu.VMEM((NY * NX, 272, 128), BF16)] * 2 + [pltpu.VMEM((OWN, 2 * RANK + EXT), BF16)],
+        (place, *(near(v) for v in (block2, pooled, both, sums))),
+        [IN_SMEM] + [IN_VMEM] * 4,
         cost=pl.CostEstimate(flops=1 << 30, bytes_accessed=4 << 20, transcendentals=0),
     )
 
@@ -338,7 +337,7 @@
         low_core = place_ref[3] == 0
         for y, grad_pooled in enumerate(grad_pooled_of(g_ref[...], rows_ref)):
             at = slice(y * 512, (y + 1) * 512)
-            slab = first_ref[at, :] + dot(in_ref[at, 2 * OWN : SAMPLES], grad_pooled, 1, 0)
+            slab = first_ref[at, :] + dot(in_ref[at, EARLY:SAMPLES], grad_pooled, 1, 0)
             for j in range(2):
                 put(
                     low_core,
@@ -417,20 +416,20 @@
     arrived = lax.all_to_all(sent, PLANE, 0, 0, tiled=True).reshape(PEERS * ROWS, SAMPLES + HALF)
     other = shift(arrived[:, SAMPLES:], dc=1)
     half = pool_half(arrived)
-    pooled, chunk2 = forward_far(place, arrived, other, half, rows)
-    part2 = shift(chunk2, dz=2)
-    chunk1, chunk3 = forward_near(pooled, rows)
+    pooled, chunk1, chunk3 = forward_near(place, arrived, other, half, rows)
     part1 = shift(chunk1, dz=1)
     part3 = shift(chunk3, dz=3)
-    parts = [part2, part1, part3]
+    chunk2 = forward_far(pooled, rows)
+    part2 = shift(chunk2, dz=2)
+    parts = [part1, part3, part2]
     chunk = forward_own(pooled, rows)
     block0 = own_samples([chunk] + parts, labels.reshape(1, OWN))
     blocks = []
     for i in ORDER[1:]:
         blocks.append(shift(block0, dz=-i))
-    block2, block1, block3 = blocks
-    both, sums, slab_first = backward_first(block0, block2, pooled, arrived, rows)
-    weights, given, g = backward_weights(place, block1, block3, pooled, both, sums)
+    block1, block3, block2 = blocks
+    both, sums, slab_first = backward_first(block0, block1, block3, pooled, arrived, rows)
+    weights, given, g = backward_weights(place, block2, pooled, both, sums)
     weights_partner = shift(given, dc=1)
     slabs, given = backward_slab(place, g, arrived, rows, slab_first)
     paired = pair_sums(slabs, shift(given, dc=1), weights, weights_partner)

time: 124 us -> 128 us (1.032)
  waiting for transfers between devices: 47.3 us -> 49.6 us
  starting transfers between devices: 14.4 us -> 16 us
    ppermute x9, waiting for transfers between devices: 22.1 us -> 24.4 us  [shift(): return lax.ppermute(value, ALL, pairs)]
    ppermute x9, starting transfers between devices: 10.7 us -> 12.3 us  [shift(): return lax.ppermute(value, ALL, pairs)]
  transfers between devices with their start and end apart: 10 -> 10, of which waited for: 9 -> 8; matrix products, arithmetic and copies ran while one was open for 0% -> 0% of each run, Pallas kernels for 5% -> 6%
where the time goes in v5:
time: 128 us
  waiting for transfers between devices  49.6 us (39%)
  blocking collectives  41.6 us (32%)
  Pallas kernels  17.4 us (14%)
  starting transfers between devices  16 us (12%)
  local copies, waits for them, and re-layouts  2.24 us (2%)
    all_to_all x1, blocking collectives, local(): lax.all_to_all(sent, PLANE, 0, 0, tiled=True)  41.6 us
    all_to_all x1, waiting for transfers between devices, local(): shares = lax.all_to_all(paired, ('y', 'x'), 0, 0, tiled=True)  25.2 us
    ppermute x9, waiting for transfers between devices, shift(): return lax.ppermute(value, ALL, pairs)  24.4 us
    pallas_call x13, Pallas kernels, call(): pl.pallas_call(body, in_specs=specs or [pl.BlockSpec(memory_space=pltpu.V...  17.4 us
    ppermute x9, starting transfers between devices, shift(): return lax.ppermute(value, ALL, pairs)  12.3 us
    all_to_all x1, starting transfers between devices, local(): shares = lax.all_to_all(paired, ('y', 'x'), 0, 0, tiled=True)  3.71 us
  transfers between devices with their start and end apart: 10, of which 8 were waited for; matrix products, arithmetic and copies ran while one was open for 0% of the time, Pallas kernels for 6%

profile of v5, /device:TPU:0, one launch (start us, length us, event | category | flops | bytes accessed | tf_op | source)
XLA Modules:
  0.0 127.7 jit_solution(7523022886165410187)
XLA Ops:
  0.6 0.1 pad_add_fusion.place_ref
  0.7 0.0 copy-start.2
  0.7 3.3 %shard_map.110 = bf16[32,64,640]{2,1,0:T(8,128)(2,1)S(1)} custom-call(s32[4]{0:T(128)S(1)} %pad_add_fusion.place_ref, s32[64,16384]{1,0:T(8,128)} %bitcast.22, bf16[64,256]{1,0:T(8,128)(2,1)} %slab_ref.1), custom_call_target="tpu_custom_call" | custom-call | tf_op jit(solution)/shard_map/pallas_call | solution.py:58
  4.0 0.0 copy-start
  4.1 0.0 copy-start.3
  4.1 0.0 copy-start.4
  4.1 41.6 %all_to_all.10 = bf16[32,64,640]{2,1,0:T(8,128)(2,1)S(1)} all-to-all(bf16[32,64,640]{2,1,0:T(8,128)(2,1)S(1)} %shard_map.110), channel_id=1, replica_groups=mesh['z'=4,'y'=4,'x'=4,'c'=2] {'y','x','c'}, dimensions={0} | all-to-all | bytes 5242880 | tf_op jit(solution)/shard_map/all_to_all | solution.py:416
  45.7 0.2 collective-permute-start
  45.9 0.0 copy-done.2
  45.9 0.0 copy-done
  45.9 0.0 copy-done.3
  45.9 0.0 copy-done.4
  45.9 1.2 shard_map.112.rows_ref
  47.1 0.5 shard_map.111.half_ref
  47.5 0.1 collective-permute-done.other_ref
  47.7 1.8 %shard_map.113 = (bf16[1024,512]{1,0:T(8,128)(2,1)S(1)}, bf16[1040,128]{1,0:T(8,128)(2,1)S(1)}, bf16[1040,128]{1,0:T(8,128)(2,1)S(1)}) custom-call(s32[4]{0:T(128)S(1)} %pad_add_fusion.place_ref, bf16[2048,640]{1,0:T(8,128)(2,1)S(1)} %bitcast.14, bf16[2048,128]{1,0:T(8,128)(2,1)S(1)} %collective-permute-done.other_ref, ...), custom_call_target="tpu_custom_call" | custom-call | flops 3221225472 | bytes 4194304 | tf_op jit(solution)/shard_map/pallas_call | solution.py:58
  49.5 0.7 shard_map.115
  50.2 0.0 copy-start.5
  50.2 4.0 %collective-permute-start.3 = (bf16[1040,128]{1,0:T(8,128)(2,1)S(1)}, bf16[1040,128]{1,0:T(8,128)(2,1)S(1)}, u32[]{:S(2)}, u32[]{:S(2)}) collective-permute-start(bf16[1040,128]{1,0:T(8,128)(2,1)S(1)} %shard_map.115), channel_id=1, source_target_pairs={{0,64},{1,65},{2,66},{3,67},{4,68},{5,69},{6,70},{7,71},{8,72},{9,... | collective-permute-start | bytes 798728 | tf_op jit(solution)/shard_map/ppermute | solution.py:46
  54.2 1.0 collective-permute-start.1
  55.2 2.2 %collective-permute-start.2 = (bf16[1040,128]{1,0:T(8,128)(2,1)S(1)}, bf16[1040,128]{1,0:T(8,128)(2,1)S(1)}, u32[]{:S(2)}, u32[]{:S(2)}) collective-permute-start(bf16[1040,128]{1,0:T(8,128)(2,1)S(1)} %get-tuple-element.25), channel_id=1, source_target_pairs={{0,96},{1,97},{2,98},{3,99},{4,100},{5,101},{6,102},{7,103},{8,104... | collective-permute-start | bytes 798728 | tf_op jit(solution)/shard_map/ppermute | solution.py:46
  57.4 0.7 shard_map.114.p0
  58.1 3.3 %collective-permute-done.3.p3 = bf16[1040,128]{1,0:T(8,128)(2,1)S(1)} collective-permute-done((bf16[1040,128]{1,0:T(8,128)(2,1)S(1)}, bf16[1040,128]{1,0:T(8,128)(2,1)S(1)}, u32[]{:S(2)}, u32[]{:S(2)}) %collective-permute-start.3) | collective-permute-done | bytes 266272 | tf_op jit(solution)/shard_map/ppermute | solution.py:46
  61.5 5.2 %collective-permute-done.1.p1 = bf16[1040,128]{1,0:T(8,128)(2,1)S(1)} collective-permute-done((bf16[1040,128]{1,0:T(8,128)(2,1)S(1)}, bf16[1040,128]{1,0:T(8,128)(2,1)S(1)}, u32[]{:S(2)}, u32[]{:S(2)}) %collective-permute-start.1) | collective-permute-done | bytes 266272 | tf_op jit(solution)/shard_map/ppermute | solution.py:46
  66.7 0.8 collective-permute-done.2.p2
  67.5 0.0 copy-done.5
  67.5 0.3 shard_map.116.b0
  67.8 2.7 %collective-permute-start.5 = (bf16[1040,128]{1,0:T(8,128)(2,1)S(1)}, bf16[1040,128]{1,0:T(8,128)(2,1)S(1)}, u32[]{:S(2)}, u32[]{:S(2)}) collective-permute-start(bf16[1040,128]{1,0:T(8,128)(2,1)S(1)} %shard_map.116.b0), channel_id=1, source_target_pairs={{0,96},{1,97},{2,98},{3,99},{4,100},{5,101},{6,102},{7,103},{8,104... | collective-permute-start | bytes 798728 | tf_op jit(solution)/shard_map/ppermute | solution.py:46
  70.5 0.0 collective-permute-start.6
  70.5 1.5 %collective-permute-start.4 = (bf16[1040,128]{1,0:T(8,128)(2,1)S(1)}, bf16[1040,128]{1,0:T(8,128)(2,1)S(1)}, u32[]{:S(2)}, u32[]{:S(2)}) collective-permute-start(bf16[1040,128]{1,0:T(8,128)(2,1)S(1)} %shard_map.116.b0), channel_id=1, source_target_pairs={{0,64},{1,65},{2,66},{3,67},{4,68},{5,69},{6,70},{7,71},{8,72},{9,... | collective-permute-start | bytes 798728 | tf_op jit(solution)/shard_map/ppermute | solution.py:46
  72.0 10.0 %collective-permute-done.5.b1 = bf16[1040,128]{1,0:T(8,128)(2,1)S(1)} collective-permute-done((bf16[1040,128]{1,0:T(8,128)(2,1)S(1)}, bf16[1040,128]{1,0:T(8,128)(2,1)S(1)}, u32[]{:S(2)}, u32[]{:S(2)}) %collective-permute-start.5) | collective-permute-done | bytes 266272 | tf_op jit(solution)/shard_map/ppermute | solution.py:46
  82.0 3.4 %collective-permute-done.6.b3 = bf16[1040,128]{1,0:T(8,128)(2,1)S(1)} collective-permute-done((bf16[1040,128]{1,0:T(8,128)(2,1)S(1)}, bf16[1040,128]{1,0:T(8,128)(2,1)S(1)}, u32[]{:S(2)}, u32[]{:S(2)}) %collective-permute-start.6) | collective-permute-done | bytes 266272 | tf_op jit(solution)/shard_map/ppermute | solution.py:46
  85.4 3.1 %shard_map.117 = (f32[1024,1024]{1,0:T(8,128)S(1)}, f32[16,1024]{1,0:T(8,128)S(1)}, f32[2048,256]{1,0:T(8,128)S(1)}) custom-call(bf16[1040,128]{1,0:T(8,128)(2,1)S(1)} %shard_map.116.b0, bf16[1040,128]{1,0:T(8,128)(2,1)S(1)} %collective-permute-done.5.b1, bf16[1040,128]{1,0:T(8,128)(2,1)S(1)} %collective-permute-done.6.b3, ...), custom_call_target="tpu_custom_call" | custom-call | flops 2147483648 | bytes 6291456 | tf_op jit(solution)/shard_map/pallas_call | solution.py:58
  88.5 0.0 collective-permute-done.4.b2
  88.5 1.3 %shard_map.118 = (bf16[16,272,128]{2,1,0:T(8,128)(2,1)S(1)}, bf16[16,272,128]{2,1,0:T(8,128)(2,1)S(1)}, bf16[128,1040]{1,0:T(8,128)(2,1)S(1)}) custom-call(s32[4]{0:T(128)S(1)} %pad_add_fusion.place_ref, bf16[1040,128]{1,0:T(8,128)(2,1)S(1)} %collective-permute-done.4.b2, bf16[1024,512]{1,0:T(8,128)(2,1)S(1)} %get-tuple-element.23.pooled_ref, ...), custom_call_target="tpu_custom_call" | custom-call | flops 1073741824 | bytes 4194304 | tf_op jit(solution)/shard_map/pallas_call | solution.py:58
  89.8 0.1 collective-permute-start.8
  89.9 1.3 %shard_map.119 = (bf16[16,128,128]{2,1,0:T(8,128)(2,1)S(1)}, bf16[16,128,128]{2,1,0:T(8,128)(2,1)S(1)}) custom-call(s32[4]{0:T(128)S(1)} %pad_add_fusion.place_ref, bf16[128,1040]{1,0:T(8,128)(2,1)S(1)} %get-tuple-element.28.g_ref, bf16[2048,640]{1,0:T(8,128)(2,1)S(1)} %bitcast.16, bf16[1040,1024]{1,0:T(8,128)(2,1)S(1)} %shard_map.112.rows_ref, ...), custom_call_target="tpu_custom_call" | custom-call | flops 1073741824 | bytes 4194304 | tf_op jit(solution)/shard_map/pallas_call | solution.py:58
  91.3 0.6 collective-permute-start.7
  91.9 1.5 %collective-permute-done.7.b = bf16[16,128,128]{2,1,0:T(8,128)(2,1)S(1)} collective-permute-done((bf16[16,128,128]{2,1,0:T(8,128)(2,1)S(1)}, bf16[16,128,128]{2,1,0:T(8,128)(2,1)S(1)}, u32[]{:S(2)}, u32[]{:S(2)}) %collective-permute-start.7) | collective-permute-done | bytes 524320 | tf_op jit(solution)/shard_map/ppermute | solution.py:46
  93.4 0.0 collective-permute-done.8.d
  93.4 1.6 %shard_map.120 = bf16[16,400,128]{2,1,0:T(8,128)(2,1)} custom-call(bf16[16,128,128]{2,1,0:T(8,128)(2,1)S(1)} %get-tuple-element.30.a, bf16[16,128,128]{2,1,0:T(8,128)(2,1)S(1)} %collective-permute-done.7.b, bf16[16,272,128]{2,1,0:T(8,128)(2,1)S(1)} %get-tuple-element.32.c, bf16[16,272,128]{2,1,0:T(8,128)(2,1)S(1)} %collective-permute-done.8.d), custom_call_target="tpu_custom_call" | custom-call | tf_op jit(solution)/shard_map/pallas_call | solution.py:58
  95.0 3.7 %all-to-all-start.1 = ((bf16[16,400,128]{2,1,0:T(8,128)(2,1)}), bf16[16,400,128]{2,1,0:T(8,128)(2,1)S(1)}, u32[]{:S(2)}, u32[]{:S(2)}) async-start(bf16[16,400,128]{2,1,0:T(8,128)(2,1)} %shard_map.120), calls=%async_computation.1 | async-start | bytes 3276800 | tf_op jit(solution)/shard_map/all_to_all | solution.py:436
  98.7 0.0 copy-start.1
  98.7 2.2 %copy-done.1 = bf16[512,4096]{1,0:T(8,128)(2,1)S(1)} copy-done((bf16[512,4096]{1,0:T(8,128)(2,1)S(1)}, bf16[512,4096]{1,0:T(8,128)(2,1)}, u32[]{:S(2)}) %copy-start.1) | copy-done | bytes 4194328
  100.9 0.7 shard_map.121
  101.6 25.2 %all-to-all-done.1.in_ref = bf16[16,400,128]{2,1,0:T(8,128)(2,1)S(1)} async-done(((bf16[16,400,128]{2,1,0:T(8,128)(2,1)}), bf16[16,400,128]{2,1,0:T(8,128)(2,1)S(1)}, u32[]{:S(2)}, u32[]{:S(2)}) %all-to-all-start.1) | async-done | bytes 1638432 | tf_op jit(solution)/shard_map/all_to_all | solution.py:436
  126.8 0.9 shard_map.122
  (1 shorter events, 0.0 us)
Async XLA Ops:
  0.7 45.2 %copy-start.2 = (bf16[4096,512]{1,0:T(8,128)(2,1)S(1)}, bf16[4096,512]{1,0:T(8,128)(2,1)}, u32[]{:S(2)}) copy-start(bf16[4096,512]{1,0:T(8,128)(2,1)} %down_ref.1) | copy-start | bytes 12582916
  4.0 41.8 %copy-start = (bf16[512,4096]{1,0:T(8,128)(2,1)S(1)}, bf16[512,4096]{1,0:T(8,128)(2,1)}, u32[]{:S(2)}) copy-start(bf16[512,4096]{1,0:T(8,128)(2,1)} %up_ref.3) | copy-start | bytes 12582916
  4.1 41.8 %copy-start.3 = (f32[4096]{0:T(1024)S(1)}, f32[4096]{0:T(1024)}, u32[]{:S(2)}) copy-start(f32[4096]{0:T(1024)} %param.12) | copy-start | bytes 49156
  4.1 41.8 %copy-start.4 = (f32[4096]{0:T(1024)S(1)}, f32[4096]{0:T(1024)}, u32[]{:S(2)}) copy-start(f32[4096]{0:T(1024)} %param.11) | copy-start | bytes 49156
  45.7 2.0 %collective-permute-start = (bf16[2048,128]{1,0:T(8,128)(2,1)S(1)}, bf16[2048,128]{1,0:T(8,128)(2,1)S(1)}, u32[]{:S(2)}, u32[]{:S(2)}) collective-permute-start(bf16[2048,128]{1,0:T(8,128)(2,1)S(1)} %slice.4), channel_id=1, source_target_pairs={{0,1},{1,0},{2,3},{3,2},{4,5},{5,4},{6,7},{7,6},{8,9},{9,8},{10,11... | collective-permute-start | bytes 1572872 | tf_op jit(solution)/shard_map/ppermute | solution.py:46
  50.2 17.3 %copy-start.5 = (s32[128]{0:T(128)S(1)}, s32[128]{0:T(128)}, u32[]{:S(2)}) copy-start(s32[128]{0:T(128)} %param.13) | copy-start | bytes 1540
  50.2 11.2 %collective-permute-start.3 = (bf16[1040,128]{1,0:T(8,128)(2,1)S(1)}, bf16[1040,128]{1,0:T(8,128)(2,1)S(1)}, u32[]{:S(2)}, u32[]{:S(2)}) collective-permute-start(bf16[1040,128]{1,0:T(8,128)(2,1)S(1)} %shard_map.115), channel_id=1, source_target_pairs={{0,64},{1,65},{2,66},{3,67},{4,68},{5,69},{6,70},{7,71},{8,72},{9,... | collective-permute-start | bytes 798728 | tf_op jit(solution)/shard_map/ppermute | solution.py:46
  54.2 12.5 %collective-permute-start.1 = (bf16[1040,128]{1,0:T(8,128)(2,1)S(1)}, bf16[1040,128]{1,0:T(8,128)(2,1)S(1)}, u32[]{:S(2)}, u32[]{:S(2)}) collective-permute-start(bf16[1040,128]{1,0:T(8,128)(2,1)S(1)} %get-tuple-element.24), channel_id=1, source_target_pairs={{0,32},{1,33},{2,34},{3,35},{4,36},{5,37},{6,38},{7,39},{8,40},{9,... | collective-permute-start | bytes 798728 | tf_op jit(solution)/shard_map/ppermute | solution.py:46
  55.2 12.3 %collective-permute-start.2 = (bf16[1040,128]{1,0:T(8,128)(2,1)S(1)}, bf16[1040,128]{1,0:T(8,128)(2,1)S(1)}, u32[]{:S(2)}, u32[]{:S(2)}) collective-permute-start(bf16[1040,128]{1,0:T(8,128)(2,1)S(1)} %get-tuple-element.25), channel_id=1, source_target_pairs={{0,96},{1,97},{2,98},{3,99},{4,100},{5,101},{6,102},{7,103},{8,104... | collective-permute-start | bytes 798728 | tf_op jit(solution)/shard_map/ppermute | solution.py:46
  67.8 14.2 %collective-permute-start.5 = (bf16[1040,128]{1,0:T(8,128)(2,1)S(1)}, bf16[1040,128]{1,0:T(8,128)(2,1)S(1)}, u32[]{:S(2)}, u32[]{:S(2)}) collective-permute-start(bf16[1040,128]{1,0:T(8,128)(2,1)S(1)} %shard_map.116.b0), channel_id=1, source_target_pairs={{0,96},{1,97},{2,98},{3,99},{4,100},{5,101},{6,102},{7,103},{8,104... | collective-permute-start | bytes 798728 | tf_op jit(solution)/shard_map/ppermute | solution.py:46
  70.5 15.0 %collective-permute-start.6 = (bf16[1040,128]{1,0:T(8,128)(2,1)S(1)}, bf16[1040,128]{1,0:T(8,128)(2,1)S(1)}, u32[]{:S(2)}, u32[]{:S(2)}) collective-permute-start(bf16[1040,128]{1,0:T(8,128)(2,1)S(1)} %shard_map.116.b0), channel_id=1, source_target_pairs={{0,32},{1,33},{2,34},{3,35},{4,36},{5,37},{6,38},{7,39},{8,40},{9,... | collective-permute-start | bytes 798728 | tf_op jit(solution)/shard_map/ppermute | solution.py:46
  70.5 18.0 %collective-permute-start.4 = (bf16[1040,128]{1,0:T(8,128)(2,1)S(1)}, bf16[1040,128]{1,0:T(8,128)(2,1)S(1)}, u32[]{:S(2)}, u32[]{:S(2)}) collective-permute-start(bf16[1040,128]{1,0:T(8,128)(2,1)S(1)} %shard_map.116.b0), channel_id=1, source_target_pairs={{0,64},{1,65},{2,66},{3,67},{4,68},{5,69},{6,70},{7,71},{8,72},{9,... | collective-permute-start | bytes 798728 | tf_op jit(solution)/shard_map/ppermute | solution.py:46
  89.8 3.6 %collective-permute-start.8 = (bf16[16,272,128]{2,1,0:T(8,128)(2,1)S(1)}, bf16[16,272,128]{2,1,0:T(8,128)(2,1)S(1)}, u32[]{:S(2)}, u32[]{:S(2)}) collective-permute-start(bf16[16,272,128]{2,1,0:T(8,128)(2,1)S(1)} %get-tuple-element.33), channel_id=1, source_target_pairs={{0,1},{1,0},{2,3},{3,2},{4,5},{5,4},{6,7},{7,6},{8,9},{9,8},{10,11... | collective-permute-start | bytes 3342344 | tf_op jit(solution)/shard_map/ppermute | solution.py:46
  91.3 2.1 %collective-permute-start.7 = (bf16[16,128,128]{2,1,0:T(8,128)(2,1)S(1)}, bf16[16,128,128]{2,1,0:T(8,128)(2,1)S(1)}, u32[]{:S(2)}, u32[]{:S(2)}) collective-permute-start(bf16[16,128,128]{2,1,0:T(8,128)(2,1)S(1)} %get-tuple-element.31), channel_id=1, source_target_pairs={{0,1},{1,0},{2,3},{3,2},{4,5},{5,4},{6,7},{7,6},{8,9},{9,8},{10,11... | collective-permute-start | bytes 1572872 | tf_op jit(solution)/shard_map/ppermute | solution.py:46
  95.0 31.8 %all-to-all-start.1 = ((bf16[16,400,128]{2,1,0:T(8,128)(2,1)}), bf16[16,400,128]{2,1,0:T(8,128)(2,1)S(1)}, u32[]{:S(2)}, u32[]{:S(2)}) async-start(bf16[16,400,128]{2,1,0:T(8,128)(2,1)} %shard_map.120), calls=%async_computation.1 | async-start | bytes 3276800 | tf_op jit(solution)/shard_map/all_to_all | solution.py:436
  98.7 2.2 %copy-start.1 = (bf16[512,4096]{1,0:T(8,128)(2,1)S(1)}, bf16[512,4096]{1,0:T(8,128)(2,1)}, u32[]{:S(2)}) copy-start(bf16[512,4096]{1,0:T(8,128)(2,1)} %up_ref.3) | copy-start | bytes 12582916
